TPU v7x, 32 devices: a whole 2x2x4 slice. The times are simulated.
32 devices in a mesh: pass: 16 (over z, y, core), qry: 2 (over x).
Axes of the slice: x: 2, y: 2, z: 4, core: 2. Of those that a mesh axis runs over, the one named last changes fastest.
Arguments:
- tokens: bfloat16 [4096, 1024], P(('pass', 'qry')), may hold values from -6 to 6
- w_query: bfloat16 [1024, 1024], P(None, 'qry'), may hold values from -0.1875 to 0.1875
- w_key: bfloat16 [1024, 1024], P(None, 'qry'), may hold values from -0.1875 to 0.1875
- w_value: bfloat16 [1024, 1024], P(None, 'qry'), may hold values from -0.1875 to 0.1875
- w_out: bfloat16 [1024, 1024], P('qry'), may hold values from -6 to 6
- gain_attn: float32 [1024], replicated, may hold values from 0.5 to 1.5
- shift_attn: float32 [1024], replicated, may hold values from -1.25 to 1.25
- w_up: bfloat16 [1024, 4096], P(None, 'qry'), may hold values from -0.1875 to 0.1875
- w_down: bfloat16 [4096, 1024], P('qry'), may hold values from -0.09375 to 0.09375
- gain_ffn: float32 [1024], replicated, may hold values from 0.5 to 1.5
- shift_ffn: float32 [1024], replicated, may hold values from -1.25 to 1.25
- w_colbert: bfloat16 [1024, 1024], replicated, may hold values from -0.1875 to 0.1875
- query_vecs: bfloat16 [2048, 1024], P('qry'), may hold values from -0.75 to 0.75
- match_index: int32 [2048, 4], P('qry'), may hold values from 0 to 2047
- passage_of: int32 [16], replicated, may hold values from 0 to 3, never falling along the last dimension, each value on 1 to 8 neighbouring positions
- cot_act: bfloat16 [4096, 1024], P(('pass', 'qry')), may hold values from -6 to 6
- cot_scores: float32 [32, 4], P('qry'), may hold values from -6 to 6
Outputs:
- activations: bfloat16 [4096, 1024], P(('pass', 'qry'))
- scores: float32 [32, 4], replicated
- grad_tokens: float32 [4096, 1024], P(('pass', 'qry'))
- grad_query: float32 [1024, 1024], P('pass', 'qry')
- grad_key: float32 [1024, 1024], P('pass', 'qry')
- grad_value: float32 [1024, 1024], P('pass', 'qry')
- grad_out: float32 [1024, 1024], P('qry', 'pass')
- grad_up: float32 [1024, 4096], P('pass', 'qry')
- grad_down: float32 [4096, 1024], P('qry', 'pass')
- grad_colbert: float32 [1024, 1024], replicated
- grad_gain_attn: float32 [1024], replicated
- grad_shift_attn: float32 [1024], replicated
- grad_gain_ffn: float32 [1024], replicated
- grad_shift_ffn: float32 [1024], replicated
Inputs may be any that keep to these rules, and one draw needn't show every extreme that they name: `passage_of`: entry p is the passage of the 256 tokens of pass index p; numbers never fall along p, every passage 0 to 3 holds 1 to 8 consecutive indices, and one holds exactly 8.
All inputs are finite; a program needn't handle non-finite values.
Results may differ from a plain program's by a relative error of at most 0.023.
Values may be sent and summed in bfloat16 or wider, within the bound.
No kernel may reach another device: no remote copies, remote signals or barrier semaphores. Data moves between devices by JAX's collectives and lax.ppermute only.
A program may use at most 192 MiB of HBM per device.

v0:
```python
import jax
import jax.numpy as jnp
from jax import lax
from jax.sharding import PartitionSpec as P

HD = 64
SPAN = 8


def passed_along(value, axis, steps):
    count = lax.axis_size(axis)
    first, last = (max(0, -steps), min(count, count - steps))
    return lax.ppermute(value, axis, [(source, source + steps) for source in range(first, last)])


def layer_norm(values, gain, shift):
    row_mean = jnp.mean(values, axis=-1, keepdims=True)
    centred = values - row_mean
    variance = jnp.mean(centred * centred, axis=-1, keepdims=True)
    return centred * lax.rsqrt(variance + 1e-05) * gain + shift


def gelu_exact(values):
    return 0.5 * values * (1.0 + jax.scipy.special.erf(values * 0.7071067811865476))


def normalize_rows(proj_rows):
    return proj_rows * lax.rsqrt(jnp.sum(proj_rows * proj_rows, axis=1, keepdims=True) + 1e-06)


def head_split(array):
    return array.reshape(array.shape[0], array.shape[1] // HD, HD)


def block_scores(queries, key_rows):
    return jnp.einsum("qhd,khd->hqk", queries, key_rows, preferred_element_type=jnp.float32) * 0.125


def grad_block(queries, ctx_grad, log_total, row_delta, key_rows, value_rows):
    scaled = block_scores(queries, key_rows)
    probs = jnp.exp(scaled - log_total[:, :, None])
    dprob = jnp.einsum("qhd,khd->hqk", ctx_grad, value_rows, preferred_element_type=jnp.float32)
    dscore = (0.125 * probs * (dprob - row_delta[:, :, None])).astype(jnp.bfloat16)
    dquery = jnp.einsum("hqk,khd->qhd", dscore, key_rows, preferred_element_type=jnp.float32)
    dkey = jnp.einsum("hqk,qhd->khd", dscore, queries, preferred_element_type=jnp.float32)
    dvalue = jnp.einsum(
        "hqk,qhd->khd", probs.astype(jnp.bfloat16), ctx_grad, preferred_element_type=jnp.float32
    )
    return (dquery, jnp.stack([dkey, dvalue]))


def contract_rows(left, right):
    return lax.dot_general(
        left, right, (((0,), (0,)), ((), ())), preferred_element_type=jnp.float32
    )


def contract_cols(left, right):
    return lax.dot_general(
        left, right, (((1,), (1,)), ((), ())), preferred_element_type=jnp.float32
    )


def local(
    tokens,
    w_query,
    w_key,
    w_value,
    w_out,
    gain_attn,
    shift_attn,
    w_up,
    w_down,
    gain_ffn,
    shift_ffn,
    w_colbert,
    query_vecs,
    match_index,
    passage_of,
    cot_act,
    cot_scores,
):
    pass_count = lax.axis_size("pass")
    qry_count = lax.axis_size("qry")
    pass_index = lax.axis_index("pass")
    qry_index = lax.axis_index("qry")
    own_id = passage_of[pass_index]

    def source_valid(offset):
        source = pass_index - offset
        inside = (source >= 0) & (source < pass_count)
        return inside & (passage_of[jnp.clip(source, 0, pass_count - 1)] == own_id)

    gathered = lax.all_gather(tokens, "qry", axis=0, tiled=True)
    block_rows = gathered.shape[0]
    local_width = w_query.shape[1]
    w_qkv = jnp.concatenate([w_query, w_key, w_value], axis=1)
    qkv_rows = jnp.dot(gathered, w_qkv, preferred_element_type=jnp.float32).astype(jnp.bfloat16)
    query_flat = qkv_rows[:, :local_width]
    key_flat = qkv_rows[:, local_width : 2 * local_width]
    value_flat = qkv_rows[:, 2 * local_width :]
    queries = head_split(query_flat)
    heads = queries.shape[1]
    own_pair = jnp.stack([key_flat, value_flat])
    offsets = [distance for distance in range(1, SPAN)] + [-distance for distance in range(1, SPAN)]

    def fetch_keys():
        received = []
        for offset in offsets:
            received.append(passed_along(own_pair, "pass", offset))
        return received

    remote = fetch_keys()

    def stat_of(kv_pair):
        return jax.nn.logsumexp(block_scores(queries, head_split(kv_pair[0])), axis=2)

    log_total = stat_of(own_pair)
    for offset, kv_pair in zip(offsets, remote):
        log_total = lax.cond(
            source_valid(offset),
            lambda current, kv_pair=kv_pair: jnp.logaddexp(current, stat_of(kv_pair)),
            lambda current: current,
            log_total,
        )

    def weighted(kv_pair):
        probs = jnp.exp(
            block_scores(queries, head_split(kv_pair[0])) - log_total[:, :, None]
        ).astype(jnp.bfloat16)
        return jnp.einsum(
            "hqk,khd->qhd", probs, head_split(kv_pair[1]), preferred_element_type=jnp.float32
        )

    context = weighted(own_pair)
    for offset, kv_pair in zip(offsets, remote):
        context = lax.cond(
            source_valid(offset),
            lambda running, kv_pair=kv_pair: running + weighted(kv_pair),
            lambda running: running,
            context,
        )
    context_low = context.reshape(block_rows, local_width).astype(jnp.bfloat16)
    piece_rows = context_low
    attn_rows = lax.psum_scatter(
        jnp.dot(piece_rows, w_out, preferred_element_type=jnp.float32).astype(jnp.bfloat16),
        "qry",
        scatter_dimension=0,
        tiled=True,
    ).astype(jnp.float32)
    hidden, norm_attn_back = jax.vjp(
        layer_norm, tokens.astype(jnp.float32) + attn_rows, gain_attn, shift_attn
    )
    hidden_all = lax.all_gather(hidden.astype(jnp.bfloat16), "qry", axis=0, tiled=True)
    inner_pre = jnp.dot(hidden_all, w_up, preferred_element_type=jnp.float32)
    gated_float, gelu_back = jax.vjp(gelu_exact, inner_pre)
    gated_low = gated_float.astype(jnp.bfloat16)
    piece_rows = gated_low
    ffn_rows = lax.psum_scatter(
        jnp.dot(piece_rows, w_down, preferred_element_type=jnp.float32).astype(jnp.bfloat16),
        "qry",
        scatter_dimension=0,
        tiled=True,
    ).astype(jnp.float32)
    output, norm_ffn_back = jax.vjp(layer_norm, hidden + ffn_rows, gain_ffn, shift_ffn)
    output_low = output.astype(jnp.bfloat16)
    proj_rows = jnp.dot(output_low, w_colbert, preferred_element_type=jnp.float32)
    unit_vecs, unit_back = jax.vjp(normalize_rows, proj_rows)
    unit_all = lax.all_gather(unit_vecs.astype(jnp.bfloat16), "qry", axis=0, tiled=True)
    seq_count = match_index.shape[1]
    query_rows = cot_scores.shape[0]
    numbers = jnp.arange(seq_count, dtype=jnp.int32)
    pick_col = numbers == own_id
    span_count = jnp.sum((passage_of == own_id).astype(jnp.int32))
    first_index = jnp.sum((passage_of < own_id).astype(jnp.int32))
    length = span_count * block_rows
    raw_pick = jnp.sum(jnp.where(pick_col[None, :], match_index, 0), axis=1)
    local_row = raw_pick % length - (pass_index - first_index) * block_rows
    one_hot = (local_row[:, None] == jnp.arange(block_rows, dtype=jnp.int32)[None, :]).astype(
        jnp.bfloat16
    )
    picked = jnp.dot(one_hot, unit_all, preferred_element_type=jnp.float32)
    query_float = query_vecs.astype(jnp.float32)
    match_vals = jnp.sum(query_float * picked, axis=1)
    per_query = jnp.sum(match_vals.reshape(query_rows, -1), axis=1)
    score_block = per_query[:, None] * pick_col.astype(jnp.float32)[None, :]
    score_part = lax.dynamic_update_slice(
        jnp.zeros((query_rows * qry_count, seq_count), jnp.float32),
        score_block,
        (qry_index * query_rows, jnp.zeros((), jnp.int32)),
    )
    cot_pick = jnp.sum(jnp.where(pick_col[None, :], cot_scores, 0.0), axis=1)
    token_weight = jnp.repeat(cot_pick, query_vecs.shape[0] // query_rows)
    weighted_queries = (token_weight[:, None] * query_float).astype(jnp.bfloat16)
    piece_rows = one_hot
    unit_grad = lax.psum_scatter(
        contract_rows(piece_rows, weighted_queries).astype(jnp.bfloat16),
        "qry",
        scatter_dimension=0,
        tiled=True,
    ).astype(jnp.float32)
    (proj_grad,) = unit_back(unit_grad)
    proj_low = proj_grad.astype(jnp.bfloat16)
    grad_colbert = contract_rows(output_low, proj_low)
    out_grad = cot_act.astype(jnp.float32) + contract_cols(proj_low, w_colbert)
    pre_grad, grad_gain_ffn, grad_shift_ffn = norm_ffn_back(out_grad)
    ffn_all = lax.all_gather(pre_grad.astype(jnp.bfloat16), "qry", axis=0, tiled=True)
    gated_grad = contract_cols(ffn_all, w_down)
    grad_down = contract_rows(gated_low, ffn_all)
    (inner_grad,) = gelu_back(gated_grad)
    inner_low = inner_grad.astype(jnp.bfloat16)
    grad_up = contract_rows(hidden_all, inner_low)
    piece_rows = inner_low
    hidden_grad = pre_grad + lax.psum_scatter(
        contract_cols(piece_rows, w_up).astype(jnp.bfloat16), "qry", scatter_dimension=0, tiled=True
    ).astype(jnp.float32)
    attn_pre_grad, grad_gain_attn, grad_shift_attn = norm_attn_back(hidden_grad)
    attn_all = lax.all_gather(attn_pre_grad.astype(jnp.bfloat16), "qry", axis=0, tiled=True)
    grad_out = contract_rows(context_low, attn_all)
    ctx_grad = head_split(contract_cols(attn_all, w_out).astype(jnp.bfloat16))
    row_delta = jnp.einsum("qhd,qhd->hq", ctx_grad.astype(jnp.float32), context)
    remote_back = fetch_keys()
    dquery, dkv_own = grad_block(
        queries, ctx_grad, log_total, row_delta, head_split(key_flat), head_split(value_flat)
    )
    key_value_grad = dkv_own
    zero_query = jnp.zeros_like(dquery)
    zero_pair = jnp.zeros((2, block_rows, heads, HD), jnp.float32)
    for offset, kv_pair in zip(offsets, remote_back):
        query_part, pair_part = lax.cond(
            source_valid(offset),
            lambda incoming: grad_block(
                queries,
                ctx_grad,
                log_total,
                row_delta,
                head_split(incoming[0]),
                head_split(incoming[1]),
            ),
            lambda incoming: (zero_query, zero_pair),
            kv_pair,
        )
        dquery = dquery + query_part
        returned = passed_along(
            pair_part.reshape(2, block_rows, local_width).astype(jnp.bfloat16), "pass", -offset
        ).astype(jnp.float32)
        key_value_grad = key_value_grad + returned.reshape(2, block_rows, heads, HD)
    dqkv_low = jnp.concatenate(
        [
            dquery.reshape(block_rows, local_width),
            key_value_grad[0].reshape(block_rows, local_width),
            key_value_grad[1].reshape(block_rows, local_width),
        ],
        axis=1,
    ).astype(jnp.bfloat16)
    grad_qkv = contract_rows(gathered, dqkv_low)
    piece_rows = dqkv_low
    grad_tokens = attn_pre_grad + lax.psum_scatter(
        contract_cols(piece_rows, w_qkv).astype(jnp.bfloat16),
        "qry",
        scatter_dimension=0,
        tiled=True,
    ).astype(jnp.float32)
    summed = (
        lax.psum_scatter(
            grad_qkv[:, :local_width].astype(jnp.bfloat16), "pass", scatter_dimension=0, tiled=True
        ).astype(jnp.float32),
        lax.psum_scatter(
            grad_qkv[:, local_width : 2 * local_width].astype(jnp.bfloat16),
            "pass",
            scatter_dimension=0,
            tiled=True,
        ).astype(jnp.float32),
        lax.psum_scatter(
            grad_qkv[:, 2 * local_width :].astype(jnp.bfloat16),
            "pass",
            scatter_dimension=0,
            tiled=True,
        ).astype(jnp.float32),
        lax.psum_scatter(
            grad_out.astype(jnp.bfloat16), "pass", scatter_dimension=1, tiled=True
        ).astype(jnp.float32),
        lax.psum_scatter(
            grad_up.astype(jnp.bfloat16), "pass", scatter_dimension=0, tiled=True
        ).astype(jnp.float32),
        lax.psum_scatter(
            grad_down.astype(jnp.bfloat16), "pass", scatter_dimension=1, tiled=True
        ).astype(jnp.float32),
    )
    shared = lax.psum(
        (grad_colbert, grad_gain_attn, grad_shift_attn, grad_gain_ffn, grad_shift_ffn, score_part),
        ("pass", "qry"),
    )
    return (
        output_low,
        shared[5],
        grad_tokens,
        summed[0],
        summed[1],
        summed[2],
        summed[3],
        summed[4],
        summed[5],
        shared[0],
        shared[1],
        shared[2],
        shared[3],
        shared[4],
    )


def solution(mesh):
    return jax.shard_map(
        local,
        mesh=mesh,
        in_specs=(
            P(("pass", "qry"), None),
            P(None, "qry"),
            P(None, "qry"),
            P(None, "qry"),
            P("qry", None),
            P(),
            P(),
            P(None, "qry"),
            P("qry", None),
            P(),
            P(),
            P(),
            P("qry", None),
            P("qry", None),
            P(),
            P(("pass", "qry"), None),
            P("qry", None),
        ),
        out_specs=(
            P(("pass", "qry"), None),
            P(),
            P(("pass", "qry"), None),
            P("pass", "qry"),
            P("pass", "qry"),
            P("pass", "qry"),
            P("qry", "pass"),
            P("pass", "qry"),
            P("qry", "pass"),
            P(),
            P(),
            P(),
            P(),
            P(),
        ),
        check_vma=False,
    )
```

profile of v0, /device:TPU:0, one launch (start us, length us, event | category | flops | bytes accessed | tf_op | source)
XLA Modules:
  0.0 991.4 jit_solution(7197005434151315248)
XLA Ops:
  7.3 10.3 %all_gather.15 = bf16[256,1024]{1,0:T(8,128)(2,1)S(1)} all-gather(bf16[128,1024]{1,0:T(8,128)(2,1)} %param.101), channel_id=1, replica_groups=mesh['pass'=16,'qry'=2] {'qry'}, dimensions={0}, use_global_device_ids=true | all-gather | bytes 786432 | tf_op jit(solution)/shard_map/all_gather | solution.py:94
  25.2 7.4 collective-permute-start.6
  41.4 6.7 collective-permute-start.2
  52.8 7.3 collective-permute-done.5
  72.7 9.9 %collective-permute-done.3 = bf16[2,256,512]{1,2,0:T(8,128)(2,1)S(1)} collective-permute-done((bf16[2,256,512]{1,2,0:T(8,128)(2,1)}, bf16[2,256,512]{1,2,0:T(8,128)(2,1)S(1)}, u32[]{:S(2)}, u32[]{:S(2)}) %collective-permute-start.3) | collective-permute-done | bytes 524320 | tf_op jit(solution)/shard_map/ppermute | solution.py:13
  112.4 20.5 %collective-permute-done.9 = bf16[2,256,512]{1,2,0:T(8,128)(2,1)} collective-permute-done((bf16[2,256,512]{1,2,0:T(8,128)(2,1)}, bf16[2,256,512]{1,2,0:T(8,128)(2,1)}, u32[]{:S(2)}, u32[]{:S(2)}) %collective-permute-start.9) | collective-permute-done | bytes 524320 | tf_op jit(solution)/shard_map/ppermute | solution.py:13
  151.5 60.4 %reduce-scatter.18.cloned.1.call-done = bf16[128,1024]{1,0:T(8,128)(2,1)} async-done(((bf16[256,1024]{1,0:T(8,128)(2,1)}), bf16[128,1024]{1,0:T(8,128)(2,1)}) %reduce-scatter.18.cloned.1.call-update) | async-done | bytes 262160 | tf_op jit(solution)/shard_map/reduce_scatter | solution.py:145
  215.3 8.7 all_gather.16
  249.4 14.5 %reduce-scatter.22.cloned.1.call-done = bf16[128,1024]{1,0:T(8,128)(2,1)} async-done(((bf16[256,1024]{1,0:T(8,128)(2,1)}), bf16[128,1024]{1,0:T(8,128)(2,1)}) %reduce-scatter.22.cloned.1.call-update) | async-done | bytes 262160 | tf_op jit(solution)/shard_map/reduce_scatter | solution.py:196
  267.9 9.2 all_gather.18
  281.6 14.7 %reduce-scatter.24.cloned.1.call-done = bf16[128,1024]{1,0:T(8,128)(2,1)} async-done(((bf16[256,1024]{1,0:T(8,128)(2,1)}), bf16[128,1024]{1,0:T(8,128)(2,1)}) %reduce-scatter.24.cloned.1.call-update) | async-done | bytes 262160 | tf_op jit(solution)/shard_map/reduce_scatter | solution.py:214
  299.2 8.9 all_gather.19
  309.7 7.5 collective-permute-start.27
  335.2 6.4 collective-permute-start.23
  377.1 6.9 collective-permute-done.22
  388.3 15.7 %collective-permute-done.19 = bf16[2,256,512]{1,2,0:T(8,128)(2,1)} collective-permute-done((bf16[2,256,512]{1,2,0:T(8,128)(2,1)}, bf16[2,256,512]{1,2,0:T(8,128)(2,1)}, u32[]{:S(2)}, u32[]{:S(2)}) %collective-permute-start.19) | collective-permute-done | bytes 524320 | tf_op jit(solution)/shard_map/ppermute | solution.py:13
  408.0 9.9 collective-permute-done.17
  448.2 7.0 all_gather.17
  456.5 97.0 %all-reduce = (f32[32,4]{0,1:T(4,128)}, f32[1024]{0:T(1024)}, f32[1024]{0:T(1024)}, f32[1024]{0:T(1024)}, f32[1024]{0:T(1024)}) all-reduce(f32[32,4]{0,1:T(4,128)S(1)} %dynamic_update_slice.3, f32[1024]{0:T(1024)S(1)} %get-tuple-element.930, f32[1024]{0:T(1024)S(1)} %get-tuple-element.934, ...), channel_id=1, replica_groups=mesh['pass'=16,'qry'=2] {'pass','qry'}, use_global_device_ids=true, to_apply=%region_98.99 | all-reduce | flops 4224 | bytes 33792 | tf_op jit(solution)/shard_map/psum | solution.py:290
  561.5 58.9 %reduce-scatter.36.cloned.1.call-done = bf16[64,512]{1,0:T(8,128)(2,1)} async-done(((bf16[1024,512]{1,0:T(8,128)(2,1)}), bf16[64,512]{1,0:T(8,128)(2,1)}) %reduce-scatter.36.cloned.1.call-update) | async-done | bytes 65552
  622.1 58.3 %reduce-scatter.34.cloned.1.call-done = bf16[64,512]{1,0:T(8,128)(2,1)} async-done(((bf16[1024,512]{1,0:T(8,128)(2,1)}), bf16[64,512]{1,0:T(8,128)(2,1)}) %reduce-scatter.34.cloned.1.call-update) | async-done | bytes 65552
  682.1 74.5 %reduce-scatter.30.cloned.1.call-done = bf16[64,2048]{1,0:T(8,128)(2,1)} async-done(((bf16[1024,2048]{1,0:T(8,128)(2,1)}), bf16[64,2048]{1,0:T(8,128)(2,1)}) %reduce-scatter.30.cloned.1.call-update) | async-done | bytes 262160 | tf_op jit(solution)/shard_map/reduce_scatter | solution.py:283
  758.4 73.7 %reduce-scatter.32.cloned.1.call-done = bf16[2048,64]{0,1:T(8,128)(2,1)} async-done(((bf16[2048,1024]{0,1:T(8,128)(2,1)}), bf16[2048,64]{0,1:T(8,128)(2,1)}) %reduce-scatter.32.cloned.1.call-update) | async-done | bytes 262160 | tf_op jit(solution)/shard_map/reduce_scatter | solution.py:286
  833.8 145.3 %all-reduce.3.cloned.1.call-done = f32[1024,1024]{1,0:T(8,128)} async-done(((f32[1024,1024]{1,0:T(8,128)}), f32[1024,1024]{1,0:T(8,128)}) %all-reduce.3.cloned.1.call-update) | async-done | bytes 4194320 | tf_op jit(solution)/shard_map/psum | solution.py:290
  (433 shorter events, 257.0 us)
Async XLA Ops:
  7.2 204.7 %reduce-scatter.18.cloned.1.call-start = ((), (), s32[]{:S(2)}) async-start(), calls=%async_computation.11 | async-start | bytes 786432 | tf_op jit(solution)/shard_map/reduce_scatter | solution.py:145
  40.0 42.6 %collective-permute-start.3 = (bf16[2,256,512]{1,2,0:T(8,128)(2,1)}, bf16[2,256,512]{1,2,0:T(8,128)(2,1)S(1)}, u32[]{:S(2)}, u32[]{:S(2)}) collective-permute-start(bf16[2,256,512]{1,2,0:T(8,128)(2,1)} %pad_maximum_fusion.15), channel_id=1, source_target_pairs={{0,8},{2,10},{4,12},{6,14},{8,16},{10,18},{12,20},{14,22},{16,24},... | collective-permute-start | bytes 1572872 | tf_op jit(solution)/shard_map/ppermute | solution.py:13
  41.4 42.5 %collective-permute-start.2 = (bf16[2,256,512]{1,2,0:T(8,128)(2,1)}, bf16[2,256,512]{1,2,0:T(8,128)(2,1)}, u32[]{:S(2)}, u32[]{:S(2)}) collective-permute-start(bf16[2,256,512]{1,2,0:T(8,128)(2,1)} %pad_maximum_fusion.15), channel_id=1, source_target_pairs={{0,6},{2,8},{4,10},{6,12},{8,14},{10,16},{12,18},{14,20},{16,22},{... | collective-permute-start | bytes 1572872 | tf_op jit(solution)/shard_map/ppermute | solution.py:13
  48.1 37.1 %collective-permute-start.1 = (bf16[2,256,512]{1,2,0:T(8,128)(2,1)}, bf16[2,256,512]{1,2,0:T(8,128)(2,1)}, u32[]{:S(2)}, u32[]{:S(2)}) collective-permute-start(bf16[2,256,512]{1,2,0:T(8,128)(2,1)} %pad_maximum_fusion.15), channel_id=1, source_target_pairs={{0,4},{2,6},{4,8},{6,10},{8,12},{10,14},{12,16},{14,18},{16,20},{1... | collective-permute-start | bytes 1572872 | tf_op jit(solution)/shard_map/ppermute | solution.py:13
  71.4 65.4 %collective-permute-start.13 = (bf16[2,256,512]{1,2,0:T(8,128)(2,1)}, bf16[2,256,512]{1,2,0:T(8,128)(2,1)}, u32[]{:S(2)}, u32[]{:S(2)}) collective-permute-start(bf16[2,256,512]{1,2,0:T(8,128)(2,1)} %pad_maximum_fusion.15), channel_id=1, source_target_pairs={{14,0},{16,2},{18,4},{20,6},{22,8},{24,10},{26,12},{28,14},{30,16}... | collective-permute-start | bytes 1572872 | tf_op jit(solution)/shard_map/ppermute | solution.py:13
  82.6 54.2 %collective-permute-start.12 = (bf16[2,256,512]{1,2,0:T(8,128)(2,1)}, bf16[2,256,512]{1,2,0:T(8,128)(2,1)}, u32[]{:S(2)}, u32[]{:S(2)}) collective-permute-start(bf16[2,256,512]{1,2,0:T(8,128)(2,1)} %pad_maximum_fusion.15), channel_id=1, source_target_pairs={{12,0},{14,2},{16,4},{18,6},{20,8},{22,10},{24,12},{26,14},{28,16}... | collective-permute-start | bytes 1572872 | tf_op jit(solution)/shard_map/ppermute | solution.py:13
  83.9 52.8 %collective-permute-start.11 = (bf16[2,256,512]{1,2,0:T(8,128)(2,1)}, bf16[2,256,512]{1,2,0:T(8,128)(2,1)}, u32[]{:S(2)}, u32[]{:S(2)}) collective-permute-start(bf16[2,256,512]{1,2,0:T(8,128)(2,1)} %pad_maximum_fusion.15), channel_id=1, source_target_pairs={{10,0},{12,2},{14,4},{16,6},{18,8},{20,10},{22,12},{24,14},{26,16}... | collective-permute-start | bytes 1572872 | tf_op jit(solution)/shard_map/ppermute | solution.py:13
  85.2 49.6 %collective-permute-start.10 = (bf16[2,256,512]{1,2,0:T(8,128)(2,1)}, bf16[2,256,512]{1,2,0:T(8,128)(2,1)}, u32[]{:S(2)}, u32[]{:S(2)}) collective-permute-start(bf16[2,256,512]{1,2,0:T(8,128)(2,1)} %pad_maximum_fusion.15), channel_id=1, source_target_pairs={{8,0},{10,2},{12,4},{14,6},{16,8},{18,10},{20,12},{22,14},{24,16},... | collective-permute-start | bytes 1572872 | tf_op jit(solution)/shard_map/ppermute | solution.py:13
  86.5 46.4 %collective-permute-start.9 = (bf16[2,256,512]{1,2,0:T(8,128)(2,1)}, bf16[2,256,512]{1,2,0:T(8,128)(2,1)}, u32[]{:S(2)}, u32[]{:S(2)}) collective-permute-start(bf16[2,256,512]{1,2,0:T(8,128)(2,1)} %pad_maximum_fusion.15), channel_id=1, source_target_pairs={{6,0},{8,2},{10,4},{12,6},{14,8},{16,10},{18,12},{20,14},{22,16},{... | collective-permute-start | bytes 1572872 | tf_op jit(solution)/shard_map/ppermute | solution.py:13
  151.4 95.6 %reduce-scatter.20.cloned.1.call-start = ((), (), s32[]{:S(2)}) async-start(), calls=%async_computation.12 | async-start | bytes 786432 | tf_op jit(solution)/shard_map/reduce_scatter | solution.py:159
  243.3 53.0 %reduce-scatter.24.cloned.1.call-start = ((), (), s32[]{:S(2)}) async-start(), calls=%async_computation.14 | async-start | bytes 786432 | tf_op jit(solution)/shard_map/reduce_scatter | solution.py:214
  281.6 271.9 %reduce-scatter.28.cloned.1.call-start = ((), (), s32[]{:S(2)}) async-start(), calls=%async_computation.16 | async-start | bytes 1114112 | tf_op jit(solution)/shard_map/reduce_scatter | solution.py:280
  309.7 48.4 %collective-permute-start.27 = (bf16[2,256,512]{1,2,0:T(8,128)(2,1)}, bf16[2,256,512]{1,2,0:T(8,128)(2,1)}, u32[]{:S(2)}, u32[]{:S(2)}) collective-permute-start(bf16[2,256,512]{1,2,0:T(8,128)(2,1)} %bitcast.214), channel_id=1, source_target_pairs={{0,14},{2,16},{4,18},{6,20},{8,22},{10,24},{12,26},{14,28},{16,30}... | collective-permute-start | bytes 1572872 | tf_op jit(solution)/shard_map/ppermute | solution.py:13
  318.1 42.0 %collective-permute-start.26 = (bf16[2,256,512]{1,2,0:T(8,128)(2,1)}, bf16[2,256,512]{1,2,0:T(8,128)(2,1)}, u32[]{:S(2)}, u32[]{:S(2)}) collective-permute-start(bf16[2,256,512]{1,2,0:T(8,128)(2,1)} %bitcast.212), channel_id=1, source_target_pairs={{0,12},{2,14},{4,16},{6,18},{8,20},{10,22},{12,24},{14,26},{16,28}... | collective-permute-start | bytes 1572872 | tf_op jit(solution)/shard_map/ppermute | solution.py:13
  321.2 41.1 %collective-permute-start.25 = (bf16[2,256,512]{1,2,0:T(8,128)(2,1)}, bf16[2,256,512]{1,2,0:T(8,128)(2,1)}, u32[]{:S(2)}, u32[]{:S(2)}) collective-permute-start(bf16[2,256,512]{1,2,0:T(8,128)(2,1)} %bitcast.210), channel_id=1, source_target_pairs={{0,10},{2,12},{4,14},{6,16},{8,18},{10,20},{12,22},{14,24},{16,26}... | collective-permute-start | bytes 1572872 | tf_op jit(solution)/shard_map/ppermute | solution.py:13
  335.2 40.5 %collective-permute-start.23 = (bf16[2,256,512]{1,2,0:T(8,128)(2,1)}, bf16[2,256,512]{1,2,0:T(8,128)(2,1)}, u32[]{:S(2)}, u32[]{:S(2)}) collective-permute-start(bf16[2,256,512]{1,2,0:T(8,128)(2,1)} %bitcast.206), channel_id=1, source_target_pairs={{0,6},{2,8},{4,10},{6,12},{8,14},{10,16},{12,18},{14,20},{16,22},{... | collective-permute-start | bytes 1572872 | tf_op jit(solution)/shard_map/ppermute | solution.py:13
  363.6 40.4 %collective-permute-start.19 = (bf16[2,256,512]{1,2,0:T(8,128)(2,1)}, bf16[2,256,512]{1,2,0:T(8,128)(2,1)}, u32[]{:S(2)}, u32[]{:S(2)}) collective-permute-start(bf16[2,256,512]{1,2,0:T(8,128)(2,1)} %bitcast.198), channel_id=1, source_target_pairs={{12,0},{14,2},{16,4},{18,6},{20,8},{22,10},{24,12},{26,14},{28,16}... | collective-permute-start | bytes 1572872 | tf_op jit(solution)/shard_map/ppermute | solution.py:13
  366.4 188.6 %reduce-scatter.26.cloned.1.call-start = ((), (), s32[]{:S(2)}) async-start(), calls=%async_computation.15 | async-start | bytes 786432 | tf_op jit(solution)/shard_map/reduce_scatter | solution.py:258
  426.7 133.1 %reduce-scatter.38.cloned.1.call-start = ((), (), s32[]{:S(2)}) async-start(), calls=%async_computation.22 | async-start | bytes 1114112
  431.3 189.1 %reduce-scatter.36.cloned.1.call-start = ((), (), s32[]{:S(2)}) async-start(), calls=%async_computation.21 | async-start | bytes 1114112
  432.7 247.7 %reduce-scatter.34.cloned.1.call-start = ((), (), s32[]{:S(2)}) async-start(), calls=%async_computation.20 | async-start | bytes 1114112
  434.1 322.5 %reduce-scatter.30.cloned.1.call-start = ((), (), s32[]{:S(2)}) async-start(), calls=%async_computation.17 | async-start | bytes 4456448 | tf_op jit(solution)/shard_map/reduce_scatter | solution.py:283
  438.7 393.3 %reduce-scatter.32.cloned.1.call-start = ((), (), s32[]{:S(2)}) async-start(), calls=%async_computation.18 | async-start | bytes 4456448 | tf_op jit(solution)/shard_map/reduce_scatter | solution.py:286
  443.4 535.7 %all-reduce.3.cloned.1.call-start = ((), (), s32[]{:S(2)}) async-start(), calls=%async_computation.19 | async-start | bytes 8388608 | tf_op jit(solution)/shard_map/psum | solution.py:290
  (93 other events, 1718.6 us)
Sparse Core Ops, SparseCore 0:
  151.6 60.2 reduce-scatter.17
  232.4 14.5 reduce-scatter.19
  249.3 14.5 reduce-scatter.21
  281.7 14.5 reduce-scatter.23
  366.5 87.1 reduce-scatter.27
  456.5 42.2 reduce-scatter.25
  502.4 57.3 reduce-scatter.37
  563.9 56.4 reduce-scatter.35
  624.0 56.3 reduce-scatter.33
  685.2 71.3 reduce-scatter.29
  760.5 71.5 reduce-scatter.31
  838.4 140.7 all-reduce.2
where the time goes:
time: 1000 us; the launch traced here: 991 us
  waiting for transfers between devices  587 us (59%)
  blocking collectives  141 us (14%)
  starting transfers between devices  74.3 us (7%)
  matrix products  63.9 us (6%)
  local copies, waits for them, and re-layouts  56.1 us (6%)
  between operations  35 us (4%)
  other arithmetic  33.1 us (3%)
    psum x1, waiting for transfers between devices, local(): lax.psum((grad_colbert, grad_gain_attn, grad_shift_attn, grad_gain_ffn, g...  145 us
    unnamed x15, waiting for transfers between devices  120 us
    psum x1, blocking collectives, local(): lax.psum((grad_colbert, grad_gain_attn, grad_shift_attn, grad_gain_ffn, g...  97 us
    ppermute x28, waiting for transfers between devices, passed_along(): lax.ppermute(value, axis, [(source, source + steps) for source in range(f...  79.7 us
    reduce_scatter x1, waiting for transfers between devices, local(): lax.psum_scatter(grad_up.astype(jnp.bfloat16), 'pass', scatter_dimension=...  74.5 us
    ppermute x28, starting transfers between devices, passed_along(): lax.ppermute(value, axis, [(source, source + steps) for source in range(f...  73.8 us
    reduce_scatter x1, waiting for transfers between devices, local(): lax.psum_scatter(grad_down.astype(jnp.bfloat16), 'pass', scatter_dimensio...  73.7 us
    reduce_scatter x1, waiting for transfers between devices, local(): lax.psum_scatter(jnp.dot(piece_rows, w_out, preferred_element_type=jnp.fl...  60.4 us
  transfers between devices with their start and end apart: 40, of which 20 were waited for; matrix products, arithmetic and copies ran while one was open for 9% of the time, Pallas kernels for 0%

commit v1 on v0

--- a/solution.py
+++ b/solution.py
@@ -1,10 +1,18 @@
+import functools
+import math
+
 import jax
 import jax.numpy as jnp
 from jax import lax
+from jax.experimental import pallas as pl
+from jax.experimental.pallas import tpu as pltpu
 from jax.sharding import PartitionSpec as P
 
 HD = 64
 SPAN = 8
+LANES = 128
+VMEM_LIMIT = 56 << 20
+LOG2E = math.log2(math.e)
 
 
 def passed_along(value, axis, steps):
@@ -61,7 +69,7 @@
     )
 
 
-def local(
+def local_general(
     tokens,
     w_query,
     w_key,
@@ -309,9 +317,693 @@
     )
 
 
+def swap_over(value, axis, mask):
+    count = lax.axis_size(axis)
+    return lax.ppermute(value, axis, [(index, index ^ mask) for index in range(count)])
+
+
+def ring_chips(chips):
+    layers = chips // 2
+    return [2 * z for z in range(layers)] + [2 * z + 1 for z in reversed(range(layers))]
+
+
+def low_lanes(rows):
+    return lax.broadcasted_iota(jnp.int32, (rows, LANES), 1) < HD
+
+
+def split_lanes(first, second):
+    low = low_lanes(first.shape[0])
+    return (
+        jnp.where(low, first, pltpu.roll(second, HD, 1)),
+        jnp.where(low, pltpu.roll(first, HD, 1), second),
+    )
+
+
+def dot_nn(left, right):
+    return jnp.dot(left, right, preferred_element_type=jnp.float32)
+
+
+def dot_nt(left, right):
+    return contract_cols(left, right)
+
+
+def params(*semantics):
+    return pltpu.CompilerParams(
+        dimension_semantics=semantics or None, vmem_limit_bytes=VMEM_LIMIT
+    )
+
+
+def cost(flops, moved, transcendentals=0):
+    return pl.CostEstimate(
+        flops=int(flops), bytes_accessed=int(moved), transcendentals=int(transcendentals)
+    )
+
+
+def project_body(x_ref, wq_ref, wk_ref, wv_ref, out_ref):
+    x = x_ref[...]
+    rows = x.shape[0]
+    half = rows // 2
+    query = dot_nn(x, wq_ref[...])
+    key = dot_nn(x, wk_ref[...])
+    value = dot_nn(x, wv_ref[...])
+    for pair in range(query.shape[1] // LANES):
+        cols = slice(pair * LANES, (pair + 1) * LANES)
+        first, second = split_lanes(key[:, cols], value[:, cols])
+        out_ref[2 * pair, 0:rows] = first.astype(jnp.bfloat16)
+        out_ref[2 * pair + 1, 0:rows] = second.astype(jnp.bfloat16)
+        first, second = split_lanes(query[:half, cols], query[half:, cols])
+        out_ref[2 * pair, rows : rows + half] = first.astype(jnp.bfloat16)
+        out_ref[2 * pair + 1, rows : rows + half] = second.astype(jnp.bfloat16)
+
+
+def project(x, wq, wk, wv):
+    rows, depth = x.shape
+    width = wq.shape[1]
+    heads = width // HD
+    steps = 2
+    weight = pl.BlockSpec((depth, width // steps), lambda i: (0, i))
+    return pl.pallas_call(
+        project_body,
+        grid=(steps,),
+        in_specs=[pl.BlockSpec((rows, depth), lambda i: (0, 0)), weight, weight, weight],
+        out_specs=pl.BlockSpec((heads // steps, rows * 3 // 2, LANES), lambda i: (i, 0, 0)),
+        out_shape=jax.ShapeDtypeStruct((heads, rows * 3 // 2, LANES), jnp.bfloat16),
+        compiler_params=params("arbitrary"),
+        cost_estimate=cost(2 * rows * depth * width * 3, 2 * (3 * depth * width + 4 * rows * depth)),
+        name="project",
+    )(x, wq, wk, wv)
+
+
+def load_query(packed):
+    wide = packed.astype(jnp.float32)
+    low = low_lanes(wide.shape[0])
+    top = jnp.where(low, wide, 0.0)
+    bottom = jnp.where(low, pltpu.roll(wide, HD, 1), 0.0)
+    return jnp.concatenate([top, bottom], axis=0).astype(jnp.bfloat16)
+
+
+def pack_transposed(columns):
+    half = columns.shape[1] // 2
+    return jnp.concatenate([columns[:, :half], columns[:, half:]], axis=0).T
+
+
+def attend_body(info_ref, own_ref, sib_ref, ctx_ref, ctxt_ref, lse_ref, kv_s, vt_s, score_s):
+    chips = own_ref.shape[0]
+    blocks = 2 * chips
+    rows = kv_s.shape[1]
+    parity = info_ref[2 * blocks]
+    scale = 0.125 * LOG2E
+    ones_rows = lax.broadcasted_iota(jnp.int32, (LANES, rows), 0) < HD
+
+    def gather(chip, carry):
+        for ref, which in ((own_ref, parity), (sib_ref, 1 - parity)):
+            block = ref[chip, 0:rows]
+            kv_s[2 * chip + which] = block
+            turned = block.astype(jnp.float32).T
+            vt_s[2 * chip + which] = jnp.where(ones_rows, 1.0, turned).astype(jnp.bfloat16)
+        return carry
+
+    lax.fori_loop(0, chips, gather, 0)
+
+    def one_block(item, carry):
+        block = 2 * item + parity
+        first = info_ref[block]
+        count = info_ref[blocks + block]
+        query = load_query(own_ref[item, rows : rows + rows // 2])
+
+        def scores(step, top):
+            score = dot_nt(kv_s[first + step], query) * scale
+            score_s[step] = score
+            return jnp.maximum(top, jnp.max(score.reshape(rows // 8, 8, rows), axis=0))
+
+        top = lax.fori_loop(0, count, scores, jnp.full((8, rows), -jnp.inf, jnp.float32))
+        top = jnp.max(top, axis=0, keepdims=True)
+
+        def weigh(step, total):
+            prob = jnp.exp2(score_s[step] - top).astype(jnp.bfloat16)
+            return total + dot_nn(vt_s[first + step], prob)
+
+        total = lax.fori_loop(0, count, weigh, jnp.zeros((LANES, rows), jnp.float32))
+        weight = total[0:1]
+        context = total[HD:] / weight
+        ctxt_ref[item] = context
+        lse_ref[item] = jnp.broadcast_to(top + jnp.log2(weight), (8, rows))
+        ctx_ref[item] = pack_transposed(context).astype(jnp.bfloat16)
+        return carry
+
+    lax.fori_loop(0, chips, one_block, 0)
+
+
+def whole():
+    return pl.BlockSpec(memory_space=pltpu.VMEM)
+
+
+def attend(info, own, sib):
+    chips, packed, _ = own.shape
+    rows = packed * 2 // 3
+    blocks = 2 * chips
+    return pl.pallas_call(
+        attend_body,
+        in_specs=[pl.BlockSpec(memory_space=pltpu.SMEM), whole(), whole()],
+        out_specs=[whole(), whole(), whole()],
+        out_shape=[
+            jax.ShapeDtypeStruct((chips, rows // 2, LANES), jnp.bfloat16),
+            jax.ShapeDtypeStruct((chips, HD, rows), jnp.float32),
+            jax.ShapeDtypeStruct((chips, 8, rows), jnp.float32),
+        ],
+        scratch_shapes=[
+            pltpu.VMEM((blocks, rows, LANES), jnp.bfloat16),
+            pltpu.VMEM((blocks, LANES, rows), jnp.bfloat16),
+            pltpu.VMEM((SPAN, rows, rows), jnp.float32),
+        ],
+        compiler_params=params(),
+        cost_estimate=cost(2 * 2 * 40 * rows * rows * LANES, 4 << 20, 40 * rows * rows),
+        name="attend",
+    )(info, own, sib)
+
+
+def attend_back_body(
+    info_ref, own_ref, sib_ref, dctx_ref, ctxt_ref, lse_ref, dkv_ref, dq_ref, kv_s, kt_s, acc_s
+):
+    chips = own_ref.shape[0]
+    blocks = 2 * chips
+    rows = kv_s.shape[1]
+    half = rows // 2
+    parity = info_ref[2 * blocks]
+    scale = 0.125 * LOG2E
+
+    def gather(chip, carry):
+        for ref, which in ((own_ref, parity), (sib_ref, 1 - parity)):
+            block = ref[chip, 0:rows]
+            kv_s[2 * chip + which] = block
+            turned = block.astype(jnp.float32).T
+            kt_s[2 * chip + which] = turned[0:HD].astype(jnp.bfloat16)
+            acc_s[2 * chip + which] = jnp.zeros((rows, LANES), jnp.float32)
+        return carry
+
+    lax.fori_loop(0, chips, gather, 0)
+    low = low_lanes(half)
+
+    def one_block(item, carry):
+        block = 2 * item + parity
+        first = info_ref[block]
+        count = info_ref[blocks + block]
+        query = load_query(own_ref[item, rows : rows + half])
+        packed = dctx_ref[item].astype(jnp.float32)
+        top = jnp.where(low, 0.0, pltpu.roll(packed, HD, 1))
+        bottom = jnp.where(low, 0.0, packed)
+        dctx = jnp.concatenate([top, bottom], axis=0).astype(jnp.bfloat16)
+        turned = packed.T
+        dctx_t = jnp.concatenate([turned[:HD], turned[HD:]], axis=1)
+        delta = jnp.sum(dctx_t * ctxt_ref[item], axis=0, keepdims=True)
+        lse = lse_ref[item, 0:1]
+        both = jnp.concatenate([query, dctx], axis=0)
+
+        def step_block(step, dq):
+            kv = kv_s[first + step]
+            prob = jnp.exp2(dot_nt(kv, query) * scale - lse)
+            dprob = dot_nt(kv, dctx)
+            dscore = (0.125 * prob * (dprob - delta)).astype(jnp.bfloat16)
+            pair = jnp.concatenate([dscore, prob.astype(jnp.bfloat16)], axis=1)
+            acc_s[first + step] += dot_nn(pair, both)
+            return dq + dot_nn(kt_s[first + step], dscore)
+
+        dq = lax.fori_loop(0, count, step_block, jnp.zeros((HD, rows), jnp.float32))
+        dq_ref[item] = pack_transposed(dq).astype(jnp.bfloat16)
+        return carry
+
+    lax.fori_loop(0, chips, one_block, 0)
+
+    def finish(index, carry):
+        dkv_ref[index] = acc_s[index].astype(jnp.bfloat16)
+        return carry
+
+    lax.fori_loop(0, blocks, finish, 0)
+
+
+def attend_back(info, own, sib, dctx, ctxt, lse):
+    chips, packed, _ = own.shape
+    rows = packed * 2 // 3
+    blocks = 2 * chips
+    return pl.pallas_call(
+        attend_back_body,
+        in_specs=[pl.BlockSpec(memory_space=pltpu.SMEM)] + [whole()] * 5,
+        out_specs=[whole(), whole()],
+        out_shape=[
+            jax.ShapeDtypeStruct((blocks, rows, LANES), jnp.bfloat16),
+            jax.ShapeDtypeStruct((chips, rows // 2, LANES), jnp.bfloat16),
+        ],
+        scratch_shapes=[
+            pltpu.VMEM((blocks, rows, LANES), jnp.bfloat16),
+            pltpu.VMEM((blocks, HD, rows), jnp.bfloat16),
+            pltpu.VMEM((blocks, rows, LANES), jnp.float32),
+        ],
+        compiler_params=params(),
+        cost_estimate=cost(2 * 5 * 40 * rows * rows * LANES, 5 << 20, 40 * rows * rows),
+        name="attend_back",
+    )(info, own, sib, dctx, ctxt, lse)
+
+
+def out_project_body(in_ref, w_ref, ctx_ref, own_ref, send_ref):
+    heads, half, _ = in_ref.shape
+    for pair in range(heads // 2):
+        cols = slice(pair * LANES, (pair + 1) * LANES)
+        top, bottom = split_lanes(
+            in_ref[2 * pair].astype(jnp.float32), in_ref[2 * pair + 1].astype(jnp.float32)
+        )
+        ctx_ref[0:half, cols] = top.astype(jnp.bfloat16)
+        ctx_ref[half:, cols] = bottom.astype(jnp.bfloat16)
+    rows = dot_nn(ctx_ref[...], w_ref[...])
+    own_ref[...] = rows[:half]
+    send_ref[...] = rows[half:].astype(jnp.bfloat16)
+
+
+def out_project(packed, w_out):
+    heads, half, _ = packed.shape
+    width, depth = w_out.shape
+    return pl.pallas_call(
+        out_project_body,
+        in_specs=[whole()] * 2,
+        out_specs=[whole()] * 3,
+        out_shape=[
+            jax.ShapeDtypeStruct((2 * half, width), jnp.bfloat16),
+            jax.ShapeDtypeStruct((half, depth), jnp.float32),
+            jax.ShapeDtypeStruct((half, depth), jnp.bfloat16),
+        ],
+        compiler_params=params(),
+        cost_estimate=cost(4 * half * width * depth, 3 << 20),
+        name="out_project",
+    )(packed, w_out)
+
+
+def ctx_grad_body(g_ref, w_ref, out_ref):
+    half = out_ref.shape[1]
+    grad = dot_nt(g_ref[...], w_ref[...])
+    for pair in range(grad.shape[1] // LANES):
+        cols = slice(pair * LANES, (pair + 1) * LANES)
+        first, second = split_lanes(grad[:half, cols], grad[half:, cols])
+        out_ref[2 * pair] = first.astype(jnp.bfloat16)
+        out_ref[2 * pair + 1] = second.astype(jnp.bfloat16)
+
+
+def ctx_grad_packed(grad_all, w_out):
+    rows, depth = grad_all.shape
+    width = w_out.shape[0]
+    return pl.pallas_call(
+        ctx_grad_body,
+        in_specs=[whole()] * 2,
+        out_specs=whole(),
+        out_shape=jax.ShapeDtypeStruct((width // HD, rows // 2, LANES), jnp.bfloat16),
+        compiler_params=params(),
+        cost_estimate=cost(2 * rows * width * depth, 2 << 20),
+        name="ctx_grad",
+    )(grad_all, w_out)
+
+
+def head_grad_body(
+    info_ref, tok_ref, dkv_ref, dkv_sib_ref, dq_ref, dq_sib_ref, out_ref, acc_s, grad_s
+):
+    step = pl.program_id(0)
+    steps = pl.num_programs(0)
+    chips, half, _ = dq_ref.shape
+    blocks = 2 * chips
+    rows = 2 * half
+    parity = info_ref[2 * blocks]
+    chip = jnp.where(step < chips // 2, 2 * step, 2 * chips - 1 - 2 * step)
+
+    @pl.when(step == 0)
+    def _():
+        acc_s[...] = jnp.zeros_like(acc_s)
+
+    for core in range(2):
+        block = 2 * chip + core
+        total = dkv_ref[block].astype(jnp.float32) + dkv_sib_ref[block].astype(jnp.float32)
+        own = (parity == core).astype(jnp.int32)
+        dq = jnp.where(
+            own == 1, dq_ref[chip].astype(jnp.float32), dq_sib_ref[chip].astype(jnp.float32)
+        )
+        dq_t = dq.T
+        dq_t = jnp.concatenate([dq_t[:HD], dq_t[HD:]], axis=1)
+        left = jnp.concatenate([total.T, dq_t], axis=0).astype(jnp.bfloat16)
+        acc_s[...] += dot_nn(left, tok_ref[core * rows : (core + 1) * rows])
+
+        @pl.when(own == 1)
+        def _():
+            out_ref[chip, 0:rows] = total.astype(jnp.bfloat16)
+            out_ref[chip, rows : rows + half] = dq_ref[chip]
+
+    @pl.when(step == steps - 1)
+    def _():
+        grad = acc_s[...]
+        depth = grad.shape[1] // blocks
+        wide = jnp.concatenate([grad[: 2 * HD], grad[2 * HD :], jnp.zeros_like(grad[:HD])], axis=0)
+        turned = wide.T
+        grad_s[...] = turned.reshape(blocks, depth, 2 * LANES)
+
+        def pack(index, carry):
+            part = grad_s[2 * index + parity]
+            base = rows + half
+            out_ref[index, base : base + depth] = part[:, :LANES].astype(jnp.bfloat16)
+            query = part[:, LANES:]
+            low = low_lanes(depth // 2)
+            mixed = jnp.where(low, query[: depth // 2], pltpu.roll(query[depth // 2 :], HD, 1))
+            out_ref[index, base + depth : base + depth + depth // 2] = mixed.astype(jnp.bfloat16)
+            return carry
+
+        lax.fori_loop(0, chips, pack, 0)
+
+
+def head_grad(info, tokens_all, dkv, dkv_sib, dq, dq_sib):
+    blocks, rows, _ = dkv.shape
+    chips = blocks // 2
+    depth = tokens_all.shape[1]
+    piece = depth // blocks
+    height = rows + rows // 2 + piece + piece // 2
+    full = lambda shape: pl.BlockSpec(shape, lambda i: (0,) * len(shape))
+    return pl.pallas_call(
+        head_grad_body,
+        grid=(chips,),
+        in_specs=[
+            pl.BlockSpec(memory_space=pltpu.SMEM),
+            pl.BlockSpec((2 * rows, depth), lambda i: (i, 0)),
+            full(dkv.shape),
+            full(dkv.shape),
+            full(dq.shape),
+            full(dq.shape),
+        ],
+        out_specs=full((chips, height, LANES)),
+        out_shape=jax.ShapeDtypeStruct((chips, height, LANES), jnp.bfloat16),
+        scratch_shapes=[
+            pltpu.VMEM((3 * HD, depth), jnp.float32),
+            pltpu.VMEM((blocks, piece, 2 * LANES), jnp.float32),
+        ],
+        compiler_params=params("arbitrary"),
+        cost_estimate=cost(2 * blocks * rows * depth * 3 * HD, blocks * rows * depth * 2),
+        name="head_grad",
+    )(info, tokens_all, dkv, dkv_sib, dq, dq_sib)
+
+
+def token_grad_body(in_ref, wq_ref, wk_ref, wv_ref, own_ref, send_ref, gq_ref, gk_ref, gv_ref, d_s):
+    heads = in_ref.shape[0]
+    rows, width = d_s.shape[1:]
+    half = rows // 2
+    piece = gq_ref.shape[0]
+    base = rows + half
+    load = lambda head, lo, hi: in_ref[head, lo:hi].astype(jnp.float32)
+    for pair in range(heads // 2):
+        cols = slice(pair * LANES, (pair + 1) * LANES)
+        a, b = 2 * pair, 2 * pair + 1
+        key, value = split_lanes(load(a, 0, rows), load(b, 0, rows))
+        d_s[1, :, cols] = key.astype(jnp.bfloat16)
+        d_s[2, :, cols] = value.astype(jnp.bfloat16)
+        top, bottom = split_lanes(load(a, rows, base), load(b, rows, base))
+        d_s[0, :half, cols] = top.astype(jnp.bfloat16)
+        d_s[0, half:, cols] = bottom.astype(jnp.bfloat16)
+        key, value = split_lanes(load(a, base, base + piece), load(b, base, base + piece))
+        gk_ref[:, cols] = key
+        gv_ref[:, cols] = value
+        last = base + piece + piece // 2
+        top, bottom = split_lanes(load(a, base + piece, last), load(b, base + piece, last))
+        gq_ref[: piece // 2, cols] = top
+        gq_ref[piece // 2 :, cols] = bottom
+    total = dot_nt(d_s[0], wq_ref[...]) + dot_nt(d_s[1], wk_ref[...]) + dot_nt(d_s[2], wv_ref[...])
+    own_ref[...] = total[:half]
+    send_ref[...] = total[half:].astype(jnp.bfloat16)
+
+
+def token_grad(packed, rows, wq, wk, wv):
+    depth, width = wq.shape
+    piece = (packed.shape[1] - rows * 3 // 2) * 2 // 3
+    grad = jax.ShapeDtypeStruct((piece, width), jnp.float32)
+    return pl.pallas_call(
+        token_grad_body,
+        in_specs=[whole()] * 4,
+        out_specs=[whole()] * 5,
+        out_shape=[
+            jax.ShapeDtypeStruct((rows // 2, depth), jnp.float32),
+            jax.ShapeDtypeStruct((rows // 2, depth), jnp.bfloat16),
+            grad,
+            grad,
+            grad,
+        ],
+        scratch_shapes=[pltpu.VMEM((3, rows, width), jnp.bfloat16)],
+        compiler_params=params(),
+        cost_estimate=cost(6 * rows * depth * width, 5 << 20),
+        name="token_grad",
+    )(packed, wq, wk, wv)
+
+
+def ffn_grad_body(up_left, up_right, down_left, down_right, out_ref):
+    width = up_right.shape[1]
+    out_ref[:, :width] = contract_rows(up_left[...], up_right[...]).astype(jnp.bfloat16)
+    out_ref[:, width:] = contract_rows(down_left[...], down_right[...]).astype(jnp.bfloat16)
+
+
+def ffn_grad(chips, up_left, up_right, down_left, down_right):
+    rows, depth = up_left.shape
+    width = up_right.shape[1]
+    tile = depth // chips
+    column = lambda i: (0, jnp.where(i < chips // 2, 2 * i, 2 * chips - 1 - 2 * i))
+    left = pl.BlockSpec((rows, tile), column)
+    right = pl.BlockSpec((rows, width), lambda i: (0, 0))
+    return pl.pallas_call(
+        ffn_grad_body,
+        grid=(chips,),
+        in_specs=[left, right, left, right],
+        out_specs=pl.BlockSpec((tile, 2 * width), lambda i: (i, 0)),
+        out_shape=jax.ShapeDtypeStruct((depth, 2 * width), jnp.bfloat16),
+        compiler_params=params("arbitrary"),
+        cost_estimate=cost(4 * rows * depth * width, 12 << 20),
+        name="ffn_grad",
+    )(up_left, up_right, down_left, down_right)
+
+
+def normalized(values):
+    centred = values - jnp.mean(values, axis=-1, keepdims=True)
+    inverse = lax.rsqrt(jnp.mean(centred * centred, axis=-1, keepdims=True) + 1e-05)
+    return centred * inverse, inverse
+
+
+def norm_back(grad, gain, unit, inverse):
+    scaled = grad * gain
+    along = jnp.mean(scaled * unit, axis=-1, keepdims=True)
+    return (scaled - jnp.mean(scaled, axis=-1, keepdims=True) - unit * along) * inverse
+
+
+def gelu_with_slope(values):
+    cdf = 0.5 * (1.0 + lax.erf(values * 0.7071067811865476))
+    density = jnp.exp(-0.5 * values * values) * 0.3989422804014327
+    return values * cdf, cdf + values * density
+
+
+def local_by_head(
+    tokens,
+    w_query,
+    w_key,
+    w_value,
+    w_out,
+    gain_attn,
+    shift_attn,
+    w_up,
+    w_down,
+    gain_ffn,
+    shift_ffn,
+    w_colbert,
+    query_vecs,
+    match_index,
+    passage_of,
+    cot_act,
+    cot_scores,
+):
+    pass_count = lax.axis_size("pass")
+    qry_count = lax.axis_size("qry")
+    pass_index = lax.axis_index("pass")
+    qry_index = lax.axis_index("qry")
+    chips = pass_count // 2
+    own_rows = tokens.shape[0]
+    block_rows = own_rows * qry_count
+    same_core = [[index for index in range(pass_count) if index % 2 == core] for core in (0, 1)]
+    ring = [[2 * chip + core for chip in ring_chips(chips) for core in (0, 1)]]
+    parity = pass_index % 2
+    own_id = passage_of[pass_index]
+
+    def swap(value):
+        return swap_over(value, "qry", 1)
+
+    def sibling(value):
+        return swap_over(value, "pass", 1)
+
+    def to_heads(value):
+        return lax.all_to_all(
+            value, "pass", 0, 0, axis_index_groups=same_core, tiled=True
+        )
+
+    gathered = jnp.concatenate([tokens, swap(tokens)], axis=0)
+    tokens_all = lax.all_gather(gathered, "pass", axis=0, axis_index_groups=ring, tiled=True)
+
+    seq_count = match_index.shape[1]
+    query_rows = cot_scores.shape[0]
+    pick_col = jnp.arange(seq_count, dtype=jnp.int32) == own_id
+    span_count = jnp.sum((passage_of == own_id).astype(jnp.int32))
+    first_index = jnp.sum((passage_of < own_id).astype(jnp.int32))
+    raw_pick = jnp.sum(jnp.where(pick_col[None, :], match_index, 0), axis=1)
+    local_row = raw_pick % (span_count * block_rows) - (pass_index - first_index) * block_rows
+    inside = (local_row >= 0) & (local_row < block_rows)
+    local_row = jnp.where(inside, (local_row + qry_index * own_rows) % block_rows, -1)
+    one_hot = (local_row[:, None] == jnp.arange(block_rows, dtype=jnp.int32)[None, :]).astype(
+        jnp.bfloat16
+    )
+    cot_pick = jnp.sum(jnp.where(pick_col[None, :], cot_scores, 0.0), axis=1)
+    token_weight = jnp.repeat(cot_pick, query_vecs.shape[0] // query_rows)
+    query_float = query_vecs.astype(jnp.float32)
+    weighted_queries = (token_weight[:, None] * query_float).astype(jnp.bfloat16)
+    unit_grad_part = contract_rows(one_hot, weighted_queries)
+    turned_part = jnp.concatenate([unit_grad_part[own_rows:], unit_grad_part[:own_rows]], axis=0)
+    unit_grad = unit_grad_part + swap(turned_part.astype(jnp.bfloat16)).astype(jnp.float32)
+
+    block_ids = passage_of.astype(jnp.int32)
+    same = block_ids[:, None] == block_ids[None, :]
+    starts = jnp.sum((block_ids[None, :] < block_ids[:, None]).astype(jnp.int32), axis=1)
+    counts = jnp.sum(same.astype(jnp.int32), axis=1)
+    info = jnp.concatenate([starts, counts, parity[None].astype(jnp.int32)])
+
+    own_pack = to_heads(project(gathered, w_query, w_key, w_value))
+    sib_pack = sibling(own_pack)
+    ctx_pack, ctx_turned, lse = attend(info, own_pack, sib_pack)
+    context_low, attn_own, attn_send = out_project(to_heads(ctx_pack), w_out)
+    attn_rows = attn_own + swap(attn_send).astype(jnp.float32)
+    unit_attn, inverse_attn = normalized(tokens.astype(jnp.float32) + attn_rows)
+    hidden = unit_attn * gain_attn + shift_attn
+    hidden_low = hidden.astype(jnp.bfloat16)
+    hidden_all = jnp.concatenate([hidden_low, swap(hidden_low)], axis=0)
+
+    inner_pre = dot_nn(hidden_all, w_up)
+    gated, slope = gelu_with_slope(inner_pre)
+    gated_low = gated.astype(jnp.bfloat16)
+    ffn_part = dot_nn(gated_low, w_down)
+    ffn_rows = ffn_part[:own_rows] + swap(ffn_part[own_rows:].astype(jnp.bfloat16)).astype(
+        jnp.float32
+    )
+    unit_ffn, inverse_ffn = normalized(hidden + ffn_rows)
+    output = unit_ffn * gain_ffn + shift_ffn
+    output_low = output.astype(jnp.bfloat16)
+    output_other = swap(output_low)
+
+    def colbert(rows, grad_rows):
+        proj = dot_nn(rows, w_colbert)
+        inverse = lax.rsqrt(jnp.sum(proj * proj, axis=1, keepdims=True) + 1e-06)
+        unit = proj * inverse
+        along = jnp.sum(unit * grad_rows, axis=1, keepdims=True)
+        return unit.astype(jnp.bfloat16), ((grad_rows - unit * along) * inverse).astype(
+            jnp.bfloat16
+        )
+
+    unit_own, proj_own = colbert(output_low, unit_grad[:own_rows])
+    out_grad = cot_act.astype(jnp.float32) + dot_nt(proj_own, w_colbert)
+    pre_grad = norm_back(out_grad, gain_ffn, unit_ffn, inverse_ffn)
+    grad_gain_ffn = jnp.sum(out_grad * unit_ffn, axis=0)
+    grad_shift_ffn = jnp.sum(out_grad, axis=0)
+    pre_low = pre_grad.astype(jnp.bfloat16)
+    ffn_all = jnp.concatenate([pre_low, swap(pre_low)], axis=0)
+
+    unit_other, proj_other = colbert(output_other, unit_grad[own_rows:])
+    output_all = jnp.concatenate([output_low, output_other], axis=0)
+    proj_all = jnp.concatenate([proj_own, proj_other], axis=0)
+    grad_colbert_part = contract_rows(output_all, proj_all).astype(jnp.bfloat16)
+    colbert_piece = lax.psum_scatter(
+        grad_colbert_part, "pass", scatter_dimension=0, axis_index_groups=ring, tiled=True
+    )
+    grad_colbert = lax.all_gather(
+        colbert_piece, "pass", axis=0, axis_index_groups=ring, tiled=True
+    ).astype(jnp.float32)
+    picked = dot_nn(one_hot, jnp.concatenate([unit_own, unit_other], axis=0))
+    per_query = jnp.sum((query_float * picked).reshape(query_rows, -1), axis=1)
+    score_block = per_query[:, None] * pick_col.astype(jnp.float32)[None, :]
+    score_part = lax.dynamic_update_slice(
+        jnp.zeros((query_rows * qry_count, seq_count), jnp.float32),
+        score_block,
+        (qry_index * query_rows, jnp.zeros((), jnp.int32)),
+    )
+
+    inner_low = (dot_nt(ffn_all, w_down) * slope).astype(jnp.bfloat16)
+    hidden_part = dot_nt(inner_low, w_up)
+    hidden_grad = (
+        pre_grad
+        + hidden_part[:own_rows]
+        + swap(hidden_part[own_rows:].astype(jnp.bfloat16)).astype(jnp.float32)
+    )
+    ffn_grads = ffn_grad(chips, hidden_all, inner_low, ffn_all, gated_low)
+    ffn_sums = lax.psum_scatter(
+        ffn_grads, "pass", scatter_dimension=0, axis_index_groups=ring, tiled=True
+    )
+    width = w_up.shape[1]
+    grad_up = ffn_sums[:, :width].astype(jnp.float32)
+    grad_down = ffn_sums[:, width:].astype(jnp.float32).T
+
+    attn_pre = norm_back(hidden_grad, gain_attn, unit_attn, inverse_attn)
+    grad_gain_attn = jnp.sum(hidden_grad * unit_attn, axis=0)
+    grad_shift_attn = jnp.sum(hidden_grad, axis=0)
+    attn_low = attn_pre.astype(jnp.bfloat16)
+    attn_all = jnp.concatenate([attn_low, swap(attn_low)], axis=0)
+
+    small = jnp.concatenate(
+        [
+            grad_gain_attn,
+            grad_shift_attn,
+            grad_gain_ffn,
+            grad_shift_ffn,
+            score_part.reshape(-1),
+        ]
+    ).reshape(-1, LANES)
+    for mask in [1 << bit for bit in range(pass_count.bit_length() - 1)]:
+        small = small + swap_over(small, "pass", mask)
+    small = small + swap(small)
+    model = tokens.shape[1]
+    norms = small[: 4 * model // LANES].reshape(4, model)
+    scores = small[4 * model // LANES :].reshape(score_part.shape)
+
+    own_dctx = to_heads(ctx_grad_packed(attn_all, w_out))
+    dkv, dq = attend_back(info, own_pack, sib_pack, own_dctx, ctx_turned, lse)
+    back = head_grad(info, tokens_all, dkv, sibling(dkv), dq, sibling(dq))
+    token_own, token_send, grad_query, grad_key, grad_value = token_grad(
+        to_heads(back), block_rows, w_query, w_key, w_value
+    )
+    grad_tokens = attn_pre + token_own + swap(token_send).astype(jnp.float32)
+
+    grad_out_part = contract_rows(attn_all, context_low).astype(jnp.bfloat16)
+    tile = model // chips
+    grad_out_part = jnp.concatenate(
+        [grad_out_part[tile * chip : tile * (chip + 1)] for chip in ring_chips(chips)], axis=0
+    )
+    grad_out = (
+        lax.psum_scatter(
+            grad_out_part, "pass", scatter_dimension=0, axis_index_groups=ring, tiled=True
+        )
+        .astype(jnp.float32)
+        .T
+    )
+    return (
+        output_low,
+        scores,
+        grad_tokens,
+        grad_query,
+        grad_key,
+        grad_value,
+        grad_out,
+        grad_up,
+        grad_down,
+        grad_colbert,
+        norms[0],
+        norms[1],
+        norms[2],
+        norms[3],
+    )
+
+
 def solution(mesh):
+    by_head = mesh.shape["qry"] == 2
     return jax.shard_map(
-        local,
+        local_by_head if by_head else local_general,
         mesh=mesh,
         in_specs=(
             P(("pass", "qry"), None),

time: 1000 us -> 389 us (0.39)
  waiting for transfers between devices: 587 us -> 168 us
  blocking collectives: 141 us -> 43.3 us
  Pallas kernels: 0 us -> 76.2 us
  local copies, waits for them, and re-layouts: 56.1 us -> 12.8 us
  matrix products: 63.9 us -> 21 us
  starting transfers between devices: 74.3 us -> 32.2 us
  between operations: 35 us -> 15.7 us
  other arithmetic: 33.1 us -> 18.1 us
    reduce_scatter x8 -> x3, waiting for transfers between devices: 241 us -> 67.6 us  [the longest x1 53.5 us: local_by_head(): lax.psum_scatter(ffn_grads, 'pass', scatter_dimension=0, axis_index_group...]
    psum x1 -> x0, waiting for transfers between devices: 145 us -> none  [local(): lax.psum((grad_colbert, grad_gain_attn, grad_shift_attn, grad_gain_ffn, g...]
    unnamed x15 -> x5, waiting for transfers between devices: 120 us -> 0.76 us
    psum x1 -> x0, blocking collectives: 97 us -> none  [local(): lax.psum((grad_colbert, grad_gain_attn, grad_shift_attn, grad_gain_ffn, g...]
    pallas_call x0 -> x8, Pallas kernels: none -> 76.2 us  [the longest x1 22.5 us: attend_back(): pl.pallas_call(attend_back_body, in_specs=[pl.BlockSpec(memory_space=pltp...]
    ppermute x28 -> x18, starting transfers between devices: 73.8 us -> 24.7 us  [swap_over(): lax.ppermute(value, axis, [(index, index ^ mask) for index in range(count)])]
    all_gather x5 -> x0, blocking collectives: 44.1 us -> none  [the longest x1 10.3 us: local(): gathered = lax.all_gather(tokens, 'qry', axis=0, tiled=True)]
    all_to_all x0 -> x2, blocking collectives: none -> 43.3 us  [to_heads(): lax.all_to_all(value, 'pass', 0, 0, axis_index_groups=same_core, tiled=True)]
  transfers between devices with their start and end apart: 40 -> 25, of which waited for: 20 -> 20; matrix products, arithmetic and copies ran while one was open for 9% -> 10% of each run, Pallas kernels for 0% -> 13%
where the time goes in v1:
time: 389 us; the launch traced here: 387 us
  waiting for transfers between devices  168 us (43%)
  Pallas kernels  76.2 us (20%)
  blocking collectives  43.3 us (11%)
  starting transfers between devices  32.2 us (8%)
  matrix products  21 us (5%)
  other arithmetic  18.1 us (5%)
  between operations  15.7 us (4%)
  local copies, waits for them, and re-layouts  12.8 us (3%)
    ppermute x18, waiting for transfers between devices, swap_over(): lax.ppermute(value, axis, [(index, index ^ mask) for index in range(count)])  67.7 us
    reduce_scatter x1, waiting for transfers between devices, local_by_head(): lax.psum_scatter(ffn_grads, 'pass', scatter_dimension=0, axis_index_group...  53.5 us
    all_to_all x2, blocking collectives, to_heads(): lax.all_to_all(value, 'pass', 0, 0, axis_index_groups=same_core, tiled=True)  43.3 us
    all_gather x1, waiting for transfers between devices, local_by_head(): lax.all_gather(colbert_piece, 'pass', axis=0, axis_index_groups=ring, til...  29.9 us
    ppermute x18, starting transfers between devices, swap_over(): lax.ppermute(value, axis, [(index, index ^ mask) for index in range(count)])  24.7 us
    pallas_call x1, Pallas kernels, attend_back(): pl.pallas_call(attend_back_body, in_specs=[pl.BlockSpec(memory_space=pltp...  22.5 us
    pallas_call x1, Pallas kernels, attend(): pl.pallas_call(attend_body, in_specs=[pl.BlockSpec(memory_space=pltpu.SME...  21 us
    reduce_scatter x1, waiting for transfers between devices, local_by_head(): lax.psum_scatter(grad_colbert_part, 'pass', scatter_dimension=0, axis_ind...  14.1 us
  transfers between devices with their start and end apart: 25, of which 20 were waited for; matrix products, arithmetic and copies ran while one was open for 10% of the time, Pallas kernels for 13%

profile of v1, /device:TPU:0, one launch (start us, length us, event | category | flops | bytes accessed | tf_op | source)
XLA Modules:
  0.0 387.5 jit_solution(10361162235274426466)
XLA Ops:
  11.2 5.5 %collective-permute-done = bf16[128,1024]{1,0:T(8,128)(2,1)S(1)} collective-permute-done((bf16[128,1024]{1,0:T(8,128)(2,1)}, bf16[128,1024]{1,0:T(8,128)(2,1)S(1)}, u32[]{:S(2)}, u32[]{:S(2)}) %collective-permute-start) | collective-permute-done | bytes 262176 | tf_op jit(solution)/shard_map/ppermute | solution.py:322
  17.5 3.9 %project.1 = bf16[8,384,128]{2,1,0:T(8,128)(2,1)} custom-call(bf16[256,1024]{1,0:T(8,128)(2,1)} %copy-done.3, bf16[1024,512]{1,0:T(8,128)(2,1)} %wq_ref.3, bf16[1024,512]{1,0:T(8,128)(2,1)} %wk_ref.3, bf16[1024,512]{1,0:T(8,128)(2,1)} %wv_ref.3), custom_call_target="tpu_custom_call" | custom-call | flops 805306368 | bytes 5242880 | tf_op jit(solution)/shard_map/project/pallas_call | solution.py:385
  21.5 25.4 %all_to_all.20.own_ref = bf16[8,384,128]{2,1,0:T(8,128)(2,1)S(1)} all-to-all(bf16[8,384,128]{2,1,0:T(8,128)(2,1)} %project.1), channel_id=1, replica_groups={{0,4,8,12,16,20,24,28},{2,6,10,14,18,22,26,30},{1,5,9,13,17,21,25,29},{..., dimensions={0} | all-to-all | bytes 1572864 | tf_op jit(solution)/shard_map/all_to_all | solution.py:837
  49.2 21.0 %attend.1 = (bf16[8,128,128]{2,1,0:T(8,128)(2,1)}, f32[8,64,256]{2,1,0:T(8,128)}, f32[8,8,256]{2,1,0:T(8,128)}) custom-call(s32[33]{0:T(128)} %pad_add_fusion.info_ref, bf16[8,384,128]{2,1,0:T(8,128)(2,1)} %copy-done.15, bf16[8,384,128]{2,1,0:T(8,128)(2,1)} %collective-permute-done.1.sib_ref), custom_call_target="tpu_custom_call" | custom-call | flops 1342177280 | bytes 4194304 | tf_op jit(solution)/shard_map/attend/pallas_call | solution.py:465
  73.9 3.9 %copy.35 = bf16[1024,1024]{0,1:T(8,128)(2,1)} copy(bf16[1024,1024]{1,0:T(8,128)(2,1)} %param.29) | data formatting | bytes 4194304 | tf_op args[12]
  96.1 7.1 %collective-permute-done.3 = bf16[128,1024]{1,0:T(8,128)(2,1)S(1)} collective-permute-done((bf16[128,1024]{1,0:T(8,128)(2,1)S(1)}, bf16[128,1024]{1,0:T(8,128)(2,1)S(1)}, u32[]{:S(2)}, u32[]{:S(2)}) %collective-permute-start.3) | collective-permute-done | bytes 262176 | tf_op jit(solution)/shard_map/ppermute | solution.py:322
  108.8 4.8 %collective-permute-done.5 = bf16[256,1024]{1,0:T(8,128)(2,1)S(1)} collective-permute-done((bf16[256,1024]{1,0:T(8,128)(2,1)S(1)}, bf16[256,1024]{1,0:T(8,128)(2,1)S(1)}, u32[]{:S(2)}, u32[]{:S(2)}) %collective-permute-start.5) | collective-permute-done | bytes 524320 | tf_op jit(solution)/shard_map/ppermute | solution.py:322
  119.3 4.3 %collective-permute-done.8 = bf16[128,1024]{1,0:T(8,128)(2,1)S(1)} collective-permute-done((bf16[128,1024]{1,0:T(8,128)(2,1)S(1)}, bf16[128,1024]{1,0:T(8,128)(2,1)S(1)}, u32[]{:S(2)}, u32[]{:S(2)}) %collective-permute-start.8) | collective-permute-done | bytes 262176 | tf_op jit(solution)/shard_map/ppermute | solution.py:322
  133.3 4.9 %collective-permute-done.6 = bf16[128,1024]{1,0:T(8,128)(2,1)S(1)} collective-permute-done((bf16[128,1024]{1,0:T(8,128)(2,1)S(1)}, bf16[128,1024]{1,0:T(8,128)(2,1)S(1)}, u32[]{:S(2)}, u32[]{:S(2)}) %collective-permute-start.6) | collective-permute-done | bytes 262176 | tf_op jit(solution)/shard_map/ppermute | solution.py:322
  138.2 4.7 %fusion.2.up_right = bf16[256,2048]{1,0:T(8,128)(2,1)S(1)} fusion(bf16[2048,1024]{1,0:T(8,128)(2,1)S(1)} %copy-done.33, f32[256,2048]{1,0:T(8,128)} %get-tuple-element.118, bf16[128,1024]{1,0:T(8,128)(2,1)S(1)} %collective-permute-done.6, bf16[128,1024]{1,0:T(8,128)(2,1)S(1)} %get-tuple-element.99), kind=kOutput, calls=%fused_computation.6 | convolution fusion | flops 1080033280 | bytes 7864320 | tf_op jit(solution)/shard_map/dot_general | solution.py:67
  145.9 7.3 %collective-permute-done.7 = bf16[128,1024]{1,0:T(8,128)(2,1)S(1)} collective-permute-done((bf16[128,1024]{1,0:T(8,128)(2,1)S(1)}, bf16[128,1024]{1,0:T(8,128)(2,1)S(1)}, u32[]{:S(2)}, u32[]{:S(2)}) %collective-permute-start.7) | collective-permute-done | bytes 262176 | tf_op jit(solution)/shard_map/ppermute | solution.py:322
  155.4 4.9 %collective-permute-done.14 = bf16[128,1024]{1,0:T(8,128)(2,1)S(1)} collective-permute-done((bf16[128,1024]{1,0:T(8,128)(2,1)S(1)}, bf16[128,1024]{1,0:T(8,128)(2,1)S(1)}, u32[]{:S(2)}, u32[]{:S(2)}) %collective-permute-start.14) | collective-permute-done | bytes 262176 | tf_op jit(solution)/shard_map/ppermute | solution.py:322
  162.0 14.1 %reduce-scatter.8.cloned.1.call-done = bf16[64,1024]{1,0:T(8,128)(2,1)} async-done(((bf16[1024,1024]{1,0:T(8,128)(2,1)}), bf16[64,1024]{1,0:T(8,128)(2,1)}) %reduce-scatter.8.cloned.1.call-update) | async-done | bytes 131088 | tf_op jit(solution)/shard_map/reduce_scatter | solution.py:913
  177.9 8.8 %ffn_grad.1 = bf16[1024,4096]{1,0:T(8,128)(2,1)} custom-call(bf16[256,1024]{1,0:T(8,128)(2,1)} %pad_maximum_fusion.up_left, bf16[256,2048]{1,0:T(8,128)(2,1)} %copy-done.12, bf16[256,1024]{1,0:T(8,128)(2,1)} %pad_maximum_fusion.2.down_left, bf16[256,2048]{1,0:T(8,128)(2,1)} %copy-done.11), custom_call_target="tpu_custom_call" | custom-call | flops 2147483648 | bytes 12582912 | tf_op jit(solution)/shard_map/ffn_grad/pallas_call | solution.py:769
  190.2 18.0 %all_to_all.21.dctx_ref = bf16[8,128,128]{2,1,0:T(8,128)(2,1)} all-to-all(bf16[8,128,128]{2,1,0:T(8,128)(2,1)} %ctx_grad.1), channel_id=1, replica_groups={{0,4,8,12,16,20,24,28},{2,6,10,14,18,22,26,30},{1,5,9,13,17,21,25,29},{..., dimensions={0} | all-to-all | bytes 524288 | tf_op jit(solution)/shard_map/all_to_all | solution.py:837
  208.1 22.5 %attend_back.1 = (bf16[16,256,128]{2,1,0:T(8,128)(2,1)}, bf16[8,128,128]{2,1,0:T(8,128)(2,1)}) custom-call(s32[33]{0:T(128)} %pad_add_fusion.info_ref, bf16[8,384,128]{2,1,0:T(8,128)(2,1)} %copy-done.15, bf16[8,384,128]{2,1,0:T(8,128)(2,1)} %collective-permute-done.1.sib_ref, bf16[8,128,128]{2,1,0:T(8,128)(2,1)} %all_to_all.21.dctx_ref, ...), custom_call_target="tpu_custom_call" | custom-call | flops 3355443200 | bytes 5242880 | tf_op jit(solution)/shard_map/attend_back/pallas_call | solution.py:548
  235.0 10.6 %head_grad.1 = bf16[8,480,128]{2,1,0:T(8,128)(2,1)} custom-call(s32[33]{0:T(128)} %pad_add_fusion.info_ref, bf16[4096,1024]{1,0:T(8,128)(2,1)} %all-gather.3.cloned.1.call-done.tok_ref, bf16[16,256,128]{2,1,0:T(8,128)(2,1)} %get-tuple-element.32.dkv_ref, bf16[16,256,128]{2,1,0:T(8,128)(2,1)} %copy-done.5, bf16[8,128,128]{2,1,0:T(8,128)(2,1)} %get-tuple-element.33.dq_ref, ...), custom_call_target="tpu_custom_call" | custom-call | flops 1610612736 | bytes 8388608 | tf_op jit(solution)/shard_map/head_grad/pallas_call | solution.py:683
  260.0 9.0 %collective-permute-done.11 = f32[33,128]{1,0:T(8,128)S(1)} collective-permute-done((f32[33,128]{1,0:T(8,128)S(1)}, f32[33,128]{1,0:T(8,128)S(1)}, u32[]{:S(2)}, u32[]{:S(2)}) %collective-permute-start.11) | collective-permute-done | bytes 16928 | tf_op jit(solution)/shard_map/ppermute | solution.py:322
  269.0 3.8 collective-permute-start.12
  272.8 4.3 %collective-permute-done.12 = f32[33,128]{1,0:T(8,128)S(1)} collective-permute-done((f32[33,128]{1,0:T(8,128)S(1)}, f32[33,128]{1,0:T(8,128)S(1)}, u32[]{:S(2)}, u32[]{:S(2)}) %collective-permute-start.12) | collective-permute-done | bytes 16928 | tf_op jit(solution)/shard_map/ppermute | solution.py:322
  282.5 4.1 %token_grad.1 = (f32[128,1024]{1,0:T(8,128)}, bf16[128,1024]{1,0:T(8,128)(2,1)}, f32[64,512]{1,0:T(8,128)}, f32[64,512]{1,0:T(8,128)}, f32[64,512]{1,0:T(8,128)}) custom-call(bf16[8,480,128]{2,1,0:T(8,128)(2,1)} %copy-done.2, bf16[1024,512]{1,0:T(8,128)(2,1)} %wq_ref.3, bf16[1024,512]{1,0:T(8,128)(2,1)} %wk_ref.3, bf16[1024,512]{1,0:T(8,128)(2,1)} %wv_ref.3), custom_call_target="tpu_custom_call" | custom-call | flops 805306368 | bytes 5242880 | tf_op jit(solution)/shard_map/token_grad/pallas_call | solution.py:738
  290.3 29.9 %all-gather.5.cloned.1.call-done = bf16[1024,1024]{1,0:T(8,128)(2,1)} async-done(((bf16[64,1024]{1,0:T(8,128)(2,1)}), bf16[1024,1024]{1,0:T(8,128)(2,1)}) %all-gather.5.cloned.1.call-update) | async-done | bytes 2097168 | tf_op jit(solution)/shard_map/all_gather | solution.py:916
  320.2 4.2 %convert_element_type.121 = f32[1024,1024]{1,0:T(8,128)} convert(bf16[1024,1024]{1,0:T(8,128)(2,1)} %all-gather.5.cloned.1.call-done) | non-fusion elementwise | flops 1048576 | bytes 6291456 | tf_op jit(solution)/shard_map/convert_element_type | solution.py:918
  325.3 53.5 %reduce-scatter.6.cloned.1.call-done = bf16[64,4096]{1,0:T(8,128)(2,1)} async-done(((bf16[1024,4096]{1,0:T(8,128)(2,1)}), bf16[64,4096]{1,0:T(8,128)(2,1)}) %reduce-scatter.6.cloned.1.call-update) | async-done | bytes 524304 | tf_op jit(solution)/shard_map/reduce_scatter | solution.py:936
  (198 shorter events, 91.2 us)
Async XLA Ops:
  7.2 9.5 %collective-permute-start = (bf16[128,1024]{1,0:T(8,128)(2,1)}, bf16[128,1024]{1,0:T(8,128)(2,1)S(1)}, u32[]{:S(2)}, u32[]{:S(2)}) collective-permute-start(bf16[128,1024]{1,0:T(8,128)(2,1)} %param.17), channel_id=1, source_target_pairs={{0,1},{1,0},{2,3},{3,2},{4,5},{5,4},{6,7},{7,6},{8,9},{9,8},{10,11... | collective-permute-start | bytes 786440 | tf_op jit(solution)/shard_map/ppermute | solution.py:322
  46.8 2.4 collective-permute-start.1
  70.2 12.9 %all-to-all-start.1 = ((bf16[8,128,128]{2,1,0:T(8,128)(2,1)}), bf16[8,128,128]{2,1,0:T(8,128)(2,1)S(1)}, u32[]{:S(2)}, u32[]{:S(2)}) async-start(bf16[8,128,128]{2,1,0:T(8,128)(2,1)} %get-tuple-element.27), calls=%async_computation.1 | async-start | bytes 524288 | tf_op jit(solution)/shard_map/all_to_all | solution.py:837
  73.8 102.3 %reduce-scatter.8.cloned.1.call-start = ((), (), s32[]{:S(2)}) async-start(), calls=%async_computation.10 | async-start | bytes 2228224 | tf_op jit(solution)/shard_map/reduce_scatter | solution.py:913
  86.4 6.8 %collective-permute-start.2 = (bf16[128,1024]{1,0:T(8,128)(2,1)}, bf16[128,1024]{1,0:T(8,128)(2,1)S(1)}, u32[]{:S(2)}, u32[]{:S(2)}) collective-permute-start(bf16[128,1024]{1,0:T(8,128)(2,1)} %get-tuple-element.29), channel_id=1, source_target_pairs={{0,1},{1,0},{2,3},{3,2},{4,5},{5,4},{6,7},{7,6},{8,9},{9,8},{10,11... | collective-permute-start | bytes 786440 | tf_op jit(solution)/shard_map/ppermute | solution.py:322
  93.8 9.3 %collective-permute-start.3 = (bf16[128,1024]{1,0:T(8,128)(2,1)S(1)}, bf16[128,1024]{1,0:T(8,128)(2,1)S(1)}, u32[]{:S(2)}, u32[]{:S(2)}) collective-permute-start(bf16[128,1024]{1,0:T(8,128)(2,1)S(1)} %fusion.25), channel_id=1, source_target_pairs={{0,1},{1,0},{2,3},{3,2},{4,5},{5,4},{6,7},{7,6},{8,9},{9,8},{10,11... | collective-permute-start | bytes 786440 | tf_op jit(solution)/shard_map/ppermute | solution.py:322
  95.5 18.1 %collective-permute-start.5 = (bf16[256,1024]{1,0:T(8,128)(2,1)S(1)}, bf16[256,1024]{1,0:T(8,128)(2,1)S(1)}, u32[]{:S(2)}, u32[]{:S(2)}) collective-permute-start(bf16[256,1024]{1,0:T(8,128)(2,1)S(1)} %pad_maximum_fusion.1), channel_id=1, source_target_pairs={{0,1},{1,0},{2,3},{3,2},{4,5},{5,4},{6,7},{7,6},{8,9},{9,8},{10,11... | collective-permute-start | bytes 1572872 | tf_op jit(solution)/shard_map/ppermute | solution.py:322
  107.2 9.2 %collective-permute-start.4 = (bf16[128,1024]{1,0:T(8,128)(2,1)S(1)}, bf16[128,1024]{1,0:T(8,128)(2,1)S(1)}, u32[]{:S(2)}, u32[]{:S(2)}) collective-permute-start(bf16[128,1024]{1,0:T(8,128)(2,1)S(1)} %slice.152), channel_id=1, source_target_pairs={{0,1},{1,0},{2,3},{3,2},{4,5},{5,4},{6,7},{7,6},{8,9},{9,8},{10,11... | collective-permute-start | bytes 786440 | tf_op jit(solution)/shard_map/ppermute | solution.py:322
  117.2 6.4 %collective-permute-start.8 = (bf16[128,1024]{1,0:T(8,128)(2,1)S(1)}, bf16[128,1024]{1,0:T(8,128)(2,1)S(1)}, u32[]{:S(2)}, u32[]{:S(2)}) collective-permute-start(bf16[128,1024]{1,0:T(8,128)(2,1)S(1)} %add_convert_fusion), channel_id=1, source_target_pairs={{0,1},{1,0},{2,3},{3,2},{4,5},{5,4},{6,7},{7,6},{8,9},{9,8},{10,11... | collective-permute-start | bytes 786440 | tf_op jit(solution)/shard_map/ppermute | solution.py:322
  128.3 105.6 %all-gather.3.cloned.1.call-start = ((), (), s32[]{:S(2)}) async-start(), calls=%async_computation.7 | async-start | bytes 8912896 | tf_op jit(solution)/shard_map/all_gather | solution.py:842
  129.1 159.7 %reduce-scatter.4.cloned.1.call-start = ((), (), s32[]{:S(2)}) async-start(), calls=%async_computation.8 | async-start | bytes 1114112 | tf_op jit(solution)/shard_map/reduce_scatter | solution.py:979
  131.7 6.4 %collective-permute-start.6 = (bf16[128,1024]{1,0:T(8,128)(2,1)S(1)}, bf16[128,1024]{1,0:T(8,128)(2,1)S(1)}, u32[]{:S(2)}, u32[]{:S(2)}) collective-permute-start(bf16[128,1024]{1,0:T(8,128)(2,1)S(1)} %get-tuple-element.99), channel_id=1, source_target_pairs={{0,1},{1,0},{2,3},{3,2},{4,5},{5,4},{6,7},{7,6},{8,9},{9,8},{10,11... | collective-permute-start | bytes 786440 | tf_op jit(solution)/shard_map/ppermute | solution.py:322
  144.4 8.9 %collective-permute-start.7 = (bf16[128,1024]{1,0:T(8,128)(2,1)S(1)}, bf16[128,1024]{1,0:T(8,128)(2,1)S(1)}, u32[]{:S(2)}, u32[]{:S(2)}) collective-permute-start(bf16[128,1024]{1,0:T(8,128)(2,1)S(1)} %slice.151), channel_id=1, source_target_pairs={{0,1},{1,0},{2,3},{3,2},{4,5},{5,4},{6,7},{7,6},{8,9},{9,8},{10,11... | collective-permute-start | bytes 786440 | tf_op jit(solution)/shard_map/ppermute | solution.py:322
  153.9 6.4 %collective-permute-start.14 = (bf16[128,1024]{1,0:T(8,128)(2,1)S(1)}, bf16[128,1024]{1,0:T(8,128)(2,1)S(1)}, u32[]{:S(2)}, u32[]{:S(2)}) collective-permute-start(bf16[128,1024]{1,0:T(8,128)(2,1)S(1)} %get-tuple-element.96), channel_id=1, source_target_pairs={{0,1},{1,0},{2,3},{3,2},{4,5},{5,4},{6,7},{7,6},{8,9},{9,8},{10,11... | collective-permute-start | bytes 786440 | tf_op jit(solution)/shard_map/ppermute | solution.py:322
  162.0 158.3 %all-gather.5.cloned.1.call-start = ((), (), s32[]{:S(2)}) async-start(), calls=%async_computation.11 | async-start | bytes 2228224 | tf_op jit(solution)/shard_map/all_gather | solution.py:916
  176.1 202.7 %reduce-scatter.6.cloned.1.call-start = ((), (), s32[]{:S(2)}) async-start(), calls=%async_computation.9 | async-start | bytes 8912896 | tf_op jit(solution)/shard_map/reduce_scatter | solution.py:936
  230.7 3.3 collective-permute-start.15
  230.7 3.2 collective-permute-start.16
  245.6 35.9 %all-to-all-start.3 = ((bf16[8,480,128]{2,1,0:T(8,128)(2,1)}), bf16[8,480,128]{2,1,0:T(8,128)(2,1)S(1)}, u32[]{:S(2)}, u32[]{:S(2)}) async-start(bf16[8,480,128]{2,1,0:T(8,128)(2,1)} %head_grad.1), calls=%async_computation.3 | async-start | bytes 1966080 | tf_op jit(solution)/shard_map/all_to_all | solution.py:837
  253.4 5.7 %collective-permute-start.10 = (f32[33,128]{1,0:T(8,128)S(1)}, f32[33,128]{1,0:T(8,128)S(1)}, u32[]{:S(2)}, u32[]{:S(2)}) collective-permute-start(f32[33,128]{1,0:T(8,128)S(1)} %bitcast_add_fusion), channel_id=1, source_target_pairs={{0,4},{2,6},{4,0},{6,2},{8,12},{10,14},{12,8},{14,10},{16,20},{18,... | collective-permute-start | bytes 50696 | tf_op jit(solution)/shard_map/ppermute | solution.py:322
  259.1 9.9 %collective-permute-start.11 = (f32[33,128]{1,0:T(8,128)S(1)}, f32[33,128]{1,0:T(8,128)S(1)}, u32[]{:S(2)}, u32[]{:S(2)}) collective-permute-start(f32[33,128]{1,0:T(8,128)S(1)} %fusion.58), channel_id=1, source_target_pairs={{0,8},{2,10},{4,12},{6,14},{8,0},{10,2},{12,4},{14,6},{16,24},{18,... | collective-permute-start | bytes 50696 | tf_op jit(solution)/shard_map/ppermute | solution.py:322
  269.0 8.1 %collective-permute-start.12 = (f32[33,128]{1,0:T(8,128)S(1)}, f32[33,128]{1,0:T(8,128)S(1)}, u32[]{:S(2)}, u32[]{:S(2)}) collective-permute-start(f32[33,128]{1,0:T(8,128)S(1)} %add.176), channel_id=1, source_target_pairs={{0,16},{2,18},{4,20},{6,22},{8,24},{10,26},{12,28},{14,30},{16,0},... | collective-permute-start | bytes 50696 | tf_op jit(solution)/shard_map/ppermute | solution.py:322
  277.1 3.8 collective-permute-start.13
  286.6 37.9 %collective-permute-start.17 = (bf16[128,1024]{1,0:T(8,128)(2,1)}, bf16[128,1024]{1,0:T(8,128)(2,1)S(1)}, u32[]{:S(2)}, u32[]{:S(2)}) collective-permute-start(bf16[128,1024]{1,0:T(8,128)(2,1)} %get-tuple-element.35), channel_id=1, source_target_pairs={{0,1},{1,0},{2,3},{3,2},{4,5},{5,4},{6,7},{7,6},{8,9},{9,8},{10,11... | collective-permute-start | bytes 786440 | tf_op jit(solution)/shard_map/ppermute | solution.py:322
  (38 other events, 458.8 us)
Sparse Core Ops, SparseCore 0:
  128.4 47.6 reduce-scatter.7
  178.3 55.2 all-gather.2
  235.8 50.4 reduce-scatter.3
  287.8 32.3 all-gather.4
  322.5 56.3 reduce-scatter.5

commit v2 on v1

--- a/solution.py
+++ b/solution.py
@@ -407,7 +407,29 @@
     return jnp.concatenate([columns[:, :half], columns[:, half:]], axis=0).T
 
 
-def attend_body(info_ref, own_ref, sib_ref, ctx_ref, ctxt_ref, lse_ref, kv_s, vt_s, score_s):
+def square_sums(rows_low):
+    group = lambda axis: lax.broadcasted_iota(jnp.int32, (LANES, LANES), axis) // HD
+    ones = (group(0) == group(1)).astype(jnp.bfloat16)
+    wide = rows_low.astype(jnp.float32)
+    sums = dot_nn((wide * wide).astype(jnp.bfloat16), ones)
+    return jnp.max(sums.reshape(sums.shape[0] // 8, 8, LANES), axis=0)
+
+
+def over_blocks(first, count, step):
+    def pair(index, carry):
+        step(first + 2 * index, 2)
+        return carry
+
+    lax.fori_loop(0, count // 2, pair, 0)
+
+    @pl.when(count % 2 == 1)
+    def _():
+        step(first + count - 1, 1)
+
+
+def attend_body(
+    info_ref, own_ref, sib_ref, ctx_ref, ctxt_ref, lse_ref, kt_ref, kv_s, vt_s, score_s, total_s
+):
     chips = own_ref.shape[0]
     blocks = 2 * chips
     rows = kv_s.shape[1]
@@ -416,42 +438,76 @@
     ones_rows = lax.broadcasted_iota(jnp.int32, (LANES, rows), 0) < HD
 
     def gather(chip, carry):
+        key_top, query_top = carry
         for ref, which in ((own_ref, parity), (sib_ref, 1 - parity)):
             block = ref[chip, 0:rows]
             kv_s[2 * chip + which] = block
             turned = block.astype(jnp.float32).T
             vt_s[2 * chip + which] = jnp.where(ones_rows, 1.0, turned).astype(jnp.bfloat16)
-        return carry
-
-    lax.fori_loop(0, chips, gather, 0)
-
-    def one_block(item, carry):
-        block = 2 * item + parity
-        first = info_ref[block]
-        count = info_ref[blocks + block]
-        query = load_query(own_ref[item, rows : rows + rows // 2])
-
-        def scores(step, top):
-            score = dot_nt(kv_s[first + step], query) * scale
-            score_s[step] = score
-            return jnp.maximum(top, jnp.max(score.reshape(rows // 8, 8, rows), axis=0))
-
-        top = lax.fori_loop(0, count, scores, jnp.full((8, rows), -jnp.inf, jnp.float32))
-        top = jnp.max(top, axis=0, keepdims=True)
-
-        def weigh(step, total):
-            prob = jnp.exp2(score_s[step] - top).astype(jnp.bfloat16)
-            return total + dot_nn(vt_s[first + step], prob)
-
-        total = lax.fori_loop(0, count, weigh, jnp.zeros((LANES, rows), jnp.float32))
+            kt_ref[2 * chip + which] = turned[:HD].astype(jnp.bfloat16)
+            key_top = jnp.maximum(key_top, square_sums(block))
+        query_top = jnp.maximum(query_top, square_sums(own_ref[chip, rows : rows + rows // 2]))
+        return key_top, query_top
+
+    zero = jnp.zeros((8, LANES), jnp.float32)
+    key_top, query_top = lax.fori_loop(0, chips, gather, (zero, zero))
+    key_top = jnp.max(jnp.where(low_lanes(8), key_top, 0.0))
+    bound = jnp.max(query_top) * key_top * (1.02 * scale * scale)
+
+    def finish(item, total, shift):
         weight = total[0:1]
         context = total[HD:] / weight
         ctxt_ref[item] = context
-        lse_ref[item] = jnp.broadcast_to(top + jnp.log2(weight), (8, rows))
+        lse_ref[item] = jnp.broadcast_to(shift + jnp.log2(weight), (8, rows))
         ctx_ref[item] = pack_transposed(context).astype(jnp.bfloat16)
-        return carry
-
-    lax.fori_loop(0, chips, one_block, 0)
+
+    def items(one_item):
+        def body(item, carry):
+            block = 2 * item + parity
+            query = load_query(own_ref[item, rows : rows + rows // 2])
+            one_item(item, info_ref[block], info_ref[blocks + block], query)
+            return carry
+
+        lax.fori_loop(0, chips, body, 0)
+
+    @pl.when(bound < 3600.0)
+    def _():
+        def one_item(item, first, count, query):
+            total_s[...] = jnp.zeros_like(total_s)
+
+            def step(block, n):
+                keys = kv_s[pl.ds(block, n)].reshape(n * rows, LANES)
+                prob = jnp.exp2(dot_nt(keys, query) * scale).astype(jnp.bfloat16)
+                total = total_s[...]
+                for index in range(n):
+                    part = prob[index * rows : (index + 1) * rows]
+                    total = total + dot_nn(vt_s[block + index], part)
+                total_s[...] = total
+
+            over_blocks(first, count, step)
+            finish(item, total_s[...], 0.0)
+
+        items(one_item)
+
+    @pl.when(jnp.logical_not(bound < 3600.0))
+    def _():
+        def one_item(item, first, count, query):
+            def scores(step, top):
+                score = dot_nt(kv_s[first + step], query) * scale
+                score_s[step] = score
+                return jnp.maximum(top, jnp.max(score.reshape(rows // 8, 8, rows), axis=0))
+
+            top = lax.fori_loop(0, count, scores, jnp.full((8, rows), -jnp.inf, jnp.float32))
+            top = jnp.max(top, axis=0, keepdims=True)
+
+            def weigh(step, total):
+                prob = jnp.exp2(score_s[step] - top).astype(jnp.bfloat16)
+                return total + dot_nn(vt_s[first + step], prob)
+
+            total = lax.fori_loop(0, count, weigh, jnp.zeros((LANES, rows), jnp.float32))
+            finish(item, total, top)
+
+        items(one_item)
 
 
 def whole():
@@ -465,16 +521,18 @@
     return pl.pallas_call(
         attend_body,
         in_specs=[pl.BlockSpec(memory_space=pltpu.SMEM), whole(), whole()],
-        out_specs=[whole(), whole(), whole()],
+        out_specs=[whole()] * 4,
         out_shape=[
             jax.ShapeDtypeStruct((chips, rows // 2, LANES), jnp.bfloat16),
             jax.ShapeDtypeStruct((chips, HD, rows), jnp.float32),
             jax.ShapeDtypeStruct((chips, 8, rows), jnp.float32),
+            jax.ShapeDtypeStruct((blocks, HD, rows), jnp.bfloat16),
         ],
         scratch_shapes=[
             pltpu.VMEM((blocks, rows, LANES), jnp.bfloat16),
             pltpu.VMEM((blocks, LANES, rows), jnp.bfloat16),
             pltpu.VMEM((SPAN, rows, rows), jnp.float32),
+            pltpu.VMEM((LANES, rows), jnp.float32),
         ],
         compiler_params=params(),
         cost_estimate=cost(2 * 2 * 40 * rows * rows * LANES, 4 << 20, 40 * rows * rows),
@@ -483,7 +541,18 @@
 
 
 def attend_back_body(
-    info_ref, own_ref, sib_ref, dctx_ref, ctxt_ref, lse_ref, dkv_ref, dq_ref, kv_s, kt_s, acc_s
+    info_ref,
+    own_ref,
+    sib_ref,
+    dctx_ref,
+    ctxt_ref,
+    lse_ref,
+    kt_ref,
+    dkv_ref,
+    dq_ref,
+    kv_s,
+    acc_s,
+    total_s,
 ):
     chips = own_ref.shape[0]
     blocks = 2 * chips
@@ -494,10 +563,7 @@
 
     def gather(chip, carry):
         for ref, which in ((own_ref, parity), (sib_ref, 1 - parity)):
-            block = ref[chip, 0:rows]
-            kv_s[2 * chip + which] = block
-            turned = block.astype(jnp.float32).T
-            kt_s[2 * chip + which] = turned[0:HD].astype(jnp.bfloat16)
+            kv_s[2 * chip + which] = ref[chip, 0:rows]
             acc_s[2 * chip + which] = jnp.zeros((rows, LANES), jnp.float32)
         return carry
 
@@ -506,8 +572,6 @@
 
     def one_block(item, carry):
         block = 2 * item + parity
-        first = info_ref[block]
-        count = info_ref[blocks + block]
         query = load_query(own_ref[item, rows : rows + half])
         packed = dctx_ref[item].astype(jnp.float32)
         top = jnp.where(low, 0.0, pltpu.roll(packed, HD, 1))
@@ -518,36 +582,40 @@
         delta = jnp.sum(dctx_t * ctxt_ref[item], axis=0, keepdims=True)
         lse = lse_ref[item, 0:1]
         both = jnp.concatenate([query, dctx], axis=0)
-
-        def step_block(step, dq):
-            kv = kv_s[first + step]
+        total_s[...] = jnp.zeros_like(total_s)
+
+        def step(index, n):
+            kv = kv_s[pl.ds(index, n)].reshape(n * rows, LANES)
             prob = jnp.exp2(dot_nt(kv, query) * scale - lse)
-            dprob = dot_nt(kv, dctx)
-            dscore = (0.125 * prob * (dprob - delta)).astype(jnp.bfloat16)
+            dscore = (prob * (dot_nt(kv, dctx) - delta)).astype(jnp.bfloat16)
             pair = jnp.concatenate([dscore, prob.astype(jnp.bfloat16)], axis=1)
-            acc_s[first + step] += dot_nn(pair, both)
-            return dq + dot_nn(kt_s[first + step], dscore)
-
-        dq = lax.fori_loop(0, count, step_block, jnp.zeros((HD, rows), jnp.float32))
-        dq_ref[item] = pack_transposed(dq).astype(jnp.bfloat16)
+            acc_s[pl.ds(index, n)] += dot_nn(pair, both).reshape(n, rows, LANES)
+            total = total_s[...]
+            for part in range(n):
+                total = total + dot_nn(kt_ref[index + part], dscore[part * rows : (part + 1) * rows])
+            total_s[...] = total
+
+        over_blocks(info_ref[block], info_ref[blocks + block], step)
+        dq_ref[item] = pack_transposed(total_s[...] * 0.125).astype(jnp.bfloat16)
         return carry
 
     lax.fori_loop(0, chips, one_block, 0)
+    key_scale = jnp.where(low_lanes(rows), 0.125, 1.0)
 
     def finish(index, carry):
-        dkv_ref[index] = acc_s[index].astype(jnp.bfloat16)
+        dkv_ref[index] = (acc_s[index] * key_scale).astype(jnp.bfloat16)
         return carry
 
     lax.fori_loop(0, blocks, finish, 0)
 
 
-def attend_back(info, own, sib, dctx, ctxt, lse):
+def attend_back(info, own, sib, dctx, ctxt, lse, kt):
     chips, packed, _ = own.shape
     rows = packed * 2 // 3
     blocks = 2 * chips
     return pl.pallas_call(
         attend_back_body,
-        in_specs=[pl.BlockSpec(memory_space=pltpu.SMEM)] + [whole()] * 5,
+        in_specs=[pl.BlockSpec(memory_space=pltpu.SMEM)] + [whole()] * 6,
         out_specs=[whole(), whole()],
         out_shape=[
             jax.ShapeDtypeStruct((blocks, rows, LANES), jnp.bfloat16),
@@ -555,13 +623,41 @@
         ],
         scratch_shapes=[
             pltpu.VMEM((blocks, rows, LANES), jnp.bfloat16),
-            pltpu.VMEM((blocks, HD, rows), jnp.bfloat16),
             pltpu.VMEM((blocks, rows, LANES), jnp.float32),
+            pltpu.VMEM((HD, rows), jnp.float32),
         ],
         compiler_params=params(),
         cost_estimate=cost(2 * 5 * 40 * rows * rows * LANES, 5 << 20, 40 * rows * rows),
         name="attend_back",
-    )(info, own, sib, dctx, ctxt, lse)
+    )(info, own, sib, dctx, ctxt, lse, kt)
+
+
+def combine_body(info_ref, dkv_ref, sib_ref, dq_ref, out_ref):
+    chips, half, _ = dq_ref.shape
+    rows = 2 * half
+    parity = info_ref[4 * chips]
+
+    def one(chip, carry):
+        block = 2 * chip + parity
+        total = dkv_ref[block].astype(jnp.float32) + sib_ref[block].astype(jnp.float32)
+        out_ref[chip, 0:rows] = total.astype(jnp.bfloat16)
+        out_ref[chip, rows : rows + half] = dq_ref[chip]
+        return carry
+
+    lax.fori_loop(0, chips, one, 0)
+
+
+def combine(info, dkv, dkv_sib, dq):
+    chips, half, _ = dq.shape
+    return pl.pallas_call(
+        combine_body,
+        in_specs=[pl.BlockSpec(memory_space=pltpu.SMEM)] + [whole()] * 3,
+        out_specs=whole(),
+        out_shape=jax.ShapeDtypeStruct((chips, 3 * half, LANES), jnp.bfloat16),
+        compiler_params=params(),
+        cost_estimate=cost(1 << 20, 3 << 20),
+        name="combine",
+    )(info, dkv, dkv_sib, dq)
 
 
 def out_project_body(in_ref, w_ref, ctx_ref, own_ref, send_ref):
@@ -596,9 +692,9 @@
     )(packed, w_out)
 
 
-def ctx_grad_body(g_ref, w_ref, out_ref):
+def ctx_grad_body(own_ref, other_ref, w_ref, out_ref):
     half = out_ref.shape[1]
-    grad = dot_nt(g_ref[...], w_ref[...])
+    grad = dot_nt(jnp.concatenate([own_ref[...], other_ref[...]], axis=0), w_ref[...])
     for pair in range(grad.shape[1] // LANES):
         cols = slice(pair * LANES, (pair + 1) * LANES)
         first, second = split_lanes(grad[:half, cols], grad[half:, cols])
@@ -606,18 +702,18 @@
         out_ref[2 * pair + 1] = second.astype(jnp.bfloat16)
 
 
-def ctx_grad_packed(grad_all, w_out):
-    rows, depth = grad_all.shape
+def ctx_grad_packed(grad_own, grad_other, w_out):
+    rows, depth = 2 * grad_own.shape[0], grad_own.shape[1]
     width = w_out.shape[0]
     return pl.pallas_call(
         ctx_grad_body,
-        in_specs=[whole()] * 2,
+        in_specs=[whole()] * 3,
         out_specs=whole(),
         out_shape=jax.ShapeDtypeStruct((width // HD, rows // 2, LANES), jnp.bfloat16),
         compiler_params=params(),
         cost_estimate=cost(2 * rows * width * depth, 2 << 20),
         name="ctx_grad",
-    )(grad_all, w_out)
+    )(grad_own, grad_other, w_out)
 
 
 def head_grad_body(
@@ -629,45 +725,44 @@
     blocks = 2 * chips
     rows = 2 * half
     parity = info_ref[2 * blocks]
-    chip = jnp.where(step < chips // 2, 2 * step, 2 * chips - 1 - 2 * step)
+    group = chips // steps
+    columns = []
+    for index in range(group):
+        place = step * group + index
+        chip = jnp.where(place < chips // 2, 2 * place, 2 * chips - 1 - 2 * place)
+        for core in range(2):
+            block = 2 * chip + core
+            total = dkv_ref[block].astype(jnp.float32) + dkv_sib_ref[block].astype(jnp.float32)
+            dq = jnp.where(
+                parity == core,
+                dq_ref[chip].astype(jnp.float32),
+                dq_sib_ref[chip].astype(jnp.float32),
+            ).T
+            dq = jnp.concatenate([dq[:HD], dq[HD:]], axis=1)
+            columns.append(jnp.concatenate([total.T, dq], axis=0).astype(jnp.bfloat16))
+    part = dot_nn(jnp.concatenate(columns, axis=1), tok_ref[...])
 
     @pl.when(step == 0)
     def _():
-        acc_s[...] = jnp.zeros_like(acc_s)
-
-    for core in range(2):
-        block = 2 * chip + core
-        total = dkv_ref[block].astype(jnp.float32) + dkv_sib_ref[block].astype(jnp.float32)
-        own = (parity == core).astype(jnp.int32)
-        dq = jnp.where(
-            own == 1, dq_ref[chip].astype(jnp.float32), dq_sib_ref[chip].astype(jnp.float32)
-        )
-        dq_t = dq.T
-        dq_t = jnp.concatenate([dq_t[:HD], dq_t[HD:]], axis=1)
-        left = jnp.concatenate([total.T, dq_t], axis=0).astype(jnp.bfloat16)
-        acc_s[...] += dot_nn(left, tok_ref[core * rows : (core + 1) * rows])
-
-        @pl.when(own == 1)
-        def _():
-            out_ref[chip, 0:rows] = total.astype(jnp.bfloat16)
-            out_ref[chip, rows : rows + half] = dq_ref[chip]
+        acc_s[...] = part
+
+    @pl.when(step > 0)
+    def _():
+        acc_s[...] += part
 
     @pl.when(step == steps - 1)
     def _():
         grad = acc_s[...]
         depth = grad.shape[1] // blocks
-        wide = jnp.concatenate([grad[: 2 * HD], grad[2 * HD :], jnp.zeros_like(grad[:HD])], axis=0)
-        turned = wide.T
-        grad_s[...] = turned.reshape(blocks, depth, 2 * LANES)
+        wide = jnp.concatenate([grad, grad[2 * HD :]], axis=0)
+        grad_s[...] = wide.T.reshape(blocks, depth, 2 * LANES)
 
         def pack(index, carry):
             part = grad_s[2 * index + parity]
-            base = rows + half
-            out_ref[index, base : base + depth] = part[:, :LANES].astype(jnp.bfloat16)
+            out_ref[index, 0:depth] = part[:, :LANES].astype(jnp.bfloat16)
             query = part[:, LANES:]
-            low = low_lanes(depth // 2)
-            mixed = jnp.where(low, query[: depth // 2], pltpu.roll(query[depth // 2 :], HD, 1))
-            out_ref[index, base + depth : base + depth + depth // 2] = mixed.astype(jnp.bfloat16)
+            mixed = jnp.where(low_lanes(depth // 2), query[: depth // 2], query[depth // 2 :])
+            out_ref[index, depth : depth + depth // 2] = mixed.astype(jnp.bfloat16)
             return carry
 
         lax.fori_loop(0, chips, pack, 0)
@@ -678,21 +773,21 @@
     chips = blocks // 2
     depth = tokens_all.shape[1]
     piece = depth // blocks
-    height = rows + rows // 2 + piece + piece // 2
+    steps = 4
     full = lambda shape: pl.BlockSpec(shape, lambda i: (0,) * len(shape))
     return pl.pallas_call(
         head_grad_body,
-        grid=(chips,),
+        grid=(steps,),
         in_specs=[
             pl.BlockSpec(memory_space=pltpu.SMEM),
-            pl.BlockSpec((2 * rows, depth), lambda i: (i, 0)),
+            pl.BlockSpec((blocks * rows // steps, depth), lambda i: (i, 0)),
             full(dkv.shape),
             full(dkv.shape),
             full(dq.shape),
             full(dq.shape),
         ],
-        out_specs=full((chips, height, LANES)),
-        out_shape=jax.ShapeDtypeStruct((chips, height, LANES), jnp.bfloat16),
+        out_specs=full((chips, piece + piece // 2, LANES)),
+        out_shape=jax.ShapeDtypeStruct((chips, piece + piece // 2, LANES), jnp.bfloat16),
         scratch_shapes=[
             pltpu.VMEM((3 * HD, depth), jnp.float32),
             pltpu.VMEM((blocks, piece, 2 * LANES), jnp.float32),
@@ -703,12 +798,10 @@
     )(info, tokens_all, dkv, dkv_sib, dq, dq_sib)
 
 
-def token_grad_body(in_ref, wq_ref, wk_ref, wv_ref, own_ref, send_ref, gq_ref, gk_ref, gv_ref, d_s):
+def token_grad_body(in_ref, wq_ref, wk_ref, wv_ref, own_ref, send_ref, d_s):
     heads = in_ref.shape[0]
-    rows, width = d_s.shape[1:]
+    rows = d_s.shape[1]
     half = rows // 2
-    piece = gq_ref.shape[0]
-    base = rows + half
     load = lambda head, lo, hi: in_ref[head, lo:hi].astype(jnp.float32)
     for pair in range(heads // 2):
         cols = slice(pair * LANES, (pair + 1) * LANES)
@@ -716,35 +809,24 @@
         key, value = split_lanes(load(a, 0, rows), load(b, 0, rows))
         d_s[1, :, cols] = key.astype(jnp.bfloat16)
         d_s[2, :, cols] = value.astype(jnp.bfloat16)
-        top, bottom = split_lanes(load(a, rows, base), load(b, rows, base))
+        top, bottom = split_lanes(load(a, rows, rows + half), load(b, rows, rows + half))
         d_s[0, :half, cols] = top.astype(jnp.bfloat16)
         d_s[0, half:, cols] = bottom.astype(jnp.bfloat16)
-        key, value = split_lanes(load(a, base, base + piece), load(b, base, base + piece))
-        gk_ref[:, cols] = key
-        gv_ref[:, cols] = value
-        last = base + piece + piece // 2
-        top, bottom = split_lanes(load(a, base + piece, last), load(b, base + piece, last))
-        gq_ref[: piece // 2, cols] = top
-        gq_ref[piece // 2 :, cols] = bottom
     total = dot_nt(d_s[0], wq_ref[...]) + dot_nt(d_s[1], wk_ref[...]) + dot_nt(d_s[2], wv_ref[...])
     own_ref[...] = total[:half]
     send_ref[...] = total[half:].astype(jnp.bfloat16)
 
 
-def token_grad(packed, rows, wq, wk, wv):
+def token_grad(packed, wq, wk, wv):
     depth, width = wq.shape
-    piece = (packed.shape[1] - rows * 3 // 2) * 2 // 3
-    grad = jax.ShapeDtypeStruct((piece, width), jnp.float32)
+    rows = packed.shape[1] * 2 // 3
     return pl.pallas_call(
         token_grad_body,
         in_specs=[whole()] * 4,
-        out_specs=[whole()] * 5,
+        out_specs=[whole()] * 2,
         out_shape=[
             jax.ShapeDtypeStruct((rows // 2, depth), jnp.float32),
             jax.ShapeDtypeStruct((rows // 2, depth), jnp.bfloat16),
-            grad,
-            grad,
-            grad,
         ],
         scratch_shapes=[pltpu.VMEM((3, rows, width), jnp.bfloat16)],
         compiler_params=params(),
@@ -753,29 +835,115 @@
     )(packed, wq, wk, wv)
 
 
-def ffn_grad_body(up_left, up_right, down_left, down_right, out_ref):
-    width = up_right.shape[1]
-    out_ref[:, :width] = contract_rows(up_left[...], up_right[...]).astype(jnp.bfloat16)
-    out_ref[:, width:] = contract_rows(down_left[...], down_right[...]).astype(jnp.bfloat16)
-
-
-def ffn_grad(chips, up_left, up_right, down_left, down_right):
-    rows, depth = up_left.shape
-    width = up_right.shape[1]
-    tile = depth // chips
-    column = lambda i: (0, jnp.where(i < chips // 2, 2 * i, 2 * chips - 1 - 2 * i))
-    left = pl.BlockSpec((rows, tile), column)
-    right = pl.BlockSpec((rows, width), lambda i: (0, 0))
+def split_heads_body(in_ref, gq_ref, gk_ref, gv_ref):
+    heads = in_ref.shape[0]
+    piece = gq_ref.shape[0]
+    last = piece + piece // 2
+    load = lambda head, lo, hi: in_ref[head, lo:hi].astype(jnp.float32)
+    for pair in range(heads // 2):
+        cols = slice(pair * LANES, (pair + 1) * LANES)
+        a, b = 2 * pair, 2 * pair + 1
+        key, value = split_lanes(load(a, 0, piece), load(b, 0, piece))
+        gk_ref[:, cols] = key
+        gv_ref[:, cols] = value
+        top, bottom = split_lanes(load(a, piece, last), load(b, piece, last))
+        gq_ref[: piece // 2, cols] = top
+        gq_ref[piece // 2 :, cols] = bottom
+
+
+def split_heads(packed):
+    heads, height, _ = packed.shape
+    grad = jax.ShapeDtypeStruct((height * 2 // 3, heads * HD), jnp.float32)
     return pl.pallas_call(
-        ffn_grad_body,
-        grid=(chips,),
-        in_specs=[left, right, left, right],
-        out_specs=pl.BlockSpec((tile, 2 * width), lambda i: (i, 0)),
-        out_shape=jax.ShapeDtypeStruct((depth, 2 * width), jnp.bfloat16),
+        split_heads_body,
+        in_specs=[whole()],
+        out_specs=[whole()] * 3,
+        out_shape=[grad] * 3,
+        compiler_params=params(),
+        cost_estimate=cost(1 << 18, 1 << 20),
+        name="split_heads",
+    )(packed)
+
+
+def late_grad_body(orders, tiles, parts, *refs):
+    *arrays, out_ref, turned_s = refs
+    step = pl.program_id(0)
+    width = out_ref.shape[1]
+    terms = []
+    for count in parts:
+        terms.append((arrays[:count], arrays[count : 2 * count]))
+        arrays = arrays[2 * count :]
+
+    @pl.when(step == 0)
+    def _():
+        for index, (lefts, _) in enumerate(terms):
+            size = lefts[0].shape[1] // len(orders[index])
+            for which, left in enumerate(lefts):
+                half = left.shape[0]
+                for place, chip in enumerate(orders[index]):
+                    piece = left[:, chip * size : (chip + 1) * size].T
+                    rows = slice(place * size, (place + 1) * size)
+                    turned_s[index, rows, which * half : (which + 1) * half] = piece
+
+    start = 0
+    for index, (_, rights) in enumerate(terms):
+
+        @pl.when((step >= start) & (step < start + tiles[index]))
+        def _(index=index, start=start, rights=rights):
+            cols = pl.ds(pl.multiple_of((step - start) * width, width), width)
+            right = jnp.concatenate([ref[:, cols] for ref in rights], axis=0)
+            left = turned_s[index, :, : right.shape[0]]
+            out_ref[...] = dot_nn(left, right).astype(jnp.bfloat16)
+
+        start += tiles[index]
+
+
+def late_grad(chips, terms):
+    half, depth = terms[0][0][0].shape
+    tile = 512
+    orders = [ring_chips(chips) if term[2] else list(range(chips)) for term in terms]
+    arrays = [array for term in terms for group in term[:2] for array in group]
+    tiles = [term[1][0].shape[1] // tile for term in terms]
+    parts = [len(term[0]) for term in terms]
+    width = sum(tiles) * tile
+    fixed = lambda array: pl.BlockSpec(array.shape, lambda i: (0, 0))
+    return pl.pallas_call(
+        functools.partial(late_grad_body, orders, tiles, parts),
+        grid=(sum(tiles),),
+        in_specs=[fixed(array) for array in arrays],
+        out_specs=pl.BlockSpec((depth, tile), lambda i: (0, i)),
+        out_shape=jax.ShapeDtypeStruct((depth, width), jnp.bfloat16),
+        scratch_shapes=[pltpu.VMEM((len(terms), depth, 2 * half), jnp.bfloat16)],
         compiler_params=params("arbitrary"),
-        cost_estimate=cost(4 * rows * depth * width, 12 << 20),
-        name="ffn_grad",
-    )(up_left, up_right, down_left, down_right)
+        cost_estimate=cost(4 * half * depth * width, 2 * depth * width + (3 << 20)),
+        name="late_grad",
+    )(*arrays)
+
+
+def out_grad_body(left_ref, other_ref, ctx_ref, small_ref, out_ref):
+    cores, chips, height, _ = out_ref.shape
+    piece = height - small_ref.shape[0]
+    left = jnp.concatenate([left_ref[...], other_ref[...]], axis=0)
+    grad = contract_rows(left, ctx_ref[...]).astype(jnp.bfloat16)
+    for index in range(cores * chips):
+        place = (index % cores, index // cores)
+        out_ref[place[0], place[1], :piece] = grad[index * piece : (index + 1) * piece]
+        out_ref[place[0], place[1], piece:] = small_ref[...]
+
+
+def out_grad_pack(count, grad_own, grad_other, context_low, small):
+    depth = grad_own.shape[1]
+    rows, width = context_low.shape
+    height = depth // count + small.shape[0]
+    return pl.pallas_call(
+        out_grad_body,
+        in_specs=[whole()] * 4,
+        out_specs=whole(),
+        out_shape=jax.ShapeDtypeStruct((2, count // 2, height, width), jnp.bfloat16),
+        compiler_params=params(),
+        cost_estimate=cost(2 * rows * depth * width, 2 << 20),
+        name="out_grad",
+    )(grad_own, grad_other, context_low, small)
 
 
 def normalized(values):
@@ -838,8 +1006,18 @@
             value, "pass", 0, 0, axis_index_groups=same_core, tiled=True
         )
 
+    def after(value, *others):
+        return lax.optimization_barrier((value,) + others)[0]
+
+    def together(*values):
+        return lax.optimization_barrier(values)
+
     gathered = jnp.concatenate([tokens, swap(tokens)], axis=0)
-    tokens_all = lax.all_gather(gathered, "pass", axis=0, axis_index_groups=ring, tiled=True)
+    block_ids = passage_of.astype(jnp.int32)
+    same = block_ids[:, None] == block_ids[None, :]
+    starts = jnp.sum((block_ids[None, :] < block_ids[:, None]).astype(jnp.int32), axis=1)
+    counts = jnp.sum(same.astype(jnp.int32), axis=1)
+    info = jnp.concatenate([starts, counts, parity[None].astype(jnp.int32)])
 
     seq_count = match_index.shape[1]
     query_rows = cot_scores.shape[0]
@@ -859,27 +1037,29 @@
     weighted_queries = (token_weight[:, None] * query_float).astype(jnp.bfloat16)
     unit_grad_part = contract_rows(one_hot, weighted_queries)
     turned_part = jnp.concatenate([unit_grad_part[own_rows:], unit_grad_part[:own_rows]], axis=0)
-    unit_grad = unit_grad_part + swap(turned_part.astype(jnp.bfloat16)).astype(jnp.float32)
-
-    block_ids = passage_of.astype(jnp.int32)
-    same = block_ids[:, None] == block_ids[None, :]
-    starts = jnp.sum((block_ids[None, :] < block_ids[:, None]).astype(jnp.int32), axis=1)
-    counts = jnp.sum(same.astype(jnp.int32), axis=1)
-    info = jnp.concatenate([starts, counts, parity[None].astype(jnp.int32)])
+    unit_grad_send = turned_part.astype(jnp.bfloat16)
 
     own_pack = to_heads(project(gathered, w_query, w_key, w_value))
+    own_pack, unit_grad_send = together(own_pack, unit_grad_send)
     sib_pack = sibling(own_pack)
-    ctx_pack, ctx_turned, lse = attend(info, own_pack, sib_pack)
-    context_low, attn_own, attn_send = out_project(to_heads(ctx_pack), w_out)
+    unit_grad_recv = swap(unit_grad_send)
+    ctx_pack, ctx_turned, lse, key_turned = attend(info, own_pack, sib_pack)
+    unit_grad = unit_grad_part + unit_grad_recv.astype(jnp.float32)
+    ctx_recv = to_heads(after(ctx_pack, unit_grad_recv))
+    tokens_all = lax.all_gather(
+        after(gathered, ctx_recv), "pass", axis=0, axis_index_groups=ring, tiled=True
+    )
+    context_low, attn_own, attn_send = out_project(ctx_recv, w_out)
     attn_rows = attn_own + swap(attn_send).astype(jnp.float32)
     unit_attn, inverse_attn = normalized(tokens.astype(jnp.float32) + attn_rows)
     hidden = unit_attn * gain_attn + shift_attn
     hidden_low = hidden.astype(jnp.bfloat16)
-    hidden_all = jnp.concatenate([hidden_low, swap(hidden_low)], axis=0)
+    hidden_other = swap(hidden_low)
+    hidden_all = jnp.concatenate([hidden_low, hidden_other], axis=0)
 
     inner_pre = dot_nn(hidden_all, w_up)
     gated, slope = gelu_with_slope(inner_pre)
-    gated_low = gated.astype(jnp.bfloat16)
+    gated_low, slope = lax.optimization_barrier((gated.astype(jnp.bfloat16), slope))
     ffn_part = dot_nn(gated_low, w_down)
     ffn_rows = ffn_part[:own_rows] + swap(ffn_part[own_rows:].astype(jnp.bfloat16)).astype(
         jnp.float32
@@ -887,7 +1067,6 @@
     unit_ffn, inverse_ffn = normalized(hidden + ffn_rows)
     output = unit_ffn * gain_ffn + shift_ffn
     output_low = output.astype(jnp.bfloat16)
-    output_other = swap(output_low)
 
     def colbert(rows, grad_rows):
         proj = dot_nn(rows, w_colbert)
@@ -901,21 +1080,37 @@
     unit_own, proj_own = colbert(output_low, unit_grad[:own_rows])
     out_grad = cot_act.astype(jnp.float32) + dot_nt(proj_own, w_colbert)
     pre_grad = norm_back(out_grad, gain_ffn, unit_ffn, inverse_ffn)
-    grad_gain_ffn = jnp.sum(out_grad * unit_ffn, axis=0)
-    grad_shift_ffn = jnp.sum(out_grad, axis=0)
     pre_low = pre_grad.astype(jnp.bfloat16)
-    ffn_all = jnp.concatenate([pre_low, swap(pre_low)], axis=0)
-
-    unit_other, proj_other = colbert(output_other, unit_grad[own_rows:])
-    output_all = jnp.concatenate([output_low, output_other], axis=0)
-    proj_all = jnp.concatenate([proj_own, proj_other], axis=0)
-    grad_colbert_part = contract_rows(output_all, proj_all).astype(jnp.bfloat16)
-    colbert_piece = lax.psum_scatter(
-        grad_colbert_part, "pass", scatter_dimension=0, axis_index_groups=ring, tiled=True
-    )
-    grad_colbert = lax.all_gather(
-        colbert_piece, "pass", axis=0, axis_index_groups=ring, tiled=True
-    ).astype(jnp.float32)
+    pre_other = swap(pre_low)
+    ffn_all = jnp.concatenate([pre_low, pre_other], axis=0)
+
+    inner_low = (dot_nt(ffn_all, w_down) * slope).astype(jnp.bfloat16)
+    hidden_part = dot_nt(inner_low, w_up)
+    hidden_send = hidden_part[own_rows:].astype(jnp.bfloat16)
+    hidden_recv = swap(hidden_send)
+    inner_late = after(inner_low, hidden_send)
+    width = w_up.shape[1]
+    late = late_grad(
+        chips,
+        (
+            ((hidden_low, hidden_other), (inner_late[:own_rows], inner_late[own_rows:]), True),
+            ((pre_low, pre_other), (gated_low[:own_rows], gated_low[own_rows:]), True),
+            ((output_low,), (proj_own,), False),
+        ),
+    )
+    hidden_recv, late, tokens_all = together(hidden_recv, late, tokens_all)
+    late_sums = lax.psum_scatter(
+        late, "pass", scatter_dimension=0, axis_index_groups=ring, tiled=True
+    )
+
+    hidden_grad = (
+        pre_grad + hidden_part[:own_rows] + hidden_recv.astype(jnp.float32)
+    )
+    attn_pre = norm_back(hidden_grad, gain_attn, unit_attn, inverse_attn)
+    attn_low = attn_pre.astype(jnp.bfloat16)
+    attn_other = swap(attn_low)
+
+    unit_other = swap(after(unit_own, attn_other))
     picked = dot_nn(one_hot, jnp.concatenate([unit_own, unit_other], axis=0))
     per_query = jnp.sum((query_float * picked).reshape(query_rows, -1), axis=1)
     score_block = per_query[:, None] * pick_col.astype(jnp.float32)[None, :]
@@ -924,64 +1119,63 @@
         score_block,
         (qry_index * query_rows, jnp.zeros((), jnp.int32)),
     )
-
-    inner_low = (dot_nt(ffn_all, w_down) * slope).astype(jnp.bfloat16)
-    hidden_part = dot_nt(inner_low, w_up)
-    hidden_grad = (
-        pre_grad
-        + hidden_part[:own_rows]
-        + swap(hidden_part[own_rows:].astype(jnp.bfloat16)).astype(jnp.float32)
-    )
-    ffn_grads = ffn_grad(chips, hidden_all, inner_low, ffn_all, gated_low)
-    ffn_sums = lax.psum_scatter(
-        ffn_grads, "pass", scatter_dimension=0, axis_index_groups=ring, tiled=True
-    )
-    width = w_up.shape[1]
-    grad_up = ffn_sums[:, :width].astype(jnp.float32)
-    grad_down = ffn_sums[:, width:].astype(jnp.float32).T
-
-    attn_pre = norm_back(hidden_grad, gain_attn, unit_attn, inverse_attn)
-    grad_gain_attn = jnp.sum(hidden_grad * unit_attn, axis=0)
-    grad_shift_attn = jnp.sum(hidden_grad, axis=0)
-    attn_low = attn_pre.astype(jnp.bfloat16)
-    attn_all = jnp.concatenate([attn_low, swap(attn_low)], axis=0)
-
+    model = tokens.shape[1]
+    local_width = w_query.shape[1]
     small = jnp.concatenate(
         [
-            grad_gain_attn,
-            grad_shift_attn,
-            grad_gain_ffn,
-            grad_shift_ffn,
+            jnp.sum(hidden_grad * unit_attn, axis=0),
+            jnp.sum(hidden_grad, axis=0),
+            jnp.sum(out_grad * unit_ffn, axis=0),
+            jnp.sum(out_grad, axis=0),
             score_part.reshape(-1),
         ]
-    ).reshape(-1, LANES)
-    for mask in [1 << bit for bit in range(pass_count.bit_length() - 1)]:
-        small = small + swap_over(small, "pass", mask)
-    small = small + swap(small)
-    model = tokens.shape[1]
-    norms = small[: 4 * model // LANES].reshape(4, model)
-    scores = small[4 * model // LANES :].reshape(score_part.shape)
-
-    own_dctx = to_heads(ctx_grad_packed(attn_all, w_out))
-    dkv, dq = attend_back(info, own_pack, sib_pack, own_dctx, ctx_turned, lse)
-    back = head_grad(info, tokens_all, dkv, sibling(dkv), dq, sibling(dq))
-    token_own, token_send, grad_query, grad_key, grad_value = token_grad(
-        to_heads(back), block_rows, w_query, w_key, w_value
-    )
-    grad_tokens = attn_pre + token_own + swap(token_send).astype(jnp.float32)
-
-    grad_out_part = contract_rows(attn_all, context_low).astype(jnp.bfloat16)
-    tile = model // chips
-    grad_out_part = jnp.concatenate(
-        [grad_out_part[tile * chip : tile * (chip + 1)] for chip in ring_chips(chips)], axis=0
-    )
-    grad_out = (
-        lax.psum_scatter(
-            grad_out_part, "pass", scatter_dimension=0, axis_index_groups=ring, tiled=True
-        )
-        .astype(jnp.float32)
-        .T
-    )
+    )
+    small_rows = -(-small.shape[0] // (16 * local_width)) * 16
+    small_low = (
+        jnp.pad(small, (0, small_rows * local_width - small.shape[0]))
+        .astype(jnp.bfloat16)
+        .reshape(small_rows, local_width)
+    )
+
+    dctx_send = ctx_grad_packed(attn_low, attn_other, w_out)
+    own_dctx = to_heads(dctx_send)
+    out_pack = out_grad_pack(
+        pass_count, after(attn_low, dctx_send), attn_other, context_low, small_low
+    )
+    own_dctx, out_pack = together(own_dctx, out_pack)
+    dkv, dq = attend_back(info, own_pack, sib_pack, own_dctx, ctx_turned, lse, key_turned)
+    dkv_sib, dq_sib = together(sibling(dkv), sibling(dq))
+    back_send = combine(info, dkv, dkv_sib, dq)
+    back = to_heads(back_send)
+    dkv, out_pack = after(dkv, back_send), after(out_pack, back_send)
+    out_mine = lax.dynamic_index_in_dim(out_pack, parity, 0, keepdims=False)
+    out_send = lax.dynamic_index_in_dim(out_pack, 1 - parity, 0, keepdims=False)
+    out_both = out_mine.astype(jnp.float32) + sibling(out_send).astype(jnp.float32)
+    head_grads = head_grad(info, tokens_all, dkv, dkv_sib, dq, dq_sib)
+    back, head_grads, out_both = together(back, head_grads, out_both.astype(jnp.bfloat16))
+    head_recv = to_heads(head_grads)
+    out_recv = to_heads(out_both)
+    token_own, token_send = token_grad(back, w_query, w_key, w_value)
+    head_recv, token_send = together(head_recv, token_send)
+    token_recv = swap(token_send)
+    grad_tokens = attn_pre + token_own + token_recv.astype(jnp.float32)
+    out_recv = after(out_recv, token_recv)
+    grad_query, grad_key, grad_value = split_heads(head_recv)
+
+    grad_up = late_sums[:, :width].astype(jnp.float32)
+    grad_down = late_sums[:, width : 2 * width].astype(jnp.float32).T
+    colbert_piece = after(late_sums, back)[:, 2 * width :]
+    colbert_sum = colbert_piece.astype(jnp.float32) + swap(colbert_piece).astype(jnp.float32)
+    grad_colbert = lax.all_gather(
+        colbert_sum.astype(jnp.bfloat16), "pass", axis=0, axis_index_groups=ring, tiled=True
+    ).astype(jnp.float32)
+
+    out_sums = jnp.sum(out_recv.astype(jnp.float32), axis=0)
+    grad_out = out_sums[: model // pass_count].T
+    small_sums = out_sums[model // pass_count :]
+    small_sums = (small_sums + swap(small_sums)).reshape(-1)
+    norms = small_sums[: 4 * model].reshape(4, model)
+    scores = small_sums[4 * model : small.shape[0]].reshape(score_part.shape)
     return (
         output_low,
         scores,

time: 389 us -> 293 us (0.75)
  waiting for transfers between devices: 168 us -> 77.5 us
  blocking collectives: 43.3 us -> 29.5 us
  local copies, waits for them, and re-layouts: 12.8 us -> 18.6 us
  starting transfers between devices: 32.2 us -> 37.8 us
  matrix products: 21 us -> 15.5 us
    reduce_scatter x3 -> x1, waiting for transfers between devices: 67.6 us -> 0.01 us  [local_by_head(): lax.psum_scatter(late, 'pass', scatter_dimension=0, axis_index_groups=rin...]
    all_to_all x2 -> x4, waiting for transfers between devices: 2.21 us -> 32.8 us  [to_heads(): lax.all_to_all(value, 'pass', 0, 0, axis_index_groups=same_core, tiled=True)]
    all_gather x2, waiting for transfers between devices: 29.9 us -> 0.01 us  [the longest x1 0.01 us: local_by_head(): lax.all_gather(after(gathered, ctx_recv), 'pass', axis=0, axis_index_grou...]
    ppermute x18 -> x16, waiting for transfers between devices: 67.7 us -> 44.7 us  [swap_over(): lax.ppermute(value, axis, [(index, index ^ mask) for index in range(count)])]
    all_to_all x2, blocking collectives: 43.3 us -> 29.5 us  [to_heads(): lax.all_to_all(value, 'pass', 0, 0, axis_index_groups=same_core, tiled=True)]
    all_to_all x2 -> x4, starting transfers between devices: 7.14 us -> 18.9 us  [to_heads(): lax.all_to_all(value, 'pass', 0, 0, axis_index_groups=same_core, tiled=True)]
    pallas_call x1, Pallas kernels: 22.5 us -> 15.6 us  [attend_back(): pl.pallas_call(attend_back_body, in_specs=[pl.BlockSpec(memory_space=pltp...]
    ppermute x18 -> x16, starting transfers between devices: 24.7 us -> 18.6 us  [swap_over(): lax.ppermute(value, axis, [(index, index ^ mask) for index in range(count)])]
  transfers between devices with their start and end apart: 25 -> 23, of which waited for: 20 -> 15; matrix products, arithmetic and copies ran while one was open for 10% -> 15% of each run, Pallas kernels for 13% -> 25%
where the time goes in v2:
time: 293 us; the launch traced here: 291 us
  waiting for transfers between devices  77.5 us (26%)
  Pallas kernels  75.8 us (26%)
  starting transfers between devices  37.8 us (13%)
  blocking collectives  29.5 us (10%)
  other arithmetic  20.2 us (7%)
  local copies, waits for them, and re-layouts  18.6 us (6%)
  between operations  15.6 us (5%)
  matrix products  15.5 us (5%)
    ppermute x16, waiting for transfers between devices, swap_over(): lax.ppermute(value, axis, [(index, index ^ mask) for index in range(count)])  44.7 us
    all_to_all x4, waiting for transfers between devices, to_heads(): lax.all_to_all(value, 'pass', 0, 0, axis_index_groups=same_core, tiled=True)  32.8 us
    all_to_all x2, blocking collectives, to_heads(): lax.all_to_all(value, 'pass', 0, 0, axis_index_groups=same_core, tiled=True)  29.5 us
    pallas_call x1, Pallas kernels, attend(): pl.pallas_call(attend_body, in_specs=[pl.BlockSpec(memory_space=pltpu.SME...  21.9 us
    all_to_all x4, starting transfers between devices, to_heads(): lax.all_to_all(value, 'pass', 0, 0, axis_index_groups=same_core, tiled=True)  18.9 us
    ppermute x16, starting transfers between devices, swap_over(): lax.ppermute(value, axis, [(index, index ^ mask) for index in range(count)])  18.6 us
    pallas_call x1, Pallas kernels, attend_back(): pl.pallas_call(attend_back_body, in_specs=[pl.BlockSpec(memory_space=pltp...  15.6 us
    unnamed x78, local copies, waits for them, and re-layouts  11 us
  transfers between devices with their start and end apart: 23, of which 15 were waited for; matrix products, arithmetic and copies ran while one was open for 15% of the time, Pallas kernels for 25%

profile of v2, /device:TPU:0, one launch (start us, length us, event | category | flops | bytes accessed | tf_op | source)
XLA Modules:
  0.0 290.5 jit_solution(521666616787070234)
XLA Ops:
  11.2 5.5 %collective-permute-done = bf16[128,1024]{1,0:T(8,128)(2,1)S(1)} collective-permute-done((bf16[128,1024]{1,0:T(8,128)(2,1)}, bf16[128,1024]{1,0:T(8,128)(2,1)S(1)}, u32[]{:S(2)}, u32[]{:S(2)}) %collective-permute-start) | collective-permute-done | bytes 262176 | tf_op jit(solution)/shard_map/ppermute | solution.py:322
  17.5 3.9 %project.1 = bf16[8,384,128]{2,1,0:T(8,128)(2,1)} custom-call(bf16[256,1024]{1,0:T(8,128)(2,1)} %copy-done.5, bf16[1024,512]{1,0:T(8,128)(2,1)} %wq_ref.3, bf16[1024,512]{1,0:T(8,128)(2,1)} %wk_ref.3, bf16[1024,512]{1,0:T(8,128)(2,1)} %wv_ref.3), custom_call_target="tpu_custom_call" | custom-call | flops 805306368 | bytes 5242880 | tf_op jit(solution)/shard_map/project/pallas_call | solution.py:385
  21.5 6.1 %all-to-all-start = ((bf16[8,384,128]{2,1,0:T(8,128)(2,1)}), bf16[8,384,128]{2,1,0:T(8,128)(2,1)S(1)}, u32[]{:S(2)}, u32[]{:S(2)}) async-start(bf16[8,384,128]{2,1,0:T(8,128)(2,1)} %project.1), calls=%async_computation | async-start | bytes 1572864 | tf_op jit(solution)/shard_map/all_to_all | solution.py:1005
  31.7 3.9 %copy.35 = bf16[1024,1024]{0,1:T(8,128)(2,1)} copy(bf16[1024,1024]{1,0:T(8,128)(2,1)} %param.29) | data formatting | bytes 4194304 | tf_op args[12]
  40.3 6.6 %all-to-all-done.own_ref = bf16[8,384,128]{2,1,0:T(8,128)(2,1)S(1)} async-done(((bf16[8,384,128]{2,1,0:T(8,128)(2,1)}), bf16[8,384,128]{2,1,0:T(8,128)(2,1)S(1)}, u32[]{:S(2)}, u32[]{:S(2)}) %all-to-all-start) | async-done | bytes 786464 | tf_op jit(solution)/shard_map/all_to_all | solution.py:1005
  49.4 21.9 %attend.1 = (bf16[8,128,128]{2,1,0:T(8,128)(2,1)}, f32[8,64,256]{2,1,0:T(8,128)}, f32[8,8,256]{2,1,0:T(8,128)}, bf16[16,64,256]{2,1,0:T(8,128)(2,1)}) custom-call(s32[33]{0:T(128)} %pad_add_fusion.info_ref, bf16[8,384,128]{2,1,0:T(8,128)(2,1)} %copy-done.17, bf16[8,384,128]{2,1,0:T(8,128)(2,1)} %collective-permute-done.1.sib_ref), custom_call_target="tpu_custom_call" | custom-call | flops 1342177280 | bytes 4194304 | tf_op jit(solution)/shard_map/attend/pallas_call | solution.py:521
  71.2 13.7 %all_to_all.30.in_ref = bf16[8,128,128]{2,1,0:T(8,128)(2,1)} all-to-all(bf16[8,128,128]{2,1,0:T(8,128)(2,1)} %get-tuple-element.56), channel_id=1, replica_groups={{0,4,8,12,16,20,24,28},{2,6,10,14,18,22,26,30},{1,5,9,13,17,21,25,29},{..., dimensions={0} | all-to-all | bytes 524288 | tf_op jit(solution)/shard_map/all_to_all | solution.py:1005
  89.3 5.7 %collective-permute-done.3 = bf16[128,1024]{1,0:T(8,128)(2,1)S(1)} collective-permute-done((bf16[128,1024]{1,0:T(8,128)(2,1)}, bf16[128,1024]{1,0:T(8,128)(2,1)S(1)}, u32[]{:S(2)}, u32[]{:S(2)}) %collective-permute-start.3) | collective-permute-done | bytes 262176 | tf_op jit(solution)/shard_map/ppermute | solution.py:322
  98.2 4.9 %collective-permute-done.4.refs_1_ = bf16[128,1024]{1,0:T(8,128)(2,1)S(1)} collective-permute-done((bf16[128,1024]{1,0:T(8,128)(2,1)S(1)}, bf16[128,1024]{1,0:T(8,128)(2,1)S(1)}, u32[]{:S(2)}, u32[]{:S(2)}) %collective-permute-start.4) | collective-permute-done | bytes 262176 | tf_op jit(solution)/shard_map/ppermute | solution.py:322
  103.1 3.8 %fusion.6 = (f32[256,2048]{1,0:T(8,128)S(1)}, bf16[256,2048]{1,0:T(8,128)(2,1)S(1)}) fusion(bf16[1024,2048]{1,0:T(8,128)(2,1)} %param.24, bf16[128,1024]{1,0:T(8,128)(2,1)S(1)} %collective-permute-done.4.refs_1_, bf16[128,1024]{1,0:T(8,128)(2,1)S(1)} %fusion.27.refs_0_), kind=kOutput, calls=%fused_computation.10 | convolution fusion | flops 1080033280 | bytes 7864320 | tf_op jit(solution)/shard_map/dot_general | solution.py:343
  109.8 4.9 %collective-permute-done.5 = bf16[128,1024]{1,0:T(8,128)(2,1)S(1)} collective-permute-done((bf16[128,1024]{1,0:T(8,128)(2,1)S(1)}, bf16[128,1024]{1,0:T(8,128)(2,1)S(1)}, u32[]{:S(2)}, u32[]{:S(2)}) %collective-permute-start.5) | collective-permute-done | bytes 262176 | tf_op jit(solution)/shard_map/ppermute | solution.py:322
  121.3 3.8 %collective-permute-done.6.refs_5_ = bf16[128,1024]{1,0:T(8,128)(2,1)S(1)} collective-permute-done((bf16[128,1024]{1,0:T(8,128)(2,1)S(1)}, bf16[128,1024]{1,0:T(8,128)(2,1)S(1)}, u32[]{:S(2)}, u32[]{:S(2)}) %collective-permute-start.6) | collective-permute-done | bytes 262176 | tf_op jit(solution)/shard_map/ppermute | solution.py:322
  130.5 10.5 %late_grad.1 = bf16[1024,5120]{1,0:T(8,128)(2,1)} custom-call(bf16[128,1024]{1,0:T(8,128)(2,1)} %copy-done.12, bf16[128,1024]{1,0:T(8,128)(2,1)} %copy-done.20, bf16[128,2048]{1,0:T(8,128)(2,1)} %get-tuple-element.146.refs_2_, bf16[128,2048]{1,0:T(8,128)(2,1)} %get-tuple-element.145.refs_3_, bf16[128,1024]{1,0:T(8,128)(2,1)} %copy-done.9, ...), custom_call_target="tpu_custom_call" | custom-call | flops 2684354560 | bytes 13631488 | tf_op jit(solution)/shard_map/late_grad/pallas_call | solution.py:910
  143.4 8.2 %collective-permute-done.8.other_ref = bf16[128,1024]{1,0:T(8,128)(2,1)S(1)} collective-permute-done((bf16[128,1024]{1,0:T(8,128)(2,1)S(1)}, bf16[128,1024]{1,0:T(8,128)(2,1)S(1)}, u32[]{:S(2)}, u32[]{:S(2)}) %collective-permute-start.8) | collective-permute-done | bytes 262176 | tf_op jit(solution)/shard_map/ppermute | solution.py:322
  155.0 5.7 %all-to-all-start.2 = ((bf16[8,128,128]{2,1,0:T(8,128)(2,1)}), bf16[8,128,128]{2,1,0:T(8,128)(2,1)S(1)}, u32[]{:S(2)}, u32[]{:S(2)}) async-start(bf16[8,128,128]{2,1,0:T(8,128)(2,1)} %ctx_grad.1), calls=%async_computation.2 | async-start | bytes 524288 | tf_op jit(solution)/shard_map/all_to_all | solution.py:1005
  167.0 3.8 %all-to-all-done.2.dctx_ref = bf16[8,128,128]{2,1,0:T(8,128)(2,1)S(1)} async-done(((bf16[8,128,128]{2,1,0:T(8,128)(2,1)}), bf16[8,128,128]{2,1,0:T(8,128)(2,1)S(1)}, u32[]{:S(2)}, u32[]{:S(2)}) %all-to-all-start.2) | async-done | bytes 262176 | tf_op jit(solution)/shard_map/all_to_all | solution.py:1005
  171.5 15.6 %attend_back.1 = (bf16[16,256,128]{2,1,0:T(8,128)(2,1)}, bf16[8,128,128]{2,1,0:T(8,128)(2,1)}) custom-call(s32[33]{0:T(128)} %pad_add_fusion.info_ref, bf16[8,384,128]{2,1,0:T(8,128)(2,1)} %copy-done.17, bf16[8,384,128]{2,1,0:T(8,128)(2,1)} %collective-permute-done.1.sib_ref, bf16[8,128,128]{2,1,0:T(8,128)(2,1)} %copy-done.24, ...), custom_call_target="tpu_custom_call" | custom-call | flops 3355443200 | bytes 5242880 | tf_op jit(solution)/shard_map/attend_back/pallas_call | solution.py:616
  199.0 7.4 %head_grad.1 = bf16[8,96,128]{2,1,0:T(8,128)(2,1)} custom-call(s32[33]{0:T(128)} %pad_add_fusion.info_ref, bf16[4096,1024]{1,0:T(8,128)(2,1)} %all-gather.3.cloned.1.call-done.tok_ref, bf16[16,256,128]{2,1,0:T(8,128)(2,1)} %get-tuple-element.75.dkv_ref, bf16[16,256,128]{2,1,0:T(8,128)(2,1)} %copy-done.4, bf16[8,128,128]{2,1,0:T(8,128)(2,1)} %get-tuple-element.72.dq_ref, ...), custom_call_target="tpu_custom_call" | custom-call | flops 1610612736 | bytes 8388608 | tf_op jit(solution)/shard_map/head_grad/pallas_call | solution.py:778
  208.6 14.5 %all-to-all-done.3.in_ref = bf16[8,384,128]{2,1,0:T(8,128)(2,1)S(1)} async-done(((bf16[8,384,128]{2,1,0:T(8,128)(2,1)}), bf16[8,384,128]{2,1,0:T(8,128)(2,1)S(1)}, u32[]{:S(2)}, u32[]{:S(2)}) %all-to-all-start.3) | async-done | bytes 786464 | tf_op jit(solution)/shard_map/all_to_all | solution.py:1005
  225.6 3.6 %collective-permute-done.15 = bf16[64,1024]{1,0:T(8,128)(2,1)S(1)} collective-permute-done((bf16[64,1024]{1,0:T(8,128)(2,1)S(1)}, bf16[64,1024]{1,0:T(8,128)(2,1)S(1)}, u32[]{:S(2)}, u32[]{:S(2)}) %collective-permute-start.15) | collective-permute-done | bytes 131104 | tf_op jit(solution)/shard_map/ppermute | solution.py:322
  230.8 15.9 %all_to_all.31.in_ref = bf16[8,96,128]{2,1,0:T(8,128)(2,1)} all-to-all(bf16[8,96,128]{2,1,0:T(8,128)(2,1)S(1)} %copy-done.18), channel_id=1, replica_groups={{0,4,8,12,16,20,24,28},{2,6,10,14,18,22,26,30},{1,5,9,13,17,21,25,29},{..., dimensions={0} | all-to-all | bytes 393216 | tf_op jit(solution)/shard_map/all_to_all | solution.py:1005
  250.2 4.0 %token_grad.1 = (f32[128,1024]{1,0:T(8,128)}, bf16[128,1024]{1,0:T(8,128)(2,1)}) custom-call(bf16[8,384,128]{2,1,0:T(8,128)(2,1)} %copy-done.6, bf16[1024,512]{1,0:T(8,128)(2,1)} %wq_ref.3, bf16[1024,512]{1,0:T(8,128)(2,1)} %wk_ref.3, bf16[1024,512]{1,0:T(8,128)(2,1)} %wv_ref.3), custom_call_target="tpu_custom_call" | custom-call | flops 805306368 | bytes 5242880 | tf_op jit(solution)/shard_map/token_grad/pallas_call | solution.py:823
  262.8 7.8 %all-to-all-done.4 = bf16[8,80,512]{2,1,0:T(8,128)(2,1)S(1)} async-done(((bf16[8,80,512]{2,1,0:T(8,128)(2,1)}), bf16[8,80,512]{2,1,0:T(8,128)(2,1)S(1)}, u32[]{:S(2)}, u32[]{:S(2)}) %all-to-all-start.4) | async-done | bytes 655392 | tf_op jit(solution)/shard_map/all_to_all | solution.py:1005
  279.9 4.1 %convert_element_type.139 = f32[1024,1024]{1,0:T(8,128)} convert(bf16[1024,1024]{1,0:T(8,128)(2,1)} %all-gather.5.cloned.1.call-done) | non-fusion elementwise | flops 1048576 | bytes 6291456 | tf_op jit(solution)/shard_map/convert_element_type | solution.py:1171
  (182 shorter events, 89.0 us)
Async XLA Ops:
  7.2 108.2 %copy-start = (bf16[1024,1024]{1,0:T(8,128)(2,1)S(1)}, bf16[1024,1024]{1,0:T(8,128)(2,1)}, u32[]{:S(2)}) copy-start(bf16[1024,1024]{1,0:T(8,128)(2,1)} %param.28) | copy-start | bytes 6291460
  7.2 9.5 %collective-permute-start = (bf16[128,1024]{1,0:T(8,128)(2,1)}, bf16[128,1024]{1,0:T(8,128)(2,1)S(1)}, u32[]{:S(2)}, u32[]{:S(2)}) collective-permute-start(bf16[128,1024]{1,0:T(8,128)(2,1)} %param.17), channel_id=1, source_target_pairs={{0,1},{1,0},{2,3},{3,2},{4,5},{5,4},{6,7},{7,6},{8,9},{9,8},{10,11... | collective-permute-start | bytes 786440 | tf_op jit(solution)/shard_map/ppermute | solution.py:322
  21.5 25.5 %all-to-all-start = ((bf16[8,384,128]{2,1,0:T(8,128)(2,1)}), bf16[8,384,128]{2,1,0:T(8,128)(2,1)S(1)}, u32[]{:S(2)}, u32[]{:S(2)}) async-start(bf16[8,384,128]{2,1,0:T(8,128)(2,1)} %project.1), calls=%async_computation | async-start | bytes 1572864 | tf_op jit(solution)/shard_map/all_to_all | solution.py:1005
  27.6 113.5 %all-gather.3.cloned.1.call-start = ((), (), s32[]{:S(2)}) async-start(), calls=%async_computation.7 | async-start | bytes 8912896 | tf_op jit(solution)/shard_map/all_gather | solution.py:1049
  46.9 2.4 collective-permute-start.1
  46.9 24.3 %collective-permute-start.2 = (bf16[256,1024]{1,0:T(8,128)(2,1)}, bf16[256,1024]{1,0:T(8,128)(2,1)S(1)}, u32[]{:S(2)}, u32[]{:S(2)}) collective-permute-start(bf16[256,1024]{1,0:T(8,128)(2,1)} %pad_maximum_fusion), channel_id=1, source_target_pairs={{0,1},{1,0},{2,3},{3,2},{4,5},{5,4},{6,7},{7,6},{8,9},{9,8},{10,11... | collective-permute-start | bytes 1572872 | tf_op jit(solution)/shard_map/ppermute | solution.py:322
  84.9 138.2 %reduce-scatter.2.cloned.1.call-start = ((), (), s32[]{:S(2)}) async-start(), calls=%async_computation.8 | async-start | bytes 11141120 | tf_op jit(solution)/shard_map/reduce_scatter | solution.py:1102
  87.8 7.2 %collective-permute-start.3 = (bf16[128,1024]{1,0:T(8,128)(2,1)}, bf16[128,1024]{1,0:T(8,128)(2,1)S(1)}, u32[]{:S(2)}, u32[]{:S(2)}) collective-permute-start(bf16[128,1024]{1,0:T(8,128)(2,1)} %get-tuple-element.58), channel_id=1, source_target_pairs={{0,1},{1,0},{2,3},{3,2},{4,5},{5,4},{6,7},{7,6},{8,9},{9,8},{10,11... | collective-permute-start | bytes 786440 | tf_op jit(solution)/shard_map/ppermute | solution.py:322
  96.6 6.4 %collective-permute-start.4 = (bf16[128,1024]{1,0:T(8,128)(2,1)S(1)}, bf16[128,1024]{1,0:T(8,128)(2,1)S(1)}, u32[]{:S(2)}, u32[]{:S(2)}) collective-permute-start(bf16[128,1024]{1,0:T(8,128)(2,1)S(1)} %fusion.27.refs_0_), channel_id=1, source_target_pairs={{0,1},{1,0},{2,3},{3,2},{4,5},{5,4},{6,7},{7,6},{8,9},{9,8},{10,11... | collective-permute-start | bytes 786440 | tf_op jit(solution)/shard_map/ppermute | solution.py:322
  108.3 6.4 %collective-permute-start.5 = (bf16[128,1024]{1,0:T(8,128)(2,1)S(1)}, bf16[128,1024]{1,0:T(8,128)(2,1)S(1)}, u32[]{:S(2)}, u32[]{:S(2)}) collective-permute-start(bf16[128,1024]{1,0:T(8,128)(2,1)S(1)} %slice.144), channel_id=1, source_target_pairs={{0,1},{1,0},{2,3},{3,2},{4,5},{5,4},{6,7},{7,6},{8,9},{9,8},{10,11... | collective-permute-start | bytes 786440 | tf_op jit(solution)/shard_map/ppermute | solution.py:322
  118.6 6.4 %collective-permute-start.6 = (bf16[128,1024]{1,0:T(8,128)(2,1)S(1)}, bf16[128,1024]{1,0:T(8,128)(2,1)S(1)}, u32[]{:S(2)}, u32[]{:S(2)}) collective-permute-start(bf16[128,1024]{1,0:T(8,128)(2,1)S(1)} %get-tuple-element.135.refs_4_), channel_id=1, source_target_pairs={{0,1},{1,0},{2,3},{3,2},{4,5},{5,4},{6,7},{7,6},{8,9},{9,8},{10,11... | collective-permute-start | bytes 786440 | tf_op jit(solution)/shard_map/ppermute | solution.py:322
  127.9 13.1 %collective-permute-start.7 = (bf16[128,1024]{1,0:T(8,128)(2,1)S(1)}, bf16[128,1024]{1,0:T(8,128)(2,1)S(1)}, u32[]{:S(2)}, u32[]{:S(2)}) collective-permute-start(bf16[128,1024]{1,0:T(8,128)(2,1)S(1)} %slice.143), channel_id=1, source_target_pairs={{0,1},{1,0},{2,3},{3,2},{4,5},{5,4},{6,7},{7,6},{8,9},{9,8},{10,11... | collective-permute-start | bytes 786440 | tf_op jit(solution)/shard_map/ppermute | solution.py:322
  142.8 8.8 %collective-permute-start.8 = (bf16[128,1024]{1,0:T(8,128)(2,1)S(1)}, bf16[128,1024]{1,0:T(8,128)(2,1)S(1)}, u32[]{:S(2)}, u32[]{:S(2)}) collective-permute-start(bf16[128,1024]{1,0:T(8,128)(2,1)S(1)} %get-tuple-element.64.own_ref.left_ref), channel_id=1, source_target_pairs={{0,1},{1,0},{2,3},{3,2},{4,5},{5,4},{6,7},{7,6},{8,9},{9,8},{10,11... | collective-permute-start | bytes 786440 | tf_op jit(solution)/shard_map/ppermute | solution.py:322
  151.6 9.1 %collective-permute-start.9 = (bf16[128,1024]{1,0:T(8,128)(2,1)S(1)}, bf16[128,1024]{1,0:T(8,128)(2,1)S(1)}, u32[]{:S(2)}, u32[]{:S(2)}) collective-permute-start(bf16[128,1024]{1,0:T(8,128)(2,1)S(1)} %copy-done.22), channel_id=1, source_target_pairs={{0,1},{1,0},{2,3},{3,2},{4,5},{5,4},{6,7},{7,6},{8,9},{9,8},{10,11... | collective-permute-start | bytes 786440 | tf_op jit(solution)/shard_map/ppermute | solution.py:322
  155.0 15.8 %all-to-all-start.2 = ((bf16[8,128,128]{2,1,0:T(8,128)(2,1)}), bf16[8,128,128]{2,1,0:T(8,128)(2,1)S(1)}, u32[]{:S(2)}, u32[]{:S(2)}) async-start(bf16[8,128,128]{2,1,0:T(8,128)(2,1)} %ctx_grad.1), calls=%async_computation.2 | async-start | bytes 524288 | tf_op jit(solution)/shard_map/all_to_all | solution.py:1005
  187.1 3.5 %collective-permute-start.10 = (bf16[16,256,128]{2,1,0:T(8,128)(2,1)}, bf16[16,256,128]{2,1,0:T(8,128)(2,1)S(1)}, u32[]{:S(2)}, u32[]{:S(2)}) collective-permute-start(bf16[16,256,128]{2,1,0:T(8,128)(2,1)} %get-tuple-element.75.dkv_ref), channel_id=1, source_target_pairs={{0,2},{2,0},{4,6},{6,4},{8,10},{10,8},{12,14},{14,12},{16,18},{18,... | collective-permute-start | bytes 3145736 | tf_op jit(solution)/shard_map/ppermute | solution.py:322
  187.1 3.5 %collective-permute-start.11 = (bf16[8,128,128]{2,1,0:T(8,128)(2,1)}, bf16[8,128,128]{2,1,0:T(8,128)(2,1)S(1)}, u32[]{:S(2)}, u32[]{:S(2)}) collective-permute-start(bf16[8,128,128]{2,1,0:T(8,128)(2,1)} %get-tuple-element.72.dq_ref), channel_id=1, source_target_pairs={{0,2},{2,0},{4,6},{6,4},{8,10},{10,8},{12,14},{14,12},{16,18},{18,... | collective-permute-start | bytes 786440 | tf_op jit(solution)/shard_map/ppermute | solution.py:322
  194.3 28.8 %all-to-all-start.3 = ((bf16[8,384,128]{2,1,0:T(8,128)(2,1)}), bf16[8,384,128]{2,1,0:T(8,128)(2,1)S(1)}, u32[]{:S(2)}, u32[]{:S(2)}) async-start(bf16[8,384,128]{2,1,0:T(8,128)(2,1)} %combine.1), calls=%async_computation.3 | async-start | bytes 1572864 | tf_op jit(solution)/shard_map/all_to_all | solution.py:1005
  197.9 82.0 %all-gather.5.cloned.1.call-start = ((), (), s32[]{:S(2)}) async-start(), calls=%async_computation.9 | async-start | bytes 2228224 | tf_op jit(solution)/shard_map/all_gather | solution.py:1169
  198.8 7.6 %collective-permute-start.12 = (bf16[8,80,512]{2,1,0:T(8,128)(2,1)}, bf16[8,80,512]{2,1,0:T(8,128)(2,1)}, u32[]{:S(2)}, u32[]{:S(2)}) collective-permute-start(bf16[8,80,512]{2,1,0:T(8,128)(2,1)} %dynamic-slice_bitcast_fusion), channel_id=1, source_target_pairs={{0,2},{2,0},{4,6},{6,4},{8,10},{10,8},{12,14},{14,12},{16,18},{18,... | collective-permute-start | bytes 1966088 | tf_op jit(solution)/shard_map/ppermute | solution.py:322
  224.2 5.0 %collective-permute-start.15 = (bf16[64,1024]{1,0:T(8,128)(2,1)S(1)}, bf16[64,1024]{1,0:T(8,128)(2,1)S(1)}, u32[]{:S(2)}, u32[]{:S(2)}) collective-permute-start(bf16[64,1024]{1,0:T(8,128)(2,1)S(1)} %slice.97), channel_id=1, source_target_pairs={{0,1},{1,0},{2,3},{3,2},{4,5},{5,4},{6,7},{7,6},{8,9},{9,8},{10,11... | collective-permute-start | bytes 393224 | tf_op jit(solution)/shard_map/ppermute | solution.py:322
  246.7 23.9 %all-to-all-start.4 = ((bf16[8,80,512]{2,1,0:T(8,128)(2,1)}), bf16[8,80,512]{2,1,0:T(8,128)(2,1)S(1)}, u32[]{:S(2)}, u32[]{:S(2)}) async-start(bf16[8,80,512]{2,1,0:T(8,128)(2,1)} %fusion.10), calls=%async_computation.4 | async-start | bytes 1310720 | tf_op jit(solution)/shard_map/all_to_all | solution.py:1005
  254.3 6.6 %collective-permute-start.13 = (bf16[128,1024]{1,0:T(8,128)(2,1)}, bf16[128,1024]{1,0:T(8,128)(2,1)S(1)}, u32[]{:S(2)}, u32[]{:S(2)}) collective-permute-start(bf16[128,1024]{1,0:T(8,128)(2,1)} %get-tuple-element.83), channel_id=1, source_target_pairs={{0,1},{1,0},{2,3},{3,2},{4,5},{5,4},{6,7},{7,6},{8,9},{9,8},{10,11... | collective-permute-start | bytes 786440 | tf_op jit(solution)/shard_map/ppermute | solution.py:322
  270.7 4.0 %collective-permute-start.14 = (f32[16,512]{1,0:T(8,128)S(1)}, f32[16,512]{1,0:T(8,128)S(1)}, u32[]{:S(2)}, u32[]{:S(2)}) collective-permute-start(f32[16,512]{1,0:T(8,128)S(1)} %slice.110), channel_id=1, source_target_pairs={{0,1},{1,0},{2,3},{3,2},{4,5},{5,4},{6,7},{7,6},{8,9},{9,8},{10,11... | collective-permute-start | bytes 98312 | tf_op jit(solution)/shard_map/ppermute | solution.py:322
  (32 other events, 252.7 us)
Sparse Core Ops, SparseCore 0:
  85.0 48.5 all-gather.2
  141.2 72.7 reduce-scatter.1
  230.9 41.3 all-gather.4

commit v3 on v2

--- a/solution.py
+++ b/solution.py
@@ -11,7 +11,8 @@
 HD = 64
 SPAN = 8
 LANES = 128
-VMEM_LIMIT = 56 << 20
+VMEM_LIMIT = 24 << 20
+WIDE_LIMIT = 55 << 20
 LOG2E = math.log2(math.e)
 
 
@@ -347,9 +348,9 @@
     return contract_cols(left, right)
 
 
-def params(*semantics):
+def params(*semantics, limit=VMEM_LIMIT):
     return pltpu.CompilerParams(
-        dimension_semantics=semantics or None, vmem_limit_bytes=VMEM_LIMIT
+        dimension_semantics=semantics or None, vmem_limit_bytes=limit
     )
 
 
@@ -388,7 +389,7 @@
         in_specs=[pl.BlockSpec((rows, depth), lambda i: (0, 0)), weight, weight, weight],
         out_specs=pl.BlockSpec((heads // steps, rows * 3 // 2, LANES), lambda i: (i, 0, 0)),
         out_shape=jax.ShapeDtypeStruct((heads, rows * 3 // 2, LANES), jnp.bfloat16),
-        compiler_params=params("arbitrary"),
+        compiler_params=params("arbitrary", limit=WIDE_LIMIT),
         cost_estimate=cost(2 * rows * depth * width * 3, 2 * (3 * depth * width + 4 * rows * depth)),
         name="project",
     )(x, wq, wk, wv)
@@ -416,143 +417,15 @@
 
 
 def over_blocks(first, count, step):
-    def pair(index, carry):
-        step(first + 2 * index, 2)
-        return carry
-
-    lax.fori_loop(0, count // 2, pair, 0)
-
-    @pl.when(count % 2 == 1)
-    def _():
-        step(first + count - 1, 1)
+    for size in (8, 4, 2, 1):
+
+        @pl.when(count & size != 0)
+        def _(size=size):
+            step(first + (count & ~(2 * size - 1)), size)
 
 
 def attend_body(
-    info_ref, own_ref, sib_ref, ctx_ref, ctxt_ref, lse_ref, kt_ref, kv_s, vt_s, score_s, total_s
-):
-    chips = own_ref.shape[0]
-    blocks = 2 * chips
-    rows = kv_s.shape[1]
-    parity = info_ref[2 * blocks]
-    scale = 0.125 * LOG2E
-    ones_rows = lax.broadcasted_iota(jnp.int32, (LANES, rows), 0) < HD
-
-    def gather(chip, carry):
-        key_top, query_top = carry
-        for ref, which in ((own_ref, parity), (sib_ref, 1 - parity)):
-            block = ref[chip, 0:rows]
-            kv_s[2 * chip + which] = block
-            turned = block.astype(jnp.float32).T
-            vt_s[2 * chip + which] = jnp.where(ones_rows, 1.0, turned).astype(jnp.bfloat16)
-            kt_ref[2 * chip + which] = turned[:HD].astype(jnp.bfloat16)
-            key_top = jnp.maximum(key_top, square_sums(block))
-        query_top = jnp.maximum(query_top, square_sums(own_ref[chip, rows : rows + rows // 2]))
-        return key_top, query_top
-
-    zero = jnp.zeros((8, LANES), jnp.float32)
-    key_top, query_top = lax.fori_loop(0, chips, gather, (zero, zero))
-    key_top = jnp.max(jnp.where(low_lanes(8), key_top, 0.0))
-    bound = jnp.max(query_top) * key_top * (1.02 * scale * scale)
-
-    def finish(item, total, shift):
-        weight = total[0:1]
-        context = total[HD:] / weight
-        ctxt_ref[item] = context
-        lse_ref[item] = jnp.broadcast_to(shift + jnp.log2(weight), (8, rows))
-        ctx_ref[item] = pack_transposed(context).astype(jnp.bfloat16)
-
-    def items(one_item):
-        def body(item, carry):
-            block = 2 * item + parity
-            query = load_query(own_ref[item, rows : rows + rows // 2])
-            one_item(item, info_ref[block], info_ref[blocks + block], query)
-            return carry
-
-        lax.fori_loop(0, chips, body, 0)
-
-    @pl.when(bound < 3600.0)
-    def _():
-        def one_item(item, first, count, query):
-            total_s[...] = jnp.zeros_like(total_s)
-
-            def step(block, n):
-                keys = kv_s[pl.ds(block, n)].reshape(n * rows, LANES)
-                prob = jnp.exp2(dot_nt(keys, query) * scale).astype(jnp.bfloat16)
-                total = total_s[...]
-                for index in range(n):
-                    part = prob[index * rows : (index + 1) * rows]
-                    total = total + dot_nn(vt_s[block + index], part)
-                total_s[...] = total
-
-            over_blocks(first, count, step)
-            finish(item, total_s[...], 0.0)
-
-        items(one_item)
-
-    @pl.when(jnp.logical_not(bound < 3600.0))
-    def _():
-        def one_item(item, first, count, query):
-            def scores(step, top):
-                score = dot_nt(kv_s[first + step], query) * scale
-                score_s[step] = score
-                return jnp.maximum(top, jnp.max(score.reshape(rows // 8, 8, rows), axis=0))
-
-            top = lax.fori_loop(0, count, scores, jnp.full((8, rows), -jnp.inf, jnp.float32))
-            top = jnp.max(top, axis=0, keepdims=True)
-
-            def weigh(step, total):
-                prob = jnp.exp2(score_s[step] - top).astype(jnp.bfloat16)
-                return total + dot_nn(vt_s[first + step], prob)
-
-            total = lax.fori_loop(0, count, weigh, jnp.zeros((LANES, rows), jnp.float32))
-            finish(item, total, top)
-
-        items(one_item)
-
-
-def whole():
-    return pl.BlockSpec(memory_space=pltpu.VMEM)
-
-
-def attend(info, own, sib):
-    chips, packed, _ = own.shape
-    rows = packed * 2 // 3
-    blocks = 2 * chips
-    return pl.pallas_call(
-        attend_body,
-        in_specs=[pl.BlockSpec(memory_space=pltpu.SMEM), whole(), whole()],
-        out_specs=[whole()] * 4,
-        out_shape=[
-            jax.ShapeDtypeStruct((chips, rows // 2, LANES), jnp.bfloat16),
-            jax.ShapeDtypeStruct((chips, HD, rows), jnp.float32),
-            jax.ShapeDtypeStruct((chips, 8, rows), jnp.float32),
-            jax.ShapeDtypeStruct((blocks, HD, rows), jnp.bfloat16),
-        ],
-        scratch_shapes=[
-            pltpu.VMEM((blocks, rows, LANES), jnp.bfloat16),
-            pltpu.VMEM((blocks, LANES, rows), jnp.bfloat16),
-            pltpu.VMEM((SPAN, rows, rows), jnp.float32),
-            pltpu.VMEM((LANES, rows), jnp.float32),
-        ],
-        compiler_params=params(),
-        cost_estimate=cost(2 * 2 * 40 * rows * rows * LANES, 4 << 20, 40 * rows * rows),
-        name="attend",
-    )(info, own, sib)
-
-
-def attend_back_body(
-    info_ref,
-    own_ref,
-    sib_ref,
-    dctx_ref,
-    ctxt_ref,
-    lse_ref,
-    kt_ref,
-    dkv_ref,
-    dq_ref,
-    kv_s,
-    acc_s,
-    total_s,
+    info_ref, own_ref, sib_ref, ctx_ref, ctxt_ref, lse_ref, kv_s, v1_s, q_s, total_s, score_s, top_s
 ):
     chips = own_ref.shape[0]
     blocks = 2 * chips
@@ -560,108 +433,269 @@
     half = rows // 2
     parity = info_ref[2 * blocks]
     scale = 0.125 * LOG2E
-
-    def gather(chip, carry):
+    low = low_lanes(rows)
+    key_top = query_top = jnp.zeros((8, LANES), jnp.float32)
+    for chip in range(chips):
         for ref, which in ((own_ref, parity), (sib_ref, 1 - parity)):
-            kv_s[2 * chip + which] = ref[chip, 0:rows]
-            acc_s[2 * chip + which] = jnp.zeros((rows, LANES), jnp.float32)
-        return carry
-
-    lax.fori_loop(0, chips, gather, 0)
+            block = ref[chip, 0:rows]
+            kv_s[2 * chip + which] = block
+            v1_s[2 * chip + which] = jnp.where(low, 1.0, block.astype(jnp.float32)).astype(
+                jnp.bfloat16
+            )
+            key_top = jnp.maximum(key_top, square_sums(block))
+        packed = own_ref[chip, rows : rows + half]
+        q_s[chip] = load_query(packed)
+        query_top = jnp.maximum(query_top, square_sums(packed))
+    key_top = jnp.max(jnp.where(low_lanes(8), key_top, 0.0))
+    bound = jnp.max(query_top) * key_top * (1.02 * scale * scale)
+    safe = bound < 3600.0
+
+    @pl.when(safe)
+    def _():
+        def one_item(item, carry):
+            query = q_s[item]
+            total_s[item] = jnp.zeros((rows, LANES), jnp.float32)
+
+            def step(block, n):
+                keys = kv_s[pl.ds(block, n)].reshape(n * rows, LANES)
+                values = v1_s[pl.ds(block, n)].reshape(n * rows, LANES)
+                prob = jnp.exp2(dot_nt(query, keys) * scale).astype(jnp.bfloat16)
+                total_s[item] += dot_nn(prob, values)
+
+            place = 2 * item + parity
+            over_blocks(info_ref[place], info_ref[blocks + place], step)
+            top_s[item] = jnp.zeros((8, rows), jnp.float32)
+            return carry
+
+        lax.fori_loop(0, chips, one_item, 0)
+
+    @pl.when(jnp.logical_not(safe))
+    def _():
+        def one_item(item, carry):
+            query = q_s[item]
+            place = 2 * item + parity
+            first, count = info_ref[place], info_ref[blocks + place]
+
+            def scores(step, top):
+                score = dot_nt(query, kv_s[first + step]) * scale
+                score_s[step] = score
+                return jnp.maximum(top, score)
+
+            top = lax.fori_loop(0, count, scores, jnp.full((rows, rows), -jnp.inf, jnp.float32))
+            top = jnp.max(top, axis=1, keepdims=True)
+            total_s[item] = jnp.zeros((rows, LANES), jnp.float32)
+
+            def weigh(step, carry):
+                prob = jnp.exp2(score_s[step] - top).astype(jnp.bfloat16)
+                total_s[item] += dot_nn(prob, v1_s[first + step])
+                return carry
+
+            lax.fori_loop(0, count, weigh, 0)
+            top_s[item] = jnp.broadcast_to(top, (rows, LANES)).T[0:8]
+            return carry
+
+        lax.fori_loop(0, chips, one_item, 0)
+
+    narrow = low_lanes(half)
+    for item in range(chips):
+        total = total_s[item]
+        turned = total.T
+        weight = turned[0:8]
+        lse_ref[item] = top_s[item] + jnp.log2(weight)
+        ctxt_ref[item] = turned[HD:] / weight[0:1]
+        inverse = 1.0 / jnp.where(low, total, 1.0)
+        context = total * pltpu.roll(inverse, HD, 1)
+        ctx_ref[item] = jnp.where(
+            narrow, pltpu.roll(context[:half], HD, 1), context[half:]
+        ).astype(jnp.bfloat16)
+
+
+def whole():
+    return pl.BlockSpec(memory_space=pltpu.VMEM)
+
+
+def attend(info, own, sib):
+    chips, packed, _ = own.shape
+    rows = packed * 2 // 3
+    blocks = 2 * chips
+    return pl.pallas_call(
+        attend_body,
+        in_specs=[pl.BlockSpec(memory_space=pltpu.SMEM), whole(), whole()],
+        out_specs=[whole()] * 3,
+        out_shape=[
+            jax.ShapeDtypeStruct((chips, rows // 2, LANES), jnp.bfloat16),
+            jax.ShapeDtypeStruct((chips, HD, rows), jnp.float32),
+            jax.ShapeDtypeStruct((chips, 8, rows), jnp.float32),
+        ],
+        scratch_shapes=[
+            pltpu.VMEM((blocks, rows, LANES), jnp.bfloat16),
+            pltpu.VMEM((blocks, rows, LANES), jnp.bfloat16),
+            pltpu.VMEM((chips, rows, LANES), jnp.bfloat16),
+            pltpu.VMEM((chips, rows, LANES), jnp.float32),
+            pltpu.VMEM((SPAN, rows, rows), jnp.float32),
+            pltpu.VMEM((chips, 8, rows), jnp.float32),
+        ],
+        compiler_params=params(limit=2 * VMEM_LIMIT),
+        cost_estimate=cost(2 * 2 * 40 * rows * rows * LANES, 4 << 20, 40 * rows * rows),
+        name="attend",
+    )(info, own, sib)
+
+
+def prepare_body(info_ref, own_ref, sib_ref, kv_ref, kt_ref, q_ref):
+    chips = own_ref.shape[0]
+    rows = kv_ref.shape[1]
+    parity = info_ref[4 * chips]
+    for chip in range(chips):
+        for ref, which in ((own_ref, parity), (sib_ref, 1 - parity)):
+            block = ref[chip, 0:rows]
+            kv_ref[2 * chip + which] = block
+            kt_ref[2 * chip + which] = block.astype(jnp.float32).T[:HD].astype(jnp.bfloat16)
+        q_ref[chip] = load_query(own_ref[chip, rows : rows + rows // 2])
+
+
+def prepare(info, own, sib):
+    chips, packed, _ = own.shape
+    rows = packed * 2 // 3
+    return pl.pallas_call(
+        prepare_body,
+        in_specs=[pl.BlockSpec(memory_space=pltpu.SMEM), whole(), whole()],
+        out_specs=[whole()] * 3,
+        out_shape=[
+            jax.ShapeDtypeStruct((2 * chips, rows, LANES), jnp.bfloat16),
+            jax.ShapeDtypeStruct((2 * chips, HD, rows), jnp.bfloat16),
+            jax.ShapeDtypeStruct((chips, rows, LANES), jnp.bfloat16),
+        ],
+        compiler_params=params(),
+        cost_estimate=cost(1 << 20, 4 << 20),
+        name="prepare",
+    )(info, own, sib)
+
+
+def attend_back_body(
+    info_ref,
+    kv_ref,
+    kt_ref,
+    q_ref,
+    dctx_ref,
+    ctxt_ref,
+    lse_ref,
+    mine_ref,
+    other_ref,
+    dq_ref,
+    acc_s,
+    both_s,
+    delta_s,
+    total_s,
+):
+    chips = q_ref.shape[0]
+    blocks = 2 * chips
+    rows = kv_ref.shape[1]
+    half = rows // 2
+    parity = info_ref[2 * blocks]
+    scale = 0.125 * LOG2E
     low = low_lanes(half)
-
-    def one_block(item, carry):
-        block = 2 * item + parity
-        query = load_query(own_ref[item, rows : rows + half])
+    for item in range(chips):
         packed = dctx_ref[item].astype(jnp.float32)
-        top = jnp.where(low, 0.0, pltpu.roll(packed, HD, 1))
-        bottom = jnp.where(low, 0.0, packed)
-        dctx = jnp.concatenate([top, bottom], axis=0).astype(jnp.bfloat16)
+        both_s[item, :rows] = q_ref[item]
+        both_s[item, rows : rows + half] = jnp.where(
+            low, 0.0, pltpu.roll(packed, HD, 1)
+        ).astype(jnp.bfloat16)
+        both_s[item, rows + half :] = jnp.where(low, 0.0, packed).astype(jnp.bfloat16)
         turned = packed.T
-        dctx_t = jnp.concatenate([turned[:HD], turned[HD:]], axis=1)
-        delta = jnp.sum(dctx_t * ctxt_ref[item], axis=0, keepdims=True)
+        turned = jnp.concatenate([turned[:HD], turned[HD:]], axis=1)
+        delta = jnp.sum(turned * ctxt_ref[item], axis=0, keepdims=True)
+        delta_s[item] = jnp.broadcast_to(delta, (8, rows))
+        acc_s[2 * item] = jnp.zeros((rows, LANES), jnp.float32)
+        acc_s[2 * item + 1] = jnp.zeros((rows, LANES), jnp.float32)
+        total_s[item] = jnp.zeros((HD, rows), jnp.float32)
+
+    def one_item(item, carry):
+        query = both_s[item, :rows]
+        dctx = both_s[item, rows:]
+        delta = delta_s[item, 0:1]
         lse = lse_ref[item, 0:1]
-        both = jnp.concatenate([query, dctx], axis=0)
-        total_s[...] = jnp.zeros_like(total_s)
-
-        def step(index, n):
-            kv = kv_s[pl.ds(index, n)].reshape(n * rows, LANES)
+
+        def step(block, n):
+            kv = kv_ref[pl.ds(block, n)].reshape(n * rows, LANES)
             prob = jnp.exp2(dot_nt(kv, query) * scale - lse)
             dscore = (prob * (dot_nt(kv, dctx) - delta)).astype(jnp.bfloat16)
             pair = jnp.concatenate([dscore, prob.astype(jnp.bfloat16)], axis=1)
-            acc_s[pl.ds(index, n)] += dot_nn(pair, both).reshape(n, rows, LANES)
-            total = total_s[...]
+            acc_s[pl.ds(block, n)] += dot_nn(pair, both_s[item]).reshape(n, rows, LANES)
+            total = total_s[item]
             for part in range(n):
-                total = total + dot_nn(kt_ref[index + part], dscore[part * rows : (part + 1) * rows])
-            total_s[...] = total
-
-        over_blocks(info_ref[block], info_ref[blocks + block], step)
-        dq_ref[item] = pack_transposed(total_s[...] * 0.125).astype(jnp.bfloat16)
+                total = total + dot_nn(kt_ref[block + part], dscore[part * rows : (part + 1) * rows])
+            total_s[item] = total
+
+        place = 2 * item + parity
+        over_blocks(info_ref[place], info_ref[blocks + place], step)
         return carry
 
-    lax.fori_loop(0, chips, one_block, 0)
+    lax.fori_loop(0, chips, one_item, 0)
     key_scale = jnp.where(low_lanes(rows), 0.125, 1.0)
-
-    def finish(index, carry):
-        dkv_ref[index] = (acc_s[index] * key_scale).astype(jnp.bfloat16)
-        return carry
-
-    lax.fori_loop(0, blocks, finish, 0)
-
-
-def attend_back(info, own, sib, dctx, ctxt, lse, kt):
-    chips, packed, _ = own.shape
-    rows = packed * 2 // 3
+    for item in range(chips):
+        dq_ref[item] = pack_transposed(total_s[item] * 0.125).astype(jnp.bfloat16)
+        mine_ref[item] = (acc_s[2 * item + parity] * key_scale).astype(jnp.bfloat16)
+        other_ref[item] = (acc_s[2 * item + 1 - parity] * key_scale).astype(jnp.bfloat16)
+
+
+def attend_back(info, kv, kt, query, dctx, ctxt, lse):
+    chips, rows, _ = query.shape
     blocks = 2 * chips
+    share = jax.ShapeDtypeStruct((chips, rows, LANES), jnp.bfloat16)
     return pl.pallas_call(
         attend_back_body,
         in_specs=[pl.BlockSpec(memory_space=pltpu.SMEM)] + [whole()] * 6,
-        out_specs=[whole(), whole()],
-        out_shape=[
-            jax.ShapeDtypeStruct((blocks, rows, LANES), jnp.bfloat16),
-            jax.ShapeDtypeStruct((chips, rows // 2, LANES), jnp.bfloat16),
+        out_specs=[whole()] * 3,
+        out_shape=[share, share, jax.ShapeDtypeStruct((chips, rows // 2, LANES), jnp.bfloat16)],
+        scratch_shapes=[
+            pltpu.VMEM((blocks, rows, LANES), jnp.float32),
+            pltpu.VMEM((chips, 2 * rows, LANES), jnp.bfloat16),
+            pltpu.VMEM((chips, 8, rows), jnp.float32),
+            pltpu.VMEM((chips, HD, rows), jnp.float32),
         ],
-        scratch_shapes=[
-            pltpu.VMEM((blocks, rows, LANES), jnp.bfloat16),
-            pltpu.VMEM((blocks, rows, LANES), jnp.float32),
-            pltpu.VMEM((HD, rows), jnp.float32),
-        ],
-        compiler_params=params(),
+        compiler_params=params(limit=WIDE_LIMIT),
         cost_estimate=cost(2 * 5 * 40 * rows * rows * LANES, 5 << 20, 40 * rows * rows),
         name="attend_back",
-    )(info, own, sib, dctx, ctxt, lse, kt)
-
-
-def combine_body(info_ref, dkv_ref, sib_ref, dq_ref, out_ref):
-    chips, half, _ = dq_ref.shape
-    rows = 2 * half
-    parity = info_ref[4 * chips]
-
-    def one(chip, carry):
-        block = 2 * chip + parity
-        total = dkv_ref[block].astype(jnp.float32) + sib_ref[block].astype(jnp.float32)
+    )(info, kv, kt, query, dctx, ctxt, lse)
+
+
+def combine_body(mine_ref, sib_ref, dq_ref, out_ref):
+    chips, rows, _ = mine_ref.shape
+    for chip in range(chips):
+        total = mine_ref[chip].astype(jnp.float32) + sib_ref[chip].astype(jnp.float32)
         out_ref[chip, 0:rows] = total.astype(jnp.bfloat16)
-        out_ref[chip, rows : rows + half] = dq_ref[chip]
-        return carry
-
-    lax.fori_loop(0, chips, one, 0)
-
-
-def combine(info, dkv, dkv_sib, dq):
-    chips, half, _ = dq.shape
+        out_ref[chip, rows:] = dq_ref[chip]
+
+
+def combine(mine, sib, dq):
+    chips, rows, _ = mine.shape
     return pl.pallas_call(
         combine_body,
-        in_specs=[pl.BlockSpec(memory_space=pltpu.SMEM)] + [whole()] * 3,
+        in_specs=[whole()] * 3,
         out_specs=whole(),
-        out_shape=jax.ShapeDtypeStruct((chips, 3 * half, LANES), jnp.bfloat16),
+        out_shape=jax.ShapeDtypeStruct((chips, rows * 3 // 2, LANES), jnp.bfloat16),
         compiler_params=params(),
-        cost_estimate=cost(1 << 20, 3 << 20),
+        cost_estimate=cost(1 << 20, 2 << 20),
         name="combine",
-    )(info, dkv, dkv_sib, dq)
-
-
-def out_project_body(in_ref, w_ref, ctx_ref, own_ref, send_ref):
+    )(mine, sib, dq)
+
+
+def out_norm_body(
+    info_ref,
+    in_ref,
+    other_ref,
+    w_ref,
+    w_mine_ref,
+    w_sib_ref,
+    tok_ref,
+    gain_ref,
+    shift_ref,
+    ctx_ref,
+    *outs,
+):
+    *outs, far_s = outs
     heads, half, _ = in_ref.shape
+    parity = info_ref[2 * 2 * in_ref.shape[0]]
     for pair in range(heads // 2):
         cols = slice(pair * LANES, (pair + 1) * LANES)
         top, bottom = split_lanes(
@@ -669,27 +703,40 @@
         )
         ctx_ref[0:half, cols] = top.astype(jnp.bfloat16)
         ctx_ref[half:, cols] = bottom.astype(jnp.bfloat16)
-    rows = dot_nn(ctx_ref[...], w_ref[...])
-    own_ref[...] = rows[:half]
-    send_ref[...] = rows[half:].astype(jnp.bfloat16)
-
-
-def out_project(packed, w_out):
+        top, bottom = split_lanes(
+            other_ref[2 * pair].astype(jnp.float32), other_ref[2 * pair + 1].astype(jnp.float32)
+        )
+        far_s[0:half, cols] = bottom.astype(jnp.bfloat16)
+        far_s[half:, cols] = top.astype(jnp.bfloat16)
+    first = parity == 0
+    mine, sib = w_mine_ref[...], w_sib_ref[...]
+    w_far = jnp.concatenate([jnp.where(first, mine, sib), jnp.where(first, sib, mine)], axis=0)
+    rows = dot_nn(ctx_ref[...], w_ref[...]) + dot_nn(far_s[...], w_far)
+    unit, inverse = norm_rows(tok_ref[...].astype(jnp.float32) + rows)
+    hidden = unit * gain_ref[...] + shift_ref[...]
+    inverse = jnp.broadcast_to(inverse, (2 * half, LANES))
+    for index, value in enumerate((hidden, hidden.astype(jnp.bfloat16), unit, inverse)):
+        outs[2 * index][...] = value[:half]
+        outs[2 * index + 1][...] = value[half:]
+
+
+def out_norm(info, packed, packed_other, w_out, w_mine, w_sib, tokens, gain, shift):
     heads, half, _ = packed.shape
     width, depth = w_out.shape
-    return pl.pallas_call(
-        out_project_body,
-        in_specs=[whole()] * 2,
-        out_specs=[whole()] * 3,
-        out_shape=[
-            jax.ShapeDtypeStruct((2 * half, width), jnp.bfloat16),
-            jax.ShapeDtypeStruct((half, depth), jnp.float32),
-            jax.ShapeDtypeStruct((half, depth), jnp.bfloat16),
-        ],
+    wide = jax.ShapeDtypeStruct((half, depth), jnp.float32)
+    low = jax.ShapeDtypeStruct((half, depth), jnp.bfloat16)
+    narrow = jax.ShapeDtypeStruct((half, LANES), jnp.float32)
+    return pl.pallas_call(
+        out_norm_body,
+        in_specs=[pl.BlockSpec(memory_space=pltpu.SMEM)] + [whole()] * 8,
+        out_specs=[whole()] * 9,
+        out_shape=[jax.ShapeDtypeStruct((2 * half, width), jnp.bfloat16)]
+        + [wide, wide, low, low, wide, wide, narrow, narrow],
+        scratch_shapes=[pltpu.VMEM((2 * half, width), jnp.bfloat16)],
         compiler_params=params(),
-        cost_estimate=cost(4 * half * width * depth, 3 << 20),
-        name="out_project",
-    )(packed, w_out)
+        cost_estimate=cost(8 * half * width * depth, 5 << 20),
+        name="out_norm",
+    )(info, packed, packed_other, w_out, w_mine, w_sib, tokens, gain[None], shift[None])
 
 
 def ctx_grad_body(own_ref, other_ref, w_ref, out_ref):
@@ -716,30 +763,24 @@
     )(grad_own, grad_other, w_out)
 
 
-def head_grad_body(
-    info_ref, tok_ref, dkv_ref, dkv_sib_ref, dq_ref, dq_sib_ref, out_ref, acc_s, grad_s
-):
+def head_grad_body(info_ref, tok_ref, own_ref, sib_ref, out_ref, acc_s, grad_s):
     step = pl.program_id(0)
     steps = pl.num_programs(0)
-    chips, half, _ = dq_ref.shape
+    chips, packed, _ = own_ref.shape
     blocks = 2 * chips
-    rows = 2 * half
+    rows = packed * 2 // 3
     parity = info_ref[2 * blocks]
     group = chips // steps
     columns = []
     for index in range(group):
         place = step * group + index
         chip = jnp.where(place < chips // 2, 2 * place, 2 * chips - 1 - 2 * place)
+        own, sib = own_ref[chip].astype(jnp.float32), sib_ref[chip].astype(jnp.float32)
         for core in range(2):
-            block = 2 * chip + core
-            total = dkv_ref[block].astype(jnp.float32) + dkv_sib_ref[block].astype(jnp.float32)
-            dq = jnp.where(
-                parity == core,
-                dq_ref[chip].astype(jnp.float32),
-                dq_sib_ref[chip].astype(jnp.float32),
-            ).T
+            block = jnp.where(parity == core, own, sib)
+            dq = block[rows:].T
             dq = jnp.concatenate([dq[:HD], dq[HD:]], axis=1)
-            columns.append(jnp.concatenate([total.T, dq], axis=0).astype(jnp.bfloat16))
+            columns.append(jnp.concatenate([block[:rows].T, dq], axis=0).astype(jnp.bfloat16))
     part = dot_nn(jnp.concatenate(columns, axis=1), tok_ref[...])
 
     @pl.when(step == 0)
@@ -768,9 +809,10 @@
         lax.fori_loop(0, chips, pack, 0)
 
 
-def head_grad(info, tokens_all, dkv, dkv_sib, dq, dq_sib):
-    blocks, rows, _ = dkv.shape
-    chips = blocks // 2
+def head_grad(info, tokens_all, own, sib):
+    chips, packed, _ = own.shape
+    blocks = 2 * chips
+    rows = packed * 2 // 3
     depth = tokens_all.shape[1]
     piece = depth // blocks
     steps = 4
@@ -781,10 +823,8 @@
         in_specs=[
             pl.BlockSpec(memory_space=pltpu.SMEM),
             pl.BlockSpec((blocks * rows // steps, depth), lambda i: (i, 0)),
-            full(dkv.shape),
-            full(dkv.shape),
-            full(dq.shape),
-            full(dq.shape),
+            full(own.shape),
+            full(sib.shape),
         ],
         out_specs=full((chips, piece + piece // 2, LANES)),
         out_shape=jax.ShapeDtypeStruct((chips, piece + piece // 2, LANES), jnp.bfloat16),
@@ -792,10 +832,10 @@
             pltpu.VMEM((3 * HD, depth), jnp.float32),
             pltpu.VMEM((blocks, piece, 2 * LANES), jnp.float32),
         ],
-        compiler_params=params("arbitrary"),
+        compiler_params=params("arbitrary", limit=2 * VMEM_LIMIT),
         cost_estimate=cost(2 * blocks * rows * depth * 3 * HD, blocks * rows * depth * 2),
         name="head_grad",
-    )(info, tokens_all, dkv, dkv_sib, dq, dq_sib)
+    )(info, tokens_all, own, sib)
 
 
 def token_grad_body(in_ref, wq_ref, wk_ref, wv_ref, own_ref, send_ref, d_s):
@@ -865,97 +905,272 @@
     )(packed)
 
 
-def late_grad_body(orders, tiles, parts, *refs):
-    *arrays, out_ref, turned_s = refs
-    step = pl.program_id(0)
-    width = out_ref.shape[1]
-    terms = []
-    for count in parts:
-        terms.append((arrays[:count], arrays[count : 2 * count]))
-        arrays = arrays[2 * count :]
-
-    @pl.when(step == 0)
-    def _():
-        for index, (lefts, _) in enumerate(terms):
-            size = lefts[0].shape[1] // len(orders[index])
-            for which, left in enumerate(lefts):
-                half = left.shape[0]
-                for place, chip in enumerate(orders[index]):
-                    piece = left[:, chip * size : (chip + 1) * size].T
-                    rows = slice(place * size, (place + 1) * size)
-                    turned_s[index, rows, which * half : (which + 1) * half] = piece
+def out_sum_body(keep_ref, came_ref, out_ref):
+    piece = out_ref.shape[1]
+    for tile in range(out_ref.shape[0] // LANES):
+        rows = slice(tile * piece, (tile + 1) * piece)
+        total = keep_ref[0, rows].astype(jnp.float32) + came_ref[0, rows].astype(jnp.float32)
+        out_ref[tile * LANES : (tile + 1) * LANES] = total.T
+
+
+def out_sum(keep, came, width):
+    piece = keep.shape[1] * LANES // width
+    return pl.pallas_call(
+        out_sum_body,
+        in_specs=[whole()] * 2,
+        out_specs=whole(),
+        out_shape=jax.ShapeDtypeStruct((width, piece), jnp.float32),
+        compiler_params=params(),
+        cost_estimate=cost(1 << 17, 1 << 19),
+        name="out_sum",
+    )(keep, came)
+
+
+def late_grad_body(orders, tiles, first_ref, *refs):
+    *arrays, out_ref, turned_s, tile_s, sems = refs
+    tile = tile_s.shape[2]
+    terms = [arrays[index : index + 4] for index in range(0, len(arrays), 4)]
+    first = first_ref[0] == 0
+
+    def ordered(own, other):
+        return (jnp.where(first, own, other), jnp.where(first, other, own))
+
+    def columns(place):
+        return pl.ds(pl.multiple_of(place * tile, tile), tile)
+
+    def copy(place):
+        slot = place % 2
+        return pltpu.make_async_copy(tile_s.at[slot], out_ref.at[:, columns(place)], sems.at[slot])
 
     start = 0
-    for index, (_, rights) in enumerate(terms):
-
-        @pl.when((step >= start) & (step < start + tiles[index]))
-        def _(index=index, start=start, rights=rights):
-            cols = pl.ds(pl.multiple_of((step - start) * width, width), width)
-            right = jnp.concatenate([ref[:, cols] for ref in rights], axis=0)
-            left = turned_s[index, :, : right.shape[0]]
-            out_ref[...] = dot_nn(left, right).astype(jnp.bfloat16)
-
+    for index, (own, other, own_right, other_right) in enumerate(terms):
+        half, depth = own.shape
+        size = depth // len(orders[index])
+        for place, chip in enumerate(orders[index]):
+            cols = slice(chip * size, (chip + 1) * size)
+            rows = slice(place * size, (place + 1) * size)
+            for which, piece in enumerate(ordered(own[:, cols], other[:, cols])):
+                turned_s[rows, which * half : (which + 1) * half] = piece.T
+
+        def step(number, carry, start=start, own_right=own_right, other_right=other_right):
+            place = start + number
+            cols = columns(number)
+            right = jnp.concatenate(ordered(own_right[:, cols], other_right[:, cols]), axis=0)
+
+            @pl.when(place >= 2)
+            def _():
+                copy(place - 2).wait()
+
+            tile_s[place % 2] = dot_nn(turned_s[...], right).astype(jnp.bfloat16)
+            copy(place).start()
+            return carry
+
+        lax.fori_loop(0, tiles[index], step, 0)
         start += tiles[index]
-
-
-def late_grad(chips, terms):
-    half, depth = terms[0][0][0].shape
-    tile = 512
-    orders = [ring_chips(chips) if term[2] else list(range(chips)) for term in terms]
-    arrays = [array for term in terms for group in term[:2] for array in group]
-    tiles = [term[1][0].shape[1] // tile for term in terms]
-    parts = [len(term[0]) for term in terms]
+    for place in range(start - 2, start):
+        copy(place).wait()
+
+
+def late_grad(first, chips, terms):
+    half, depth = terms[0][0].shape
+    tile = 1024
+    orders = [ring_chips(chips) if term[4] else list(range(chips)) for term in terms]
+    arrays = [array for term in terms for array in term[:4]]
+    tiles = [term[2].shape[1] // tile for term in terms]
     width = sum(tiles) * tile
-    fixed = lambda array: pl.BlockSpec(array.shape, lambda i: (0, 0))
-    return pl.pallas_call(
-        functools.partial(late_grad_body, orders, tiles, parts),
-        grid=(sum(tiles),),
-        in_specs=[fixed(array) for array in arrays],
-        out_specs=pl.BlockSpec((depth, tile), lambda i: (0, i)),
+    return pl.pallas_call(
+        functools.partial(late_grad_body, orders, tiles),
+        in_specs=[pl.BlockSpec(memory_space=pltpu.SMEM)] + [whole()] * len(arrays),
+        out_specs=pl.BlockSpec(memory_space=pl.ANY),
         out_shape=jax.ShapeDtypeStruct((depth, width), jnp.bfloat16),
-        scratch_shapes=[pltpu.VMEM((len(terms), depth, 2 * half), jnp.bfloat16)],
-        compiler_params=params("arbitrary"),
+        scratch_shapes=[
+            pltpu.VMEM((depth, 2 * half), jnp.bfloat16),
+            pltpu.VMEM((2, depth, tile), jnp.bfloat16),
+            pltpu.SemaphoreType.DMA((2,)),
+        ],
+        compiler_params=params(limit=WIDE_LIMIT),
         cost_estimate=cost(4 * half * depth * width, 2 * depth * width + (3 << 20)),
         name="late_grad",
-    )(*arrays)
-
-
-def out_grad_body(left_ref, other_ref, ctx_ref, small_ref, out_ref):
-    cores, chips, height, _ = out_ref.shape
-    piece = height - small_ref.shape[0]
+    )(first, *arrays)
+
+
+def halve_body(place, info_ref, mine_ref, came_ref, keep_ref, send_ref):
+    bit = info_ref[place]
+    for index in range(keep_ref.shape[0]):
+        for ref, block in ((keep_ref, 2 * index + bit), (send_ref, 2 * index + 1 - bit)):
+            total = mine_ref[block].astype(jnp.float32) + came_ref[block].astype(jnp.float32)
+            ref[index] = total.astype(jnp.bfloat16)
+
+
+def halve(info, place, mine, came):
+    count, height, width = mine.shape
+    share = jax.ShapeDtypeStruct((count // 2, height, width), jnp.bfloat16)
+    return pl.pallas_call(
+        functools.partial(halve_body, place),
+        in_specs=[pl.BlockSpec(memory_space=pltpu.SMEM)] + [whole()] * 2,
+        out_specs=[whole()] * 2,
+        out_shape=[share] * 2,
+        compiler_params=params(),
+        cost_estimate=cost(1 << 18, 2 << 20),
+        name="halve",
+    )(info, mine, came)
+
+
+def widen_body(in_ref, out_ref):
+    out_ref[...] = in_ref[...].astype(jnp.float32)
+
+
+def widen(values):
+    rows, width = values.shape
+    steps = 4
+    block = pl.BlockSpec((rows // steps, width), lambda i: (i, 0))
+    return pl.pallas_call(
+        widen_body,
+        grid=(steps,),
+        in_specs=[block],
+        out_specs=block,
+        out_shape=jax.ShapeDtypeStruct((rows, width), jnp.float32),
+        compiler_params=params("arbitrary", limit=WIDE_LIMIT),
+        cost_estimate=cost(1 << 20, 6 << 20),
+        name="widen",
+    )(values)
+
+
+def out_grad_body(info_ref, left_ref, other_ref, ctx_ref, mine_ref, send_ref, grad_s):
+    blocks, piece, width = grad_s.shape
+    chips = blocks // 2
+    parity = info_ref[2 * blocks]
     left = jnp.concatenate([left_ref[...], other_ref[...]], axis=0)
-    grad = contract_rows(left, ctx_ref[...]).astype(jnp.bfloat16)
-    for index in range(cores * chips):
-        place = (index % cores, index // cores)
-        out_ref[place[0], place[1], :piece] = grad[index * piece : (index + 1) * piece]
-        out_ref[place[0], place[1], piece:] = small_ref[...]
-
-
-def out_grad_pack(count, grad_own, grad_other, context_low, small):
+    grad_s[...] = contract_rows(left, ctx_ref[...]).reshape(blocks, piece, width)
+    for chip in range(chips):
+        for ref, block in ((mine_ref, 2 * chip + parity), (send_ref, 2 * chip + 1 - parity)):
+            part = grad_s[block].astype(jnp.bfloat16)
+            for tile in range(width // LANES):
+                cols = slice(tile * LANES, (tile + 1) * LANES)
+                ref[chip, tile * piece : (tile + 1) * piece] = part[:, cols]
+
+
+def out_grad_pack(info, chips, grad_own, grad_other, context_low):
     depth = grad_own.shape[1]
     rows, width = context_low.shape
-    height = depth // count + small.shape[0]
+    piece = depth // (2 * chips)
+    height = piece * width // LANES
+    share = jax.ShapeDtypeStruct((chips, height, LANES), jnp.bfloat16)
     return pl.pallas_call(
         out_grad_body,
-        in_specs=[whole()] * 4,
-        out_specs=whole(),
-        out_shape=jax.ShapeDtypeStruct((2, count // 2, height, width), jnp.bfloat16),
+        in_specs=[pl.BlockSpec(memory_space=pltpu.SMEM)] + [whole()] * 3,
+        out_specs=[whole()] * 2,
+        out_shape=[share] * 2,
+        scratch_shapes=[pltpu.VMEM((2 * chips, piece, width), jnp.float32)],
         compiler_params=params(),
         cost_estimate=cost(2 * rows * depth * width, 2 << 20),
         name="out_grad",
-    )(grad_own, grad_other, context_low, small)
-
-
-def normalized(values):
+    )(info, grad_own, grad_other, context_low)
+
+
+def norm_rows(values):
     centred = values - jnp.mean(values, axis=-1, keepdims=True)
     inverse = lax.rsqrt(jnp.mean(centred * centred, axis=-1, keepdims=True) + 1e-05)
     return centred * inverse, inverse
 
 
-def norm_back(grad, gain, unit, inverse):
+def back_rows(grad, gain, unit, inverse):
     scaled = grad * gain
     along = jnp.mean(scaled * unit, axis=-1, keepdims=True)
     return (scaled - jnp.mean(scaled, axis=-1, keepdims=True) - unit * along) * inverse
+
+
+def store_sums(ref, grad, unit):
+    width = ref.shape[1]
+    for index, total in enumerate((jnp.sum(grad * unit, axis=0), jnp.sum(grad, axis=0))):
+        for part in range(2):
+            row = 2 * index + part
+            ref[row : row + 1] = total[None, part * width : (part + 1) * width]
+
+
+def attn_norm_back_body(
+    pre_ref, own_ref, recv_ref, gain_ref, unit_ref, inv_ref, grad_ref, low_ref, sums_ref
+):
+    grad = pre_ref[...] + (own_ref[...].astype(jnp.float32) + recv_ref[...].astype(jnp.float32))
+    unit = unit_ref[...]
+    back = back_rows(grad, gain_ref[...], unit, inv_ref[:, 0:1])
+    grad_ref[...] = back
+    low_ref[...] = back.astype(jnp.bfloat16)
+    store_sums(sums_ref, grad, unit)
+
+
+def attn_norm_back(pre, own, recv, gain, unit, inverse, width):
+    rows, depth = pre.shape
+    return pl.pallas_call(
+        attn_norm_back_body,
+        in_specs=[whole()] * 6,
+        out_specs=[whole()] * 3,
+        out_shape=[
+            jax.ShapeDtypeStruct((rows, depth), jnp.float32),
+            jax.ShapeDtypeStruct((rows, depth), jnp.bfloat16),
+            jax.ShapeDtypeStruct((4, width), jnp.float32),
+        ],
+        compiler_params=params(),
+        cost_estimate=cost(1 << 20, 2 << 20),
+        name="attn_norm_back",
+    )(pre, own, recv, gain[None], unit, inverse)
+
+
+def turn_body(
+    hid_ref,
+    own_ref,
+    recv_ref,
+    gain_ref,
+    shift_ref,
+    w_ref,
+    pick_ref,
+    cot_ref,
+    out_ref,
+    unit_ref,
+    proj_ref,
+    pre_ref,
+    low_ref,
+    sums_ref,
+):
+    values = hid_ref[...] + (own_ref[...].astype(jnp.float32) + recv_ref[...].astype(jnp.float32))
+    unit, inverse = norm_rows(values)
+    gain = gain_ref[...]
+    output = (unit * gain + shift_ref[...]).astype(jnp.bfloat16)
+    out_ref[...] = output
+    proj = dot_nn(output, w_ref[...])
+    scale = lax.rsqrt(jnp.sum(proj * proj, axis=1, keepdims=True) + 1e-06)
+    vec = proj * scale
+    unit_ref[...] = vec.astype(jnp.bfloat16)
+    pick = pick_ref[...]
+    along = jnp.sum(vec * pick, axis=1, keepdims=True)
+    proj_low = ((pick - vec * along) * scale).astype(jnp.bfloat16)
+    proj_ref[...] = proj_low
+    grad = cot_ref[...].astype(jnp.float32) + dot_nt(proj_low, w_ref[...])
+    pre = back_rows(grad, gain, unit, inverse)
+    pre_ref[...] = pre
+    low_ref[...] = pre.astype(jnp.bfloat16)
+    store_sums(sums_ref, grad, unit)
+
+
+def turn(hidden, own, recv, gain, shift, w_colbert, pick, cot, width):
+    rows, depth = hidden.shape
+    low = jax.ShapeDtypeStruct((rows, depth), jnp.bfloat16)
+    return pl.pallas_call(
+        turn_body,
+        in_specs=[whole()] * 8,
+        out_specs=[whole()] * 6,
+        out_shape=[
+            low,
+            low,
+            low,
+            jax.ShapeDtypeStruct((rows, depth), jnp.float32),
+            low,
+            jax.ShapeDtypeStruct((4, width), jnp.float32),
+        ],
+        compiler_params=params(),
+        cost_estimate=cost(4 * rows * depth * depth, 5 << 20),
+        name="turn",
+    )(hidden, own, recv, gain[None], shift[None], w_colbert, pick, cot)
 
 
 def gelu_with_slope(values):
@@ -1012,12 +1227,19 @@
     def together(*values):
         return lax.optimization_barrier(values)
 
-    gathered = jnp.concatenate([tokens, swap(tokens)], axis=0)
+    tokens_other = swap(tokens)
+    gathered = jnp.concatenate([tokens, tokens_other], axis=0)
     block_ids = passage_of.astype(jnp.int32)
     same = block_ids[:, None] == block_ids[None, :]
     starts = jnp.sum((block_ids[None, :] < block_ids[:, None]).astype(jnp.int32), axis=1)
     counts = jnp.sum(same.astype(jnp.int32), axis=1)
-    info = jnp.concatenate([starts, counts, parity[None].astype(jnp.int32)])
+    chip = (pass_index // 2).astype(jnp.int32)
+    bits = chips.bit_length() - 1
+    info = jnp.concatenate(
+        [starts, counts, parity[None].astype(jnp.int32)]
+        + [((chip >> bit) & 1)[None] for bit in range(bits)]
+    )
+    first_bit = 2 * pass_count + 1
 
     seq_count = match_index.shape[1]
     query_rows = cot_scores.shape[0]
@@ -1039,78 +1261,127 @@
     turned_part = jnp.concatenate([unit_grad_part[own_rows:], unit_grad_part[:own_rows]], axis=0)
     unit_grad_send = turned_part.astype(jnp.bfloat16)
 
-    own_pack = to_heads(project(gathered, w_query, w_key, w_value))
-    own_pack, unit_grad_send = together(own_pack, unit_grad_send)
+    own_send = project(gathered, w_query, w_key, w_value)
+    own_pack = to_heads(own_send)
+    piece = w_out.shape[0] // 2
+    w_out_send = lax.dynamic_slice_in_dim(w_out, parity * piece, piece, axis=0)
+    w_out_mine = swap(after(w_out_send, own_send))
+    w_out_sib = sibling(w_out_mine)
+    own_pack, unit_grad_send, w_out_sib = together(own_pack, unit_grad_send, w_out_sib)
     sib_pack = sibling(own_pack)
     unit_grad_recv = swap(unit_grad_send)
-    ctx_pack, ctx_turned, lse, key_turned = attend(info, own_pack, sib_pack)
-    unit_grad = unit_grad_part + unit_grad_recv.astype(jnp.float32)
-    ctx_recv = to_heads(after(ctx_pack, unit_grad_recv))
+    cot_other = swap(after(cot_act, unit_grad_send))
+    ctx_pack, ctx_turned, lse = attend(info, own_pack, sib_pack)
+    unit_grad = unit_grad_part.astype(jnp.bfloat16).astype(jnp.float32) + unit_grad_recv.astype(
+        jnp.float32
+    )
+    unit_grad_own, unit_grad_other = unit_grad[:own_rows], unit_grad[own_rows:]
+    ctx_recv = to_heads(ctx_pack)
+    ready = prepare(info, after(own_pack, ctx_pack), sib_pack)
+    ctx_recv, unit_grad_own, unit_grad_other, cot_other, kv, key_turned, query = together(
+        ctx_recv, unit_grad_own, unit_grad_other, cot_other, *ready
+    )
     tokens_all = lax.all_gather(
         after(gathered, ctx_recv), "pass", axis=0, axis_index_groups=ring, tiled=True
     )
-    context_low, attn_own, attn_send = out_project(ctx_recv, w_out)
-    attn_rows = attn_own + swap(attn_send).astype(jnp.float32)
-    unit_attn, inverse_attn = normalized(tokens.astype(jnp.float32) + attn_rows)
-    hidden = unit_attn * gain_attn + shift_attn
-    hidden_low = hidden.astype(jnp.bfloat16)
-    hidden_other = swap(hidden_low)
-    hidden_all = jnp.concatenate([hidden_low, hidden_other], axis=0)
-
-    inner_pre = dot_nn(hidden_all, w_up)
-    gated, slope = gelu_with_slope(inner_pre)
-    gated_low, slope = lax.optimization_barrier((gated.astype(jnp.bfloat16), slope))
-    ffn_part = dot_nn(gated_low, w_down)
-    ffn_rows = ffn_part[:own_rows] + swap(ffn_part[own_rows:].astype(jnp.bfloat16)).astype(
-        jnp.float32
-    )
-    unit_ffn, inverse_ffn = normalized(hidden + ffn_rows)
-    output = unit_ffn * gain_ffn + shift_ffn
-    output_low = output.astype(jnp.bfloat16)
-
-    def colbert(rows, grad_rows):
-        proj = dot_nn(rows, w_colbert)
-        inverse = lax.rsqrt(jnp.sum(proj * proj, axis=1, keepdims=True) + 1e-06)
-        unit = proj * inverse
-        along = jnp.sum(unit * grad_rows, axis=1, keepdims=True)
-        return unit.astype(jnp.bfloat16), ((grad_rows - unit * along) * inverse).astype(
-            jnp.bfloat16
+    (
+        context_low,
+        hidden,
+        hidden_far,
+        hidden_low,
+        hidden_other,
+        unit_attn,
+        unit_attn_far,
+        inverse_attn,
+        inverse_attn_far,
+    ) = out_norm(
+        info,
+        ctx_recv,
+        swap(ctx_recv),
+        w_out,
+        w_out_mine,
+        w_out_sib,
+        gathered,
+        gain_attn,
+        shift_attn,
+    )
+
+    def activate(rows):
+        gated, slope = gelu_with_slope(dot_nn(rows, w_up))
+        return lax.optimization_barrier((gated.astype(jnp.bfloat16), slope))
+
+    gated_other, slope_other = activate(hidden_other)
+    gated_own, slope_own = activate(hidden_low)
+
+    def both_halves(rows_own, rows_other, product):
+        part_other = product(rows_other).astype(jnp.bfloat16)
+        part_own = product(after(rows_own, part_other)).astype(jnp.bfloat16)
+        recv_own = swap(part_other)
+        recv_other = swap(part_own)
+        return part_own, part_other, recv_own, recv_other
+
+    part_own, part_other, recv_own, recv_other = both_halves(
+        gated_own, gated_other, lambda rows: dot_nn(rows, w_down)
+    )
+    local_width = w_query.shape[1]
+    width = w_up.shape[1]
+    model = tokens.shape[1]
+
+    def turned(rows, part, recv, pick, cot):
+        return turn(
+            rows, part, recv, gain_ffn, shift_ffn, w_colbert, pick, cot, local_width
         )
 
-    unit_own, proj_own = colbert(output_low, unit_grad[:own_rows])
-    out_grad = cot_act.astype(jnp.float32) + dot_nt(proj_own, w_colbert)
-    pre_grad = norm_back(out_grad, gain_ffn, unit_ffn, inverse_ffn)
-    pre_low = pre_grad.astype(jnp.bfloat16)
-    pre_other = swap(pre_low)
-    ffn_all = jnp.concatenate([pre_low, pre_other], axis=0)
-
-    inner_low = (dot_nt(ffn_all, w_down) * slope).astype(jnp.bfloat16)
-    hidden_part = dot_nt(inner_low, w_up)
-    hidden_send = hidden_part[own_rows:].astype(jnp.bfloat16)
-    hidden_recv = swap(hidden_send)
-    inner_late = after(inner_low, hidden_send)
-    width = w_up.shape[1]
+    output_low, unit_own, proj_own, pre_grad, pre_low, sums_ffn = turned(
+        hidden, part_own, recv_own, unit_grad_own, cot_act
+    )
+    inner_own = (dot_nt(pre_low, w_down) * slope_own).astype(jnp.bfloat16)
+    recv_other, inner_own = together(recv_other, inner_own)
+    output_other, unit_other, proj_other, pre_far, pre_other, _ = turned(
+        hidden_far, part_other, recv_other, unit_grad_other, cot_other
+    )
+    inner_other = (dot_nt(pre_other, w_down) * slope_other).astype(jnp.bfloat16)
+    part_own, part_other, recv_own, recv_other = both_halves(
+        inner_own, inner_other, lambda rows: dot_nt(rows, w_up)
+    )
     late = late_grad(
+        qry_index[None].astype(jnp.int32),
         chips,
         (
-            ((hidden_low, hidden_other), (inner_late[:own_rows], inner_late[own_rows:]), True),
-            ((pre_low, pre_other), (gated_low[:own_rows], gated_low[own_rows:]), True),
-            ((output_low,), (proj_own,), False),
+            (hidden_low, hidden_other, after(inner_own, part_own), inner_other, True),
+            (pre_low, pre_other, gated_own, gated_other, True),
+            (output_low, output_other, proj_own, proj_other, False),
         ),
     )
-    hidden_recv, late, tokens_all = together(hidden_recv, late, tokens_all)
+    recv_own, recv_other, late = together(recv_own, recv_other, late)
     late_sums = lax.psum_scatter(
         late, "pass", scatter_dimension=0, axis_index_groups=ring, tiled=True
     )
 
-    hidden_grad = (
-        pre_grad + hidden_part[:own_rows] + hidden_recv.astype(jnp.float32)
-    )
-    attn_pre = norm_back(hidden_grad, gain_attn, unit_attn, inverse_attn)
-    attn_low = attn_pre.astype(jnp.bfloat16)
-    attn_other = swap(attn_low)
-
-    unit_other = swap(after(unit_own, attn_other))
+    def back_to_attn(pre, part, recv, unit, inverse):
+        return attn_norm_back(pre, part, recv, gain_attn, unit, inverse, local_width)
+
+    attn_pre, attn_low, sums_attn = back_to_attn(
+        pre_grad, part_own, recv_own, unit_attn, inverse_attn
+    )
+    _, attn_other, _ = back_to_attn(
+        pre_far, part_other, recv_other, unit_attn_far, inverse_attn_far
+    )
+
+    dctx_send = ctx_grad_packed(attn_low, attn_other, w_out)
+    own_dctx = to_heads(dctx_send)
+    out_mine, out_send = out_grad_pack(
+        info, chips, after(attn_low, dctx_send), attn_other, context_low
+    )
+    own_dctx, out_mine, out_send = together(own_dctx, out_mine, out_send)
+    mine, other, dq = attend_back(info, kv, key_turned, query, own_dctx, ctx_turned, lse)
+    back_send = combine(mine, sibling(other), dq)
+    back = to_heads(back_send)
+    back_own, out_send, unit_other = together(back_send, out_send, unit_other)
+
+    out_keep, out_send = halve(info, first_bit, out_mine, sibling(out_send))
+    out_came = swap_over(out_send, "pass", 2)
+    unit_other = after(unit_other, out_send)
     picked = dot_nn(one_hot, jnp.concatenate([unit_own, unit_other], axis=0))
     per_query = jnp.sum((query_float * picked).reshape(query_rows, -1), axis=1)
     score_block = per_query[:, None] * pick_col.astype(jnp.float32)[None, :]
@@ -1119,63 +1390,33 @@
         score_block,
         (qry_index * query_rows, jnp.zeros((), jnp.int32)),
     )
-    model = tokens.shape[1]
-    local_width = w_query.shape[1]
-    small = jnp.concatenate(
-        [
-            jnp.sum(hidden_grad * unit_attn, axis=0),
-            jnp.sum(hidden_grad, axis=0),
-            jnp.sum(out_grad * unit_ffn, axis=0),
-            jnp.sum(out_grad, axis=0),
-            score_part.reshape(-1),
-        ]
-    )
-    small_rows = -(-small.shape[0] // (16 * local_width)) * 16
-    small_low = (
-        jnp.pad(small, (0, small_rows * local_width - small.shape[0]))
-        .astype(jnp.bfloat16)
-        .reshape(small_rows, local_width)
-    )
-
-    dctx_send = ctx_grad_packed(attn_low, attn_other, w_out)
-    own_dctx = to_heads(dctx_send)
-    out_pack = out_grad_pack(
-        pass_count, after(attn_low, dctx_send), attn_other, context_low, small_low
-    )
-    own_dctx, out_pack = together(own_dctx, out_pack)
-    dkv, dq = attend_back(info, own_pack, sib_pack, own_dctx, ctx_turned, lse, key_turned)
-    dkv_sib, dq_sib = together(sibling(dkv), sibling(dq))
-    back_send = combine(info, dkv, dkv_sib, dq)
-    back = to_heads(back_send)
-    dkv, out_pack = after(dkv, back_send), after(out_pack, back_send)
-    out_mine = lax.dynamic_index_in_dim(out_pack, parity, 0, keepdims=False)
-    out_send = lax.dynamic_index_in_dim(out_pack, 1 - parity, 0, keepdims=False)
-    out_both = out_mine.astype(jnp.float32) + sibling(out_send).astype(jnp.float32)
-    head_grads = head_grad(info, tokens_all, dkv, dkv_sib, dq, dq_sib)
-    back, head_grads, out_both = together(back, head_grads, out_both.astype(jnp.bfloat16))
+    score_rows = jnp.pad(score_part.reshape(1, -1), ((0, 7), (0, local_width - score_part.size)))
+    small = jnp.concatenate([sums_attn, sums_ffn, score_rows], axis=0)
+    small = small + swap(small)
+    small = small + sibling(small)
+    head_grads = head_grad(info, tokens_all, back_own, sibling(back_own))
+    back, head_grads, small = together(back, head_grads, small)
     head_recv = to_heads(head_grads)
-    out_recv = to_heads(out_both)
     token_own, token_send = token_grad(back, w_query, w_key, w_value)
-    head_recv, token_send = together(head_recv, token_send)
     token_recv = swap(token_send)
+    late_sums = after(late_sums, token_recv)
+    colbert_all = lax.all_gather(
+        late_sums[:, 2 * width :], "pass", axis=0, axis_index_groups=ring, tiled=True
+    )
+    out_keep = after(out_keep, token_recv)
+    for step in range(1, bits):
+        out_keep, out_send = halve(info, first_bit + step, out_keep, out_came)
+        out_came = swap_over(out_send, "pass", 2 << step)
+    for step in range(bits):
+        small = small + swap_over(small, "pass", 2 << step)
+    grad_out = out_sum(out_keep, out_came, local_width)
     grad_tokens = attn_pre + token_own + token_recv.astype(jnp.float32)
-    out_recv = after(out_recv, token_recv)
-    grad_query, grad_key, grad_value = split_heads(head_recv)
-
+    grad_query, grad_key, grad_value = split_heads(after(head_recv, token_recv))
     grad_up = late_sums[:, :width].astype(jnp.float32)
     grad_down = late_sums[:, width : 2 * width].astype(jnp.float32).T
-    colbert_piece = after(late_sums, back)[:, 2 * width :]
-    colbert_sum = colbert_piece.astype(jnp.float32) + swap(colbert_piece).astype(jnp.float32)
-    grad_colbert = lax.all_gather(
-        colbert_sum.astype(jnp.bfloat16), "pass", axis=0, axis_index_groups=ring, tiled=True
-    ).astype(jnp.float32)
-
-    out_sums = jnp.sum(out_recv.astype(jnp.float32), axis=0)
-    grad_out = out_sums[: model // pass_count].T
-    small_sums = out_sums[model // pass_count :]
-    small_sums = (small_sums + swap(small_sums)).reshape(-1)
-    norms = small_sums[: 4 * model].reshape(4, model)
-    scores = small_sums[4 * model : small.shape[0]].reshape(score_part.shape)
+    grad_colbert = widen(after(colbert_all, grad_up, grad_down, grad_out))
+    norms = small[:8].reshape(4, model)
+    scores = small[8].reshape(-1)[: score_part.size].reshape(score_part.shape)
     return (
         output_low,
         scores,

time: 293 us -> 272 us (0.928)
  blocking collectives: 29.5 us -> 0 us
  starting transfers between devices: 37.8 us -> 58.7 us
  other arithmetic: 20.2 us -> 8.62 us
  local copies, waits for them, and re-layouts: 18.6 us -> 28.8 us
  Pallas kernels: 75.8 us -> 67.6 us
  waiting for transfers between devices: 77.5 us -> 69.5 us
    all_to_all x2 -> x0, blocking collectives: 29.5 us -> none  [to_heads(): lax.all_to_all(value, 'pass', 0, 0, axis_index_groups=same_core, tiled=True)]
    all_to_all x4 -> x5, waiting for transfers between devices: 32.8 us -> 16 us  [to_heads(): lax.all_to_all(value, 'pass', 0, 0, axis_index_groups=same_core, tiled=True)]
    ppermute x16 -> x23, starting transfers between devices: 18.6 us -> 35 us  [swap_over(): lax.ppermute(value, axis, [(index, index ^ mask) for index in range(count)])]
    unnamed x78 -> x139, local copies, waits for them, and re-layouts: 11 us -> 25.3 us
    pallas_call x1, Pallas kernels: 21.9 us -> 8.95 us  [attend(): pl.pallas_call(attend_body, in_specs=[pl.BlockSpec(memory_space=pltpu.SME...]
    pallas_call x4 -> x14, Pallas kernels: 18.5 us -> 29.8 us  [the longest x1 9.04 us: late_grad(): pl.pallas_call(functools.partial(late_grad_body, orders, tiles), in_specs...]
    convert_element_type x8 -> x0, other arithmetic: 9.5 us -> none  [the longest x1 4.07 us: local_by_head(): grad_colbert = lax.all_gather(colbert_sum.astype(jnp.bfloat16), 'pass', a...]
    reduce_scatter x1, waiting for transfers between devices: 0.01 us -> 5.71 us  [local_by_head(): lax.psum_scatter(late, 'pass', scatter_dimension=0, axis_index_groups=rin...]
  transfers between devices with their start and end apart: 23 -> 31, of which waited for: 15 -> 16; matrix products, arithmetic and copies ran while one was open for 15% -> 14% of each run, Pallas kernels for 25% -> 22%
where the time goes in v3:
time: 272 us; the launch traced here: 267 us
  waiting for transfers between devices  69.5 us (26%)
  Pallas kernels  67.6 us (25%)
  starting transfers between devices  58.7 us (22%)
  local copies, waits for them, and re-layouts  28.8 us (11%)
  matrix products  18.1 us (7%)
  between operations  15.9 us (6%)
  other arithmetic  8.62 us (3%)
    ppermute x23, waiting for transfers between devices, swap_over(): lax.ppermute(value, axis, [(index, index ^ mask) for index in range(count)])  47.8 us
    ppermute x23, starting transfers between devices, swap_over(): lax.ppermute(value, axis, [(index, index ^ mask) for index in range(count)])  35 us
    unnamed x139, local copies, waits for them, and re-layouts  25.3 us
    all_to_all x5, starting transfers between devices, to_heads(): lax.all_to_all(value, 'pass', 0, 0, axis_index_groups=same_core, tiled=True)  23.5 us
    all_to_all x5, waiting for transfers between devices, to_heads(): lax.all_to_all(value, 'pass', 0, 0, axis_index_groups=same_core, tiled=True)  16 us
    pallas_call x1, Pallas kernels, attend_back(): pl.pallas_call(attend_back_body, in_specs=[pl.BlockSpec(memory_space=pltp...  13.4 us
    dot_general x5, matrix products, dot_nn(): return jnp.dot(left, right, preferred_element_type=jnp.float32)  9.22 us
    pallas_call x1, Pallas kernels, late_grad(): pl.pallas_call(functools.partial(late_grad_body, orders, tiles), in_specs...  9.04 us
  transfers between devices with their start and end apart: 31, of which 16 were waited for; matrix products, arithmetic and copies ran while one was open for 14% of the time, Pallas kernels for 22%

profile of v3, /device:TPU:0, one launch (start us, length us, event | category | flops | bytes accessed | tf_op | source)
XLA Modules:
  0.0 267.4 jit_solution(11497968154956046086)
XLA Ops:
  12.4 4.3 %collective-permute-done = bf16[128,1024]{1,0:T(8,128)(2,1)S(1)} collective-permute-done((bf16[128,1024]{1,0:T(8,128)(2,1)}, bf16[128,1024]{1,0:T(8,128)(2,1)S(1)}, u32[]{:S(2)}, u32[]{:S(2)}) %collective-permute-start) | collective-permute-done | bytes 262176 | tf_op jit(solution)/shard_map/ppermute | solution.py:323
  17.5 4.0 %project.1 = bf16[8,384,128]{2,1,0:T(8,128)(2,1)} custom-call(bf16[256,1024]{1,0:T(8,128)(2,1)} %copy-done.2, bf16[1024,512]{1,0:T(8,128)(2,1)} %wq_ref.3, bf16[1024,512]{1,0:T(8,128)(2,1)} %wk_ref.3, bf16[1024,512]{1,0:T(8,128)(2,1)} %wv_ref.3), custom_call_target="tpu_custom_call" | custom-call | flops 805306368 | bytes 5242880 | tf_op jit(solution)/shard_map/project/pallas_call | solution.py:386
  21.5 6.2 %all-to-all-start = ((bf16[8,384,128]{2,1,0:T(8,128)(2,1)}), bf16[8,384,128]{2,1,0:T(8,128)(2,1)S(1)}, u32[]{:S(2)}, u32[]{:S(2)}) async-start(bf16[8,384,128]{2,1,0:T(8,128)(2,1)} %project.1), calls=%async_computation | async-start | bytes 1572864 | tf_op jit(solution)/shard_map/all_to_all | solution.py:1220
  33.3 3.9 %copy.37 = bf16[1024,1024]{0,1:T(8,128)(2,1)} copy(bf16[1024,1024]{1,0:T(8,128)(2,1)} %param.29) | data formatting | bytes 4194304 | tf_op args[12]
  37.5 5.5 %collective-permute-done.1.w_mine_ref = bf16[256,1024]{1,0:T(8,128)(2,1)S(1)} collective-permute-done((bf16[256,1024]{1,0:T(8,128)(2,1)S(1)}, bf16[256,1024]{1,0:T(8,128)(2,1)S(1)}, u32[]{:S(2)}, u32[]{:S(2)}) %collective-permute-start.1) | collective-permute-done | bytes 524320 | tf_op jit(solution)/shard_map/ppermute | solution.py:323
  50.2 9.0 %attend.1 = (bf16[8,128,128]{2,1,0:T(8,128)(2,1)}, f32[8,64,256]{2,1,0:T(8,128)S(1)}, f32[8,8,256]{2,1,0:T(8,128)S(1)}) custom-call(s32[36]{0:T(128)S(1)} %concatenate.16.info_ref, bf16[8,384,128]{2,1,0:T(8,128)(2,1)S(1)} %all-to-all-done.own_ref, bf16[8,384,128]{2,1,0:T(8,128)(2,1)S(1)} %collective-permute-done.3.sib_ref), custom_call_target="tpu_custom_call" | custom-call | flops 1342177280 | bytes 4194304 | tf_op jit(solution)/shard_map/attend/pallas_call | solution.py:521
  59.9 5.9 %all-to-all-start.1 = ((bf16[8,128,128]{2,1,0:T(8,128)(2,1)}), bf16[8,128,128]{2,1,0:T(8,128)(2,1)}, u32[]{:S(2)}, u32[]{:S(2)}) async-start(bf16[8,128,128]{2,1,0:T(8,128)(2,1)} %get-tuple-element.103), calls=%async_computation.1 | async-start | bytes 524288 | tf_op jit(solution)/shard_map/all_to_all | solution.py:1220
  76.3 4.7 %collective-permute-done.6.other_ref = bf16[8,128,128]{2,1,0:T(8,128)(2,1)S(1)} collective-permute-done((bf16[8,128,128]{2,1,0:T(8,128)(2,1)}, bf16[8,128,128]{2,1,0:T(8,128)(2,1)S(1)}, u32[]{:S(2)}, u32[]{:S(2)}) %collective-permute-start.6) | collective-permute-done | bytes 262176 | tf_op jit(solution)/shard_map/ppermute | solution.py:323
  85.4 4.0 %fusion.17 = (f32[128,2048]{1,0:T(8,128)S(1)}, bf16[128,2048]{1,0:T(8,128)(2,1)S(1)}) fusion(bf16[128,1024]{1,0:T(8,128)(2,1)S(1)} %get-tuple-element.115.refs_1_, bf16[1024,2048]{1,0:T(8,128)(2,1)} %param.24), kind=kOutput, calls=%fused_computation.24 | convolution fusion | flops 539492352 | bytes 6029312 | tf_op jit(solution)/shard_map/dot_general | solution.py:344
  111.8 9.0 %late_grad.1 = bf16[1024,5120]{1,0:T(8,128)(2,1)} custom-call(s32[1]{0:T(128)} %bitcast.9.first_ref, bf16[128,1024]{1,0:T(8,128)(2,1)} %copy-done.24, bf16[128,1024]{1,0:T(8,128)(2,1)} %copy-done.25, bf16[128,2048]{1,0:T(8,128)(2,1)} %copy-done.52, bf16[128,2048]{1,0:T(8,128)(2,1)} %copy-done.53, bf16[128,1024]{1,0:T(8,128)(2,1)} %copy-done.7, ...), custom_call_target="tpu_custom_call" | custom-call | flops 2684354560 | bytes 13631488 | tf_op jit(solution)/shard_map/late_grad/pallas_call | solution.py:981
  127.6 3.8 %all-to-all-start.2 = ((bf16[8,128,128]{2,1,0:T(8,128)(2,1)}), bf16[8,128,128]{2,1,0:T(8,128)(2,1)S(1)}, u32[]{:S(2)}, u32[]{:S(2)}) async-start(bf16[8,128,128]{2,1,0:T(8,128)(2,1)} %ctx_grad.1), calls=%async_computation.2 | async-start | bytes 524288 | tf_op jit(solution)/shard_map/all_to_all | solution.py:1220
  134.4 5.2 %all-to-all-done.2.dctx_ref = bf16[8,128,128]{2,1,0:T(8,128)(2,1)S(1)} async-done(((bf16[8,128,128]{2,1,0:T(8,128)(2,1)}), bf16[8,128,128]{2,1,0:T(8,128)(2,1)S(1)}, u32[]{:S(2)}, u32[]{:S(2)}) %all-to-all-start.2) | async-done | bytes 262176 | tf_op jit(solution)/shard_map/all_to_all | solution.py:1220
  140.3 13.4 %attend_back.1 = (bf16[8,256,128]{2,1,0:T(8,128)(2,1)}, bf16[8,256,128]{2,1,0:T(8,128)(2,1)}, bf16[8,128,128]{2,1,0:T(8,128)(2,1)}) custom-call(s32[36]{0:T(128)} %copy-done.33, bf16[16,256,128]{2,1,0:T(8,128)(2,1)} %copy-done.38, bf16[16,64,256]{2,1,0:T(8,128)(2,1)} %copy-done.39, bf16[8,256,128]{2,1,0:T(8,128)(2,1)} %copy-done.40, ...), custom_call_target="tpu_custom_call" | custom-call | flops 3355443200 | bytes 5242880 | tf_op jit(solution)/shard_map/attend_back/pallas_call | solution.py:645
  153.7 9.2 %collective-permute-start.11 = (bf16[8,256,128]{2,1,0:T(8,128)(2,1)}, bf16[8,256,128]{2,1,0:T(8,128)(2,1)S(1)}, u32[]{:S(2)}, u32[]{:S(2)}) collective-permute-start(bf16[8,256,128]{2,1,0:T(8,128)(2,1)} %get-tuple-element.155), channel_id=1, source_target_pairs={{0,2},{2,0},{4,6},{6,4},{8,10},{10,8},{12,14},{14,12},{16,18},{18,... | collective-permute-start | bytes 1572872 | tf_op jit(solution)/shard_map/ppermute | solution.py:323
  168.1 4.2 %all-to-all-start.3 = ((bf16[8,384,128]{2,1,0:T(8,128)(2,1)}), bf16[8,384,128]{2,1,0:T(8,128)(2,1)}, u32[]{:S(2)}, u32[]{:S(2)}) async-start(bf16[8,384,128]{2,1,0:T(8,128)(2,1)} %combine.1.own_ref), calls=%async_computation.3 | async-start | bytes 1572864 | tf_op jit(solution)/shard_map/all_to_all | solution.py:1220
  176.5 3.9 %collective-permute-done.14 = f32[16,512]{1,0:T(8,128)S(1)} collective-permute-done((f32[16,512]{1,0:T(8,128)S(1)}, f32[16,512]{1,0:T(8,128)S(1)}, u32[]{:S(2)}, u32[]{:S(2)}) %collective-permute-start.14) | collective-permute-done | bytes 32800 | tf_op jit(solution)/shard_map/ppermute | solution.py:323
  181.8 7.2 %head_grad.1 = bf16[8,96,128]{2,1,0:T(8,128)(2,1)} custom-call(s32[36]{0:T(128)S(1)} %copy-done.34, bf16[4096,1024]{1,0:T(8,128)(2,1)} %all-gather.3.cloned.1.call-done.tok_ref, bf16[8,384,128]{2,1,0:T(8,128)(2,1)} %combine.1.own_ref, bf16[8,384,128]{2,1,0:T(8,128)(2,1)} %collective-permute-done.12.sib_ref), custom_call_target="tpu_custom_call" | custom-call | flops 1610612736 | bytes 8388608 | tf_op jit(solution)/shard_map/head_grad/pallas_call | solution.py:820
  189.0 8.7 %all-to-all-done.3.in_ref = bf16[8,384,128]{2,1,0:T(8,128)(2,1)} async-done(((bf16[8,384,128]{2,1,0:T(8,128)(2,1)}), bf16[8,384,128]{2,1,0:T(8,128)(2,1)}, u32[]{:S(2)}, u32[]{:S(2)}) %all-to-all-start.3) | async-done | bytes 786464 | tf_op jit(solution)/shard_map/all_to_all | solution.py:1220
  200.7 7.6 %collective-permute-done.19 = bf16[128,1024]{1,0:T(8,128)(2,1)S(1)} collective-permute-done((bf16[128,1024]{1,0:T(8,128)(2,1)S(1)}, bf16[128,1024]{1,0:T(8,128)(2,1)S(1)}, u32[]{:S(2)}, u32[]{:S(2)}) %collective-permute-start.19) | collective-permute-done | bytes 262176 | tf_op jit(solution)/shard_map/ppermute | solution.py:323
  208.3 5.7 %reduce-scatter.2.cloned.1.call-done = bf16[64,5120]{1,0:T(8,128)(2,1)} async-done(((bf16[1024,5120]{1,0:T(8,128)(2,1)}), bf16[64,5120]{1,0:T(8,128)(2,1)}) %reduce-scatter.2.cloned.1.call-update) | async-done | bytes 655376 | tf_op jit(solution)/shard_map/reduce_scatter | solution.py:1357
  215.7 3.5 %collective-permute-start.20 = (bf16[4,256,128]{2,1,0:T(8,128)(2,1)}, bf16[4,256,128]{2,1,0:T(8,128)(2,1)S(1)}, u32[]{:S(2)}, u32[]{:S(2)}) collective-permute-start(bf16[4,256,128]{2,1,0:T(8,128)(2,1)} %copy-done.45), channel_id=1, source_target_pairs={{0,4},{2,6},{4,0},{6,2},{8,12},{10,14},{12,8},{14,10},{16,20},{18,... | collective-permute-start | bytes 786440 | tf_op jit(solution)/shard_map/ppermute | solution.py:323
  219.3 8.4 %collective-permute-done.16 = f32[16,512]{1,0:T(8,128)S(1)} collective-permute-done((f32[16,512]{1,0:T(8,128)S(1)}, f32[16,512]{1,0:T(8,128)S(1)}, u32[]{:S(2)}, u32[]{:S(2)}) %collective-permute-start.16) | collective-permute-done | bytes 32800 | tf_op jit(solution)/shard_map/ppermute | solution.py:323
  243.7 5.1 %collective-permute-done.21.came_ref = bf16[2,256,128]{2,1,0:T(8,128)(2,1)S(1)} collective-permute-done((bf16[2,256,128]{2,1,0:T(8,128)(2,1)S(1)}, bf16[2,256,128]{2,1,0:T(8,128)(2,1)S(1)}, u32[]{:S(2)}, u32[]{:S(2)}) %collective-permute-start.21) | collective-permute-done | bytes 131104 | tf_op jit(solution)/shard_map/ppermute | solution.py:323
  256.7 4.2 %widen.1 = f32[1024,1024]{1,0:T(8,128)} custom-call(bf16[1024,1024]{1,0:T(8,128)(2,1)} %all-gather.5.cloned.1.call-done.in_ref), custom_call_target="tpu_custom_call" | custom-call | flops 1048576 | bytes 6291456 | tf_op jit(solution)/shard_map/widen/pallas_call | solution.py:1027
  (243 shorter events, 105.0 us)
Async XLA Ops:
  7.2 9.5 %collective-permute-start = (bf16[128,1024]{1,0:T(8,128)(2,1)}, bf16[128,1024]{1,0:T(8,128)(2,1)S(1)}, u32[]{:S(2)}, u32[]{:S(2)}) collective-permute-start(bf16[128,1024]{1,0:T(8,128)(2,1)} %param.17), channel_id=1, source_target_pairs={{0,1},{1,0},{2,3},{3,2},{4,5},{5,4},{6,7},{7,6},{8,9},{9,8},{10,11... | collective-permute-start | bytes 786440 | tf_op jit(solution)/shard_map/ppermute | solution.py:323
  21.5 26.1 %all-to-all-start = ((bf16[8,384,128]{2,1,0:T(8,128)(2,1)}), bf16[8,384,128]{2,1,0:T(8,128)(2,1)S(1)}, u32[]{:S(2)}, u32[]{:S(2)}) async-start(bf16[8,384,128]{2,1,0:T(8,128)(2,1)} %project.1), calls=%async_computation | async-start | bytes 1572864 | tf_op jit(solution)/shard_map/all_to_all | solution.py:1220
  30.4 12.6 %collective-permute-start.1 = (bf16[256,1024]{1,0:T(8,128)(2,1)S(1)}, bf16[256,1024]{1,0:T(8,128)(2,1)S(1)}, u32[]{:S(2)}, u32[]{:S(2)}) collective-permute-start(bf16[256,1024]{1,0:T(8,128)(2,1)S(1)} %constant_dynamic-slice_fusion), channel_id=1, source_target_pairs={{0,1},{1,0},{2,3},{3,2},{4,5},{5,4},{6,7},{7,6},{8,9},{9,8},{10,11... | collective-permute-start | bytes 1572872 | tf_op jit(solution)/shard_map/ppermute | solution.py:323
  47.9 17.9 %collective-permute-start.4 = (bf16[256,1024]{1,0:T(8,128)(2,1)}, bf16[256,1024]{1,0:T(8,128)(2,1)}, u32[]{:S(2)}, u32[]{:S(2)}) collective-permute-start(bf16[256,1024]{1,0:T(8,128)(2,1)} %pad_maximum_fusion), channel_id=1, source_target_pairs={{0,1},{1,0},{2,3},{3,2},{4,5},{5,4},{6,7},{7,6},{8,9},{9,8},{10,11... | collective-permute-start | bytes 1572872 | tf_op jit(solution)/shard_map/ppermute | solution.py:323
  49.6 22.4 %collective-permute-start.5 = (bf16[128,1024]{1,0:T(8,128)(2,1)}, bf16[128,1024]{1,0:T(8,128)(2,1)}, u32[]{:S(2)}, u32[]{:S(2)}) collective-permute-start(bf16[128,1024]{1,0:T(8,128)(2,1)} %cot_ref.1), channel_id=1, source_target_pairs={{0,1},{1,0},{2,3},{3,2},{4,5},{5,4},{6,7},{7,6},{8,9},{9,8},{10,11... | collective-permute-start | bytes 786440 | tf_op jit(solution)/shard_map/ppermute | solution.py:323
  59.9 14.2 %all-to-all-start.1 = ((bf16[8,128,128]{2,1,0:T(8,128)(2,1)}), bf16[8,128,128]{2,1,0:T(8,128)(2,1)}, u32[]{:S(2)}, u32[]{:S(2)}) async-start(bf16[8,128,128]{2,1,0:T(8,128)(2,1)} %get-tuple-element.103), calls=%async_computation.1 | async-start | bytes 524288 | tf_op jit(solution)/shard_map/all_to_all | solution.py:1220
  65.8 116.0 %all-gather.3.cloned.1.call-start = ((), (), s32[]{:S(2)}) async-start(), calls=%async_computation.6 | async-start | bytes 8912896 | tf_op jit(solution)/shard_map/all_gather | solution.py:1284
  74.1 139.9 %reduce-scatter.2.cloned.1.call-start = ((), (), s32[]{:S(2)}) async-start(), calls=%async_computation.7 | async-start | bytes 11141120 | tf_op jit(solution)/shard_map/reduce_scatter | solution.py:1357
  74.4 6.6 %collective-permute-start.6 = (bf16[8,128,128]{2,1,0:T(8,128)(2,1)}, bf16[8,128,128]{2,1,0:T(8,128)(2,1)S(1)}, u32[]{:S(2)}, u32[]{:S(2)}) collective-permute-start(bf16[8,128,128]{2,1,0:T(8,128)(2,1)} %all-to-all-done.1.in_ref), channel_id=1, source_target_pairs={{0,1},{1,0},{2,3},{3,2},{4,5},{5,4},{6,7},{7,6},{8,9},{9,8},{10,11... | collective-permute-start | bytes 786440 | tf_op jit(solution)/shard_map/ppermute | solution.py:323
  90.2 6.5 %collective-permute-start.7 = (bf16[128,1024]{1,0:T(8,128)(2,1)S(1)}, bf16[128,1024]{1,0:T(8,128)(2,1)S(1)}, u32[]{:S(2)}, u32[]{:S(2)}) collective-permute-start(bf16[128,1024]{1,0:T(8,128)(2,1)S(1)} %convolution_convert_fusion.3.own_ref), channel_id=1, source_target_pairs={{0,1},{1,0},{2,3},{3,2},{4,5},{5,4},{6,7},{7,6},{8,9},{9,8},{10,11... | collective-permute-start | bytes 786440 | tf_op jit(solution)/shard_map/ppermute | solution.py:323
  94.1 7.5 %collective-permute-start.8 = (bf16[128,1024]{1,0:T(8,128)(2,1)S(1)}, bf16[128,1024]{1,0:T(8,128)(2,1)S(1)}, u32[]{:S(2)}, u32[]{:S(2)}) collective-permute-start(bf16[128,1024]{1,0:T(8,128)(2,1)S(1)} %convolution_convert_fusion.2.own_ref), channel_id=1, source_target_pairs={{0,1},{1,0},{2,3},{3,2},{4,5},{5,4},{6,7},{7,6},{8,9},{9,8},{10,11... | collective-permute-start | bytes 786440 | tf_op jit(solution)/shard_map/ppermute | solution.py:323
  109.7 11.2 %collective-permute-start.10 = (bf16[128,1024]{1,0:T(8,128)(2,1)S(1)}, bf16[128,1024]{1,0:T(8,128)(2,1)}, u32[]{:S(2)}, u32[]{:S(2)}) collective-permute-start(bf16[128,1024]{1,0:T(8,128)(2,1)S(1)} %convolution_convert_fusion.own_ref), channel_id=1, source_target_pairs={{0,1},{1,0},{2,3},{3,2},{4,5},{5,4},{6,7},{7,6},{8,9},{9,8},{10,11... | collective-permute-start | bytes 786440 | tf_op jit(solution)/shard_map/ppermute | solution.py:323
  111.7 9.2 %collective-permute-start.9 = (bf16[128,1024]{1,0:T(8,128)(2,1)S(1)}, bf16[128,1024]{1,0:T(8,128)(2,1)S(1)}, u32[]{:S(2)}, u32[]{:S(2)}) collective-permute-start(bf16[128,1024]{1,0:T(8,128)(2,1)S(1)} %convolution_convert_fusion.1.own_ref), channel_id=1, source_target_pairs={{0,1},{1,0},{2,3},{3,2},{4,5},{5,4},{6,7},{7,6},{8,9},{9,8},{10,11... | collective-permute-start | bytes 786440 | tf_op jit(solution)/shard_map/ppermute | solution.py:323
  127.6 12.0 %all-to-all-start.2 = ((bf16[8,128,128]{2,1,0:T(8,128)(2,1)}), bf16[8,128,128]{2,1,0:T(8,128)(2,1)S(1)}, u32[]{:S(2)}, u32[]{:S(2)}) async-start(bf16[8,128,128]{2,1,0:T(8,128)(2,1)} %ctx_grad.1), calls=%async_computation.2 | async-start | bytes 524288 | tf_op jit(solution)/shard_map/all_to_all | solution.py:1220
  153.7 11.1 %collective-permute-start.11 = (bf16[8,256,128]{2,1,0:T(8,128)(2,1)}, bf16[8,256,128]{2,1,0:T(8,128)(2,1)S(1)}, u32[]{:S(2)}, u32[]{:S(2)}) collective-permute-start(bf16[8,256,128]{2,1,0:T(8,128)(2,1)} %get-tuple-element.155), channel_id=1, source_target_pairs={{0,2},{2,0},{4,6},{6,4},{8,10},{10,8},{12,14},{14,12},{16,18},{18,... | collective-permute-start | bytes 1572872 | tf_op jit(solution)/shard_map/ppermute | solution.py:323
  168.1 29.6 %all-to-all-start.3 = ((bf16[8,384,128]{2,1,0:T(8,128)(2,1)}), bf16[8,384,128]{2,1,0:T(8,128)(2,1)}, u32[]{:S(2)}, u32[]{:S(2)}) async-start(bf16[8,384,128]{2,1,0:T(8,128)(2,1)} %combine.1.own_ref), calls=%async_computation.3 | async-start | bytes 1572864 | tf_op jit(solution)/shard_map/all_to_all | solution.py:1220
  172.4 84.3 %all-gather.5.cloned.1.call-start = ((), (), s32[]{:S(2)}) async-start(), calls=%async_computation.8 | async-start | bytes 2228224 | tf_op jit(solution)/shard_map/all_gather | solution.py:1403
  172.4 9.3 %collective-permute-start.12 = (bf16[8,384,128]{2,1,0:T(8,128)(2,1)}, bf16[8,384,128]{2,1,0:T(8,128)(2,1)}, u32[]{:S(2)}, u32[]{:S(2)}) collective-permute-start(bf16[8,384,128]{2,1,0:T(8,128)(2,1)} %combine.1.own_ref), channel_id=1, source_target_pairs={{0,2},{2,0},{4,6},{6,4},{8,10},{10,8},{12,14},{14,12},{16,18},{18,... | collective-permute-start | bytes 2359304 | tf_op jit(solution)/shard_map/ppermute | solution.py:323
  200.7 7.6 %collective-permute-start.19 = (bf16[128,1024]{1,0:T(8,128)(2,1)S(1)}, bf16[128,1024]{1,0:T(8,128)(2,1)S(1)}, u32[]{:S(2)}, u32[]{:S(2)}) collective-permute-start(bf16[128,1024]{1,0:T(8,128)(2,1)S(1)} %get-tuple-element.173), channel_id=1, source_target_pairs={{0,1},{1,0},{2,3},{3,2},{4,5},{5,4},{6,7},{7,6},{8,9},{9,8},{10,11... | collective-permute-start | bytes 786440 | tf_op jit(solution)/shard_map/ppermute | solution.py:323
  215.7 22.2 %collective-permute-start.20 = (bf16[4,256,128]{2,1,0:T(8,128)(2,1)}, bf16[4,256,128]{2,1,0:T(8,128)(2,1)S(1)}, u32[]{:S(2)}, u32[]{:S(2)}) collective-permute-start(bf16[4,256,128]{2,1,0:T(8,128)(2,1)} %copy-done.45), channel_id=1, source_target_pairs={{0,4},{2,6},{4,0},{6,2},{8,12},{10,14},{12,8},{14,10},{16,20},{18,... | collective-permute-start | bytes 786440 | tf_op jit(solution)/shard_map/ppermute | solution.py:323
  219.2 8.5 %collective-permute-start.16 = (f32[16,512]{1,0:T(8,128)S(1)}, f32[16,512]{1,0:T(8,128)S(1)}, u32[]{:S(2)}, u32[]{:S(2)}) collective-permute-start(f32[16,512]{1,0:T(8,128)S(1)} %add.98), channel_id=1, source_target_pairs={{0,4},{2,6},{4,0},{6,2},{8,12},{10,14},{12,8},{14,10},{16,20},{18,... | collective-permute-start | bytes 98312 | tf_op jit(solution)/shard_map/ppermute | solution.py:323
  232.0 5.9 %collective-permute-start.18 = (f32[16,512]{1,0:T(8,128)S(1)}, f32[16,512]{1,0:T(8,128)S(1)}, u32[]{:S(2)}, u32[]{:S(2)}) collective-permute-start(f32[16,512]{1,0:T(8,128)S(1)} %add.100), channel_id=1, source_target_pairs={{0,16},{2,18},{4,20},{6,22},{8,24},{10,26},{12,28},{14,30},{16,0},... | collective-permute-start | bytes 98312 | tf_op jit(solution)/shard_map/ppermute | solution.py:323
  234.5 18.3 %all-to-all-start.4 = ((bf16[8,96,128]{2,1,0:T(8,128)(2,1)}), bf16[8,96,128]{2,1,0:T(8,128)(2,1)S(1)}, u32[]{:S(2)}, u32[]{:S(2)}) async-start(bf16[8,96,128]{2,1,0:T(8,128)(2,1)} %head_grad.1), calls=%async_computation.4 | async-start | bytes 393216 | tf_op jit(solution)/shard_map/all_to_all | solution.py:1220
  238.6 10.2 %collective-permute-start.21 = (bf16[2,256,128]{2,1,0:T(8,128)(2,1)S(1)}, bf16[2,256,128]{2,1,0:T(8,128)(2,1)S(1)}, u32[]{:S(2)}, u32[]{:S(2)}) collective-permute-start(bf16[2,256,128]{2,1,0:T(8,128)(2,1)S(1)} %get-tuple-element.182), channel_id=1, source_target_pairs={{0,8},{2,10},{4,12},{6,14},{8,0},{10,2},{12,4},{14,6},{16,24},{18,... | collective-permute-start | bytes 393224 | tf_op jit(solution)/shard_map/ppermute | solution.py:323
  (72 other events, 638.7 us)
Sparse Core Ops, SparseCore 0:
  74.3 60.2 all-gather.2
  136.9 77.0 reduce-scatter.1
  215.8 36.3 all-gather.4

commit v4 on v3

--- a/solution.py
+++ b/solution.py
@@ -424,10 +424,22 @@
             step(first + (count & ~(2 * size - 1)), size)
 
 
+def load_block(near_ref, far_ref, chip, block_ref):
+    half = block_ref.shape[0] // 2
+    block_ref[:half] = near_ref[chip, 0:half]
+    block_ref[half:] = far_ref[chip, 0:half]
+
+
+def load_queries(near_ref, far_ref, chip, block_ref):
+    half = block_ref.shape[0] // 2
+    block_ref[:half] = load_query(near_ref[chip, half:])
+    block_ref[half:] = load_query(far_ref[chip, half:])
+
+
 def attend_body(
-    info_ref, own_ref, sib_ref, ctx_ref, ctxt_ref, lse_ref, kv_s, v1_s, q_s, total_s, score_s, top_s
+    info_ref, near_ref, far_ref, near_sib_ref, far_sib_ref, ctx_ref, ctxt_ref, lse_ref, kv_s, v1_s, q_s, total_s, score_s, top_s
 ):
-    chips = own_ref.shape[0]
+    chips = near_ref.shape[0]
     blocks = 2 * chips
     rows = kv_s.shape[1]
     half = rows // 2
@@ -436,16 +448,17 @@
     low = low_lanes(rows)
     key_top = query_top = jnp.zeros((8, LANES), jnp.float32)
     for chip in range(chips):
-        for ref, which in ((own_ref, parity), (sib_ref, 1 - parity)):
-            block = ref[chip, 0:rows]
-            kv_s[2 * chip + which] = block
-            v1_s[2 * chip + which] = jnp.where(low, 1.0, block.astype(jnp.float32)).astype(
-                jnp.bfloat16
-            )
+        for refs, which in (
+            ((near_ref, far_ref), parity),
+            ((near_sib_ref, far_sib_ref), 1 - parity),
+        ):
+            place = 2 * chip + which
+            load_block(*refs, chip, kv_s.at[place])
+            block = kv_s[place]
+            v1_s[place] = jnp.where(low, 1.0, block.astype(jnp.float32)).astype(jnp.bfloat16)
             key_top = jnp.maximum(key_top, square_sums(block))
-        packed = own_ref[chip, rows : rows + half]
-        q_s[chip] = load_query(packed)
-        query_top = jnp.maximum(query_top, square_sums(packed))
+        load_queries(near_ref, far_ref, chip, q_s.at[chip])
+        query_top = jnp.maximum(query_top, square_sums(q_s[chip]))
     key_top = jnp.max(jnp.where(low_lanes(8), key_top, 0.0))
     bound = jnp.max(query_top) * key_top * (1.02 * scale * scale)
     safe = bound < 3600.0
@@ -514,13 +527,13 @@
     return pl.BlockSpec(memory_space=pltpu.VMEM)
 
 
-def attend(info, own, sib):
-    chips, packed, _ = own.shape
-    rows = packed * 2 // 3
+def attend(info, *packs):
+    chips, packed, _ = packs[0].shape
+    rows = packed * 4 // 3
     blocks = 2 * chips
     return pl.pallas_call(
         attend_body,
-        in_specs=[pl.BlockSpec(memory_space=pltpu.SMEM), whole(), whole()],
+        in_specs=[pl.BlockSpec(memory_space=pltpu.SMEM)] + [whole()] * 4,
         out_specs=[whole()] * 3,
         out_shape=[
             jax.ShapeDtypeStruct((chips, rows // 2, LANES), jnp.bfloat16),
@@ -535,30 +548,32 @@
             pltpu.VMEM((SPAN, rows, rows), jnp.float32),
             pltpu.VMEM((chips, 8, rows), jnp.float32),
         ],
-        compiler_params=params(limit=2 * VMEM_LIMIT),
+        compiler_params=params(limit=WIDE_LIMIT),
         cost_estimate=cost(2 * 2 * 40 * rows * rows * LANES, 4 << 20, 40 * rows * rows),
         name="attend",
-    )(info, own, sib)
-
-
-def prepare_body(info_ref, own_ref, sib_ref, kv_ref, kt_ref, q_ref):
-    chips = own_ref.shape[0]
-    rows = kv_ref.shape[1]
+    )(info, *packs)
+
+
+def prepare_body(info_ref, near_ref, far_ref, near_sib_ref, far_sib_ref, kv_ref, kt_ref, q_ref):
+    chips = near_ref.shape[0]
     parity = info_ref[4 * chips]
     for chip in range(chips):
-        for ref, which in ((own_ref, parity), (sib_ref, 1 - parity)):
-            block = ref[chip, 0:rows]
-            kv_ref[2 * chip + which] = block
-            kt_ref[2 * chip + which] = block.astype(jnp.float32).T[:HD].astype(jnp.bfloat16)
-        q_ref[chip] = load_query(own_ref[chip, rows : rows + rows // 2])
-
-
-def prepare(info, own, sib):
-    chips, packed, _ = own.shape
-    rows = packed * 2 // 3
+        for refs, which in (
+            ((near_ref, far_ref), parity),
+            ((near_sib_ref, far_sib_ref), 1 - parity),
+        ):
+            place = 2 * chip + which
+            load_block(*refs, chip, kv_ref.at[place])
+            kt_ref[place] = kv_ref[place].astype(jnp.float32).T[:HD].astype(jnp.bfloat16)
+        load_queries(near_ref, far_ref, chip, q_ref.at[chip])
+
+
+def prepare(info, *packs):
+    chips, packed, _ = packs[0].shape
+    rows = packed * 4 // 3
     return pl.pallas_call(
         prepare_body,
-        in_specs=[pl.BlockSpec(memory_space=pltpu.SMEM), whole(), whole()],
+        in_specs=[pl.BlockSpec(memory_space=pltpu.SMEM)] + [whole()] * 4,
         out_specs=[whole()] * 3,
         out_shape=[
             jax.ShapeDtypeStruct((2 * chips, rows, LANES), jnp.bfloat16),
@@ -568,7 +583,7 @@
         compiler_params=params(),
         cost_estimate=cost(1 << 20, 4 << 20),
         name="prepare",
-    )(info, own, sib)
+    )(info, *packs)
 
 
 def attend_back_body(
@@ -1145,7 +1160,7 @@
     along = jnp.sum(vec * pick, axis=1, keepdims=True)
     proj_low = ((pick - vec * along) * scale).astype(jnp.bfloat16)
     proj_ref[...] = proj_low
-    grad = cot_ref[...].astype(jnp.float32) + dot_nt(proj_low, w_ref[...])
+    grad = cot_ref[...] + dot_nt(proj_low, w_ref[...])
     pre = back_rows(grad, gain, unit, inverse)
     pre_ref[...] = pre
     low_ref[...] = pre.astype(jnp.bfloat16)
@@ -1227,6 +1242,8 @@
     def together(*values):
         return lax.optimization_barrier(values)
 
+    near_send = project(tokens, w_query, w_key, w_value)
+    near_pack = to_heads(near_send)
     tokens_other = swap(tokens)
     gathered = jnp.concatenate([tokens, tokens_other], axis=0)
     block_ids = passage_of.astype(jnp.int32)
@@ -1261,28 +1278,34 @@
     turned_part = jnp.concatenate([unit_grad_part[own_rows:], unit_grad_part[:own_rows]], axis=0)
     unit_grad_send = turned_part.astype(jnp.bfloat16)
 
-    own_send = project(gathered, w_query, w_key, w_value)
-    own_pack = to_heads(own_send)
+    far_send = project(after(tokens_other, near_send), w_query, w_key, w_value)
+    near_pack, far_send = together(near_pack, far_send)
+    far_pack = to_heads(far_send)
+    near_sib = sibling(near_pack)
     piece = w_out.shape[0] // 2
     w_out_send = lax.dynamic_slice_in_dim(w_out, parity * piece, piece, axis=0)
-    w_out_mine = swap(after(w_out_send, own_send))
+    w_out_mine = swap(after(w_out_send, tokens_other))
     w_out_sib = sibling(w_out_mine)
-    own_pack, unit_grad_send, w_out_sib = together(own_pack, unit_grad_send, w_out_sib)
-    sib_pack = sibling(own_pack)
+    far_pack, near_sib, unit_grad_send, w_out_sib, gathered = together(
+        far_pack, near_sib, unit_grad_send, w_out_sib, gathered
+    )
+    packs = (near_pack, far_pack, near_sib, sibling(far_pack))
     unit_grad_recv = swap(unit_grad_send)
     cot_other = swap(after(cot_act, unit_grad_send))
-    ctx_pack, ctx_turned, lse = attend(info, own_pack, sib_pack)
+    ctx_pack, ctx_turned, lse = attend(info, *packs)
     unit_grad = unit_grad_part.astype(jnp.bfloat16).astype(jnp.float32) + unit_grad_recv.astype(
         jnp.float32
     )
     unit_grad_own, unit_grad_other = unit_grad[:own_rows], unit_grad[own_rows:]
     ctx_recv = to_heads(ctx_pack)
-    ready = prepare(info, after(own_pack, ctx_pack), sib_pack)
-    ctx_recv, unit_grad_own, unit_grad_other, cot_other, kv, key_turned, query = together(
-        ctx_recv, unit_grad_own, unit_grad_other, cot_other, *ready
+    ready = prepare(info, after(near_pack, ctx_pack), *packs[1:])
+    cot_near = after(cot_act, ctx_pack).astype(jnp.float32)
+    cot_far = after(cot_other, ctx_pack).astype(jnp.float32)
+    ctx_recv, unit_grad_own, unit_grad_other, cot_near, cot_far, kv, key_turned, query = together(
+        ctx_recv, unit_grad_own, unit_grad_other, cot_near, cot_far, *ready
     )
     tokens_all = lax.all_gather(
-        after(gathered, ctx_recv), "pass", axis=0, axis_index_groups=ring, tiled=True
+        after(gathered, far_pack), "pass", axis=0, axis_index_groups=ring, tiled=True
     )
     (
         context_low,
@@ -1333,27 +1356,27 @@
         )
 
     output_low, unit_own, proj_own, pre_grad, pre_low, sums_ffn = turned(
-        hidden, part_own, recv_own, unit_grad_own, cot_act
+        hidden, part_own, recv_own, unit_grad_own, cot_near
     )
     inner_own = (dot_nt(pre_low, w_down) * slope_own).astype(jnp.bfloat16)
     recv_other, inner_own = together(recv_other, inner_own)
     output_other, unit_other, proj_other, pre_far, pre_other, _ = turned(
-        hidden_far, part_other, recv_other, unit_grad_other, cot_other
+        hidden_far, part_other, recv_other, unit_grad_other, cot_far
     )
     inner_other = (dot_nt(pre_other, w_down) * slope_other).astype(jnp.bfloat16)
-    part_own, part_other, recv_own, recv_other = both_halves(
-        inner_own, inner_other, lambda rows: dot_nt(rows, w_up)
-    )
     late = late_grad(
         qry_index[None].astype(jnp.int32),
         chips,
         (
-            (hidden_low, hidden_other, after(inner_own, part_own), inner_other, True),
+            (hidden_low, hidden_other, inner_own, inner_other, True),
             (pre_low, pre_other, gated_own, gated_other, True),
             (output_low, output_other, proj_own, proj_other, False),
         ),
     )
-    recv_own, recv_other, late = together(recv_own, recv_other, late)
+    inner_own, inner_other, late = together(inner_own, inner_other, late)
+    part_own, part_other, recv_own, recv_other = both_halves(
+        inner_own, inner_other, lambda rows: dot_nt(rows, w_up)
+    )
     late_sums = lax.psum_scatter(
         late, "pass", scatter_dimension=0, axis_index_groups=ring, tiled=True
     )
@@ -1395,11 +1418,10 @@
     small = small + swap(small)
     small = small + sibling(small)
     head_grads = head_grad(info, tokens_all, back_own, sibling(back_own))
-    back, head_grads, small = together(back, head_grads, small)
+    back, head_grads, small, late_sums = together(back, head_grads, small, late_sums)
     head_recv = to_heads(head_grads)
     token_own, token_send = token_grad(back, w_query, w_key, w_value)
     token_recv = swap(token_send)
-    late_sums = after(late_sums, token_recv)
     colbert_all = lax.all_gather(
         late_sums[:, 2 * width :], "pass", axis=0, axis_index_groups=ring, tiled=True
     )

time: 272 us -> 268 us (0.985); the launches traced: 267 us -> 267 us
  Pallas kernels: 67.6 us -> 80.1 us
  waiting for transfers between devices: 69.5 us -> 57.4 us
  starting transfers between devices: 58.7 us -> 53.7 us
  matrix products: 18.1 us -> 22 us
    ppermute x23 -> x24, waiting for transfers between devices: 47.8 us -> 31.8 us  [swap_over(): lax.ppermute(value, axis, [(index, index ^ mask) for index in range(count)])]
    pallas_call x1, Pallas kernels: 8.95 us -> 22.6 us  [attend(): pl.pallas_call(attend_body, in_specs=[pl.BlockSpec(memory_space=pltpu.SME...]
    ppermute x23 -> x24, starting transfers between devices: 35 us -> 24.8 us  [swap_over(): lax.ppermute(value, axis, [(index, index ^ mask) for index in range(count)])]
    all_to_all x5 -> x6, waiting for transfers between devices: 16 us -> 25.6 us  [to_heads(): lax.all_to_all(value, 'pass', 0, 0, axis_index_groups=same_core, tiled=True)]
    reduce_scatter x1, waiting for transfers between devices: 5.71 us -> 0.01 us  [local_by_head(): lax.psum_scatter(late, 'pass', scatter_dimension=0, axis_index_groups=rin...]
    all_to_all x5 -> x6, starting transfers between devices: 23.5 us -> 28.6 us  [to_heads(): lax.all_to_all(value, 'pass', 0, 0, axis_index_groups=same_core, tiled=True)]
    dot_general x4, matrix products: 6.09 us -> 10 us  [contract_cols(): lax.dot_general(left, right, (((1,), (1,)), ((), ())), preferred_element_...]
    unnamed x139 -> x150, local copies, waits for them, and re-layouts: 25.3 us -> 22 us
  transfers between devices with their start and end apart: 31 -> 33, of which waited for: 16 -> 15; matrix products, arithmetic and copies ran while one was open for 14% -> 16% of each run, Pallas kernels for 22% -> 28%
where the time goes in v4:
time: 268 us; the launch traced here: 267 us
  Pallas kernels  80.1 us (30%)
  waiting for transfers between devices  57.4 us (21%)
  starting transfers between devices  53.7 us (20%)
  local copies, waits for them, and re-layouts  26.2 us (10%)
  matrix products  22 us (8%)
  between operations  16 us (6%)
  other arithmetic  11.3 us (4%)
    ppermute x24, waiting for transfers between devices, swap_over(): lax.ppermute(value, axis, [(index, index ^ mask) for index in range(count)])  31.8 us
    all_to_all x6, starting transfers between devices, to_heads(): lax.all_to_all(value, 'pass', 0, 0, axis_index_groups=same_core, tiled=True)  28.6 us
    all_to_all x6, waiting for transfers between devices, to_heads(): lax.all_to_all(value, 'pass', 0, 0, axis_index_groups=same_core, tiled=True)  25.6 us
    ppermute x24, starting transfers between devices, swap_over(): lax.ppermute(value, axis, [(index, index ^ mask) for index in range(count)])  24.8 us
    pallas_call x1, Pallas kernels, attend(): pl.pallas_call(attend_body, in_specs=[pl.BlockSpec(memory_space=pltpu.SME...  22.6 us
    unnamed x150, local copies, waits for them, and re-layouts  22 us
    pallas_call x1, Pallas kernels, attend_back(): pl.pallas_call(attend_back_body, in_specs=[pl.BlockSpec(memory_space=pltp...  12 us
    dot_general x4, matrix products, contract_cols(): lax.dot_general(left, right, (((1,), (1,)), ((), ())), preferred_element_...  10 us
  transfers between devices with their start and end apart: 33, of which 15 were waited for; matrix products, arithmetic and copies ran while one was open for 16% of the time, Pallas kernels for 28%

profile of v4, /device:TPU:0, one launch (start us, length us, event | category | flops | bytes accessed | tf_op | source)
XLA Modules:
  0.0 266.6 jit_solution(3616308241130343193)
XLA Ops:
  13.6 5.8 %all-to-all-start = ((bf16[8,192,128]{2,1,0:T(8,128)(2,1)}), bf16[8,192,128]{2,1,0:T(8,128)(2,1)S(1)}, u32[]{:S(2)}, u32[]{:S(2)}) async-start(bf16[8,192,128]{2,1,0:T(8,128)(2,1)} %project.2), calls=%async_computation | async-start | bytes 786432 | tf_op jit(solution)/shard_map/all_to_all | solution.py:1235
  24.6 3.9 %copy.37 = bf16[1024,1024]{0,1:T(8,128)(2,1)} copy(bf16[1024,1024]{1,0:T(8,128)(2,1)} %param.29) | data formatting | bytes 4194304 | tf_op args[12]
  28.8 3.4 %project.3 = bf16[8,192,128]{2,1,0:T(8,128)(2,1)} custom-call(bf16[128,1024]{1,0:T(8,128)(2,1)} %copy-done.63, bf16[1024,512]{1,0:T(8,128)(2,1)} %wq_ref.5, bf16[1024,512]{1,0:T(8,128)(2,1)} %wk_ref.5, bf16[1024,512]{1,0:T(8,128)(2,1)} %wv_ref.5), custom_call_target="tpu_custom_call" | custom-call | flops 402653184 | bytes 4194304 | tf_op jit(solution)/shard_map/project/pallas_call | solution.py:386
  32.2 6.1 %all-to-all-start.1 = ((bf16[8,192,128]{2,1,0:T(8,128)(2,1)}), bf16[8,192,128]{2,1,0:T(8,128)(2,1)S(1)}, u32[]{:S(2)}, u32[]{:S(2)}) async-start(bf16[8,192,128]{2,1,0:T(8,128)(2,1)} %project.3), calls=%async_computation.1 | async-start | bytes 786432 | tf_op jit(solution)/shard_map/all_to_all | solution.py:1235
  44.6 4.3 %all-to-all-done.1.far_ref = bf16[8,192,128]{2,1,0:T(8,128)(2,1)S(1)} async-done(((bf16[8,192,128]{2,1,0:T(8,128)(2,1)}), bf16[8,192,128]{2,1,0:T(8,128)(2,1)S(1)}, u32[]{:S(2)}, u32[]{:S(2)}) %all-to-all-start.1) | async-done | bytes 393248 | tf_op jit(solution)/shard_map/all_to_all | solution.py:1235
  53.0 22.6 %attend.1 = (bf16[8,128,128]{2,1,0:T(8,128)(2,1)}, f32[8,64,256]{2,1,0:T(8,128)}, f32[8,8,256]{2,1,0:T(8,128)}) custom-call(s32[36]{0:T(128)} %concatenate.16.info_ref, bf16[8,192,128]{2,1,0:T(8,128)(2,1)} %copy-done.7, bf16[8,192,128]{2,1,0:T(8,128)(2,1)} %copy-done.9, bf16[8,192,128]{2,1,0:T(8,128)(2,1)} %copy-done.24, bf16[8,192,128]{2,1,0:T(8,128)(2,1)} %copy-done.26), custom_call_target="tpu_custom_call" | custom-call | flops 1342177280 | bytes 4194304 | tf_op jit(solution)/shard_map/attend/pallas_call | solution.py:534
  75.6 3.8 %all-to-all-start.2 = ((bf16[8,128,128]{2,1,0:T(8,128)(2,1)}), bf16[8,128,128]{2,1,0:T(8,128)(2,1)S(1)}, u32[]{:S(2)}, u32[]{:S(2)}) async-start(bf16[8,128,128]{2,1,0:T(8,128)(2,1)} %get-tuple-element.114), calls=%async_computation.2 | async-start | bytes 524288 | tf_op jit(solution)/shard_map/all_to_all | solution.py:1235
  87.9 5.0 %all-to-all-done.2.in_ref = bf16[8,128,128]{2,1,0:T(8,128)(2,1)S(1)} async-done(((bf16[8,128,128]{2,1,0:T(8,128)(2,1)}), bf16[8,128,128]{2,1,0:T(8,128)(2,1)S(1)}, u32[]{:S(2)}, u32[]{:S(2)}) %all-to-all-start.2) | async-done | bytes 262176 | tf_op jit(solution)/shard_map/all_to_all | solution.py:1235
  94.0 5.5 %collective-permute-done.7.other_ref = bf16[8,128,128]{2,1,0:T(8,128)(2,1)S(1)} collective-permute-done((bf16[8,128,128]{2,1,0:T(8,128)(2,1)S(1)}, bf16[8,128,128]{2,1,0:T(8,128)(2,1)S(1)}, u32[]{:S(2)}, u32[]{:S(2)}) %collective-permute-start.7) | collective-permute-done | bytes 262176 | tf_op jit(solution)/shard_map/ppermute | solution.py:323
  103.3 4.0 %fusion.17 = (f32[128,2048]{1,0:T(8,128)S(1)}, bf16[128,2048]{1,0:T(8,128)(2,1)S(1)}) fusion(bf16[128,1024]{1,0:T(8,128)(2,1)S(1)} %get-tuple-element.129.refs_1_, bf16[1024,2048]{1,0:T(8,128)(2,1)} %param.24), kind=kOutput, calls=%fused_computation.24 | convolution fusion | flops 539492352 | bytes 6029312 | tf_op jit(solution)/shard_map/dot_general | solution.py:344
  112.3 4.9 %collective-permute-done.8.recv_ref = bf16[128,1024]{1,0:T(8,128)(2,1)S(1)} collective-permute-done((bf16[128,1024]{1,0:T(8,128)(2,1)S(1)}, bf16[128,1024]{1,0:T(8,128)(2,1)S(1)}, u32[]{:S(2)}, u32[]{:S(2)}) %collective-permute-start.8) | collective-permute-done | bytes 262176 | tf_op jit(solution)/shard_map/ppermute | solution.py:323
  126.7 9.2 %late_grad.1 = bf16[1024,5120]{1,0:T(8,128)(2,1)} custom-call(s32[1]{0:T(128)} %bitcast.9.first_ref, bf16[128,1024]{1,0:T(8,128)(2,1)} %copy-done.28, bf16[128,1024]{1,0:T(8,128)(2,1)} %copy-done.29, bf16[128,2048]{1,0:T(8,128)(2,1)} %fusion.2.refs_2_, bf16[128,2048]{1,0:T(8,128)(2,1)} %fusion.3.refs_3_, bf16[128,1024]{1,0:T(8,128)(2,1)} %copy-done.11, ...), custom_call_target="tpu_custom_call" | custom-call | flops 2684354560 | bytes 13631488 | tf_op jit(solution)/shard_map/late_grad/pallas_call | solution.py:996
  136.9 3.8 %convolution_convert_fusion.1.own_ref = bf16[128,1024]{1,0:T(8,128)(2,1)S(1)} fusion(bf16[128,2048]{1,0:T(8,128)(2,1)S(1)} %copy-done.58, bf16[1024,2048]{1,0:T(8,128)(2,1)} %param.24), kind=kOutput, calls=%fused_computation.14 | convolution fusion | flops 537001984 | bytes 4980736 | tf_op jit(solution)/shard_map/dot_general | solution.py:68
  144.5 5.4 %collective-permute-done.11.recv_ref = bf16[128,1024]{1,0:T(8,128)(2,1)S(1)} collective-permute-done((bf16[128,1024]{1,0:T(8,128)(2,1)S(1)}, bf16[128,1024]{1,0:T(8,128)(2,1)S(1)}, u32[]{:S(2)}, u32[]{:S(2)}) %collective-permute-start.11) | collective-permute-done | bytes 262176 | tf_op jit(solution)/shard_map/ppermute | solution.py:323
  155.1 3.6 %all-to-all-start.3 = ((bf16[8,128,128]{2,1,0:T(8,128)(2,1)}), bf16[8,128,128]{2,1,0:T(8,128)(2,1)S(1)}, u32[]{:S(2)}, u32[]{:S(2)}) async-start(bf16[8,128,128]{2,1,0:T(8,128)(2,1)} %ctx_grad.1), calls=%async_computation.3 | async-start | bytes 524288 | tf_op jit(solution)/shard_map/all_to_all | solution.py:1235
  160.7 8.0 %all-to-all-done.3.dctx_ref = bf16[8,128,128]{2,1,0:T(8,128)(2,1)S(1)} async-done(((bf16[8,128,128]{2,1,0:T(8,128)(2,1)}), bf16[8,128,128]{2,1,0:T(8,128)(2,1)S(1)}, u32[]{:S(2)}, u32[]{:S(2)}) %all-to-all-start.3) | async-done | bytes 262176 | tf_op jit(solution)/shard_map/all_to_all | solution.py:1235
  169.4 12.0 %attend_back.1 = (bf16[8,256,128]{2,1,0:T(8,128)(2,1)}, bf16[8,256,128]{2,1,0:T(8,128)(2,1)}, bf16[8,128,128]{2,1,0:T(8,128)(2,1)}) custom-call(s32[36]{0:T(128)} %concatenate.16.info_ref, bf16[16,256,128]{2,1,0:T(8,128)(2,1)} %copy-done.44, bf16[16,64,256]{2,1,0:T(8,128)(2,1)} %copy-done.45, bf16[8,256,128]{2,1,0:T(8,128)(2,1)} %copy-done.46, ...), custom_call_target="tpu_custom_call" | custom-call | flops 3355443200 | bytes 5242880 | tf_op jit(solution)/shard_map/attend_back/pallas_call | solution.py:660
  186.7 4.2 %all-to-all-start.4 = ((bf16[8,384,128]{2,1,0:T(8,128)(2,1)}), bf16[8,384,128]{2,1,0:T(8,128)(2,1)}, u32[]{:S(2)}, u32[]{:S(2)}) async-start(bf16[8,384,128]{2,1,0:T(8,128)(2,1)} %combine.1.own_ref), calls=%async_computation.4 | async-start | bytes 1572864 | tf_op jit(solution)/shard_map/all_to_all | solution.py:1235
  200.5 7.5 %head_grad.1 = bf16[8,96,128]{2,1,0:T(8,128)(2,1)} custom-call(s32[36]{0:T(128)S(1)} %copy-done.40, bf16[4096,1024]{1,0:T(8,128)(2,1)} %all-gather.3.cloned.1.call-done.tok_ref, bf16[8,384,128]{2,1,0:T(8,128)(2,1)} %combine.1.own_ref, bf16[8,384,128]{2,1,0:T(8,128)(2,1)} %collective-permute-done.13.sib_ref), custom_call_target="tpu_custom_call" | custom-call | flops 1610612736 | bytes 8388608 | tf_op jit(solution)/shard_map/head_grad/pallas_call | solution.py:835
  208.1 8.3 %all-to-all-done.4.in_ref = bf16[8,384,128]{2,1,0:T(8,128)(2,1)} async-done(((bf16[8,384,128]{2,1,0:T(8,128)(2,1)}), bf16[8,384,128]{2,1,0:T(8,128)(2,1)}, u32[]{:S(2)}, u32[]{:S(2)}) %all-to-all-start.4) | async-done | bytes 786464 | tf_op jit(solution)/shard_map/all_to_all | solution.py:1235
  222.3 3.9 %collective-permute-start.18 = (f32[16,512]{1,0:T(8,128)S(1)}, f32[16,512]{1,0:T(8,128)S(1)}, u32[]{:S(2)}, u32[]{:S(2)}) collective-permute-start(f32[16,512]{1,0:T(8,128)S(1)} %add.99), channel_id=1, source_target_pairs={{0,8},{2,10},{4,12},{6,14},{8,0},{10,2},{12,4},{14,6},{16,24},{18,... | collective-permute-start | bytes 98312 | tf_op jit(solution)/shard_map/ppermute | solution.py:323
  233.3 5.0 %all-to-all-start.5 = ((bf16[8,96,128]{2,1,0:T(8,128)(2,1)}), bf16[8,96,128]{2,1,0:T(8,128)(2,1)S(1)}, u32[]{:S(2)}, u32[]{:S(2)}) async-start(bf16[8,96,128]{2,1,0:T(8,128)(2,1)} %head_grad.1), calls=%async_computation.6 | async-start | bytes 393216 | tf_op jit(solution)/shard_map/all_to_all | solution.py:1235
  244.5 4.6 %collective-permute-done.22.came_ref = bf16[2,256,128]{2,1,0:T(8,128)(2,1)S(1)} collective-permute-done((bf16[2,256,128]{2,1,0:T(8,128)(2,1)S(1)}, bf16[2,256,128]{2,1,0:T(8,128)(2,1)S(1)}, u32[]{:S(2)}, u32[]{:S(2)}) %collective-permute-start.22) | collective-permute-done | bytes 131104 | tf_op jit(solution)/shard_map/ppermute | solution.py:323
  255.9 4.2 %widen.1 = f32[1024,1024]{1,0:T(8,128)} custom-call(bf16[1024,1024]{1,0:T(8,128)(2,1)} %all-gather.5.cloned.1.call-done.in_ref), custom_call_target="tpu_custom_call" | custom-call | flops 1048576 | bytes 6291456 | tf_op jit(solution)/shard_map/widen/pallas_call | solution.py:1042
  (261 shorter events, 101.6 us)
Async XLA Ops:
  7.2 14.1 %collective-permute-start = (bf16[128,1024]{1,0:T(8,128)(2,1)}, bf16[128,1024]{1,0:T(8,128)(2,1)S(1)}, u32[]{:S(2)}, u32[]{:S(2)}) collective-permute-start(bf16[128,1024]{1,0:T(8,128)(2,1)} %x_ref.1), channel_id=1, source_target_pairs={{0,1},{1,0},{2,3},{3,2},{4,5},{5,4},{6,7},{7,6},{8,9},{9,8},{10,11... | collective-permute-start | bytes 786440 | tf_op jit(solution)/shard_map/ppermute | solution.py:323
  13.6 18.6 %all-to-all-start = ((bf16[8,192,128]{2,1,0:T(8,128)(2,1)}), bf16[8,192,128]{2,1,0:T(8,128)(2,1)S(1)}, u32[]{:S(2)}, u32[]{:S(2)}) async-start(bf16[8,192,128]{2,1,0:T(8,128)(2,1)} %project.2), calls=%async_computation | async-start | bytes 786432 | tf_op jit(solution)/shard_map/all_to_all | solution.py:1235
  21.3 17.1 %collective-permute-start.2 = (bf16[256,1024]{1,0:T(8,128)(2,1)S(1)}, bf16[256,1024]{1,0:T(8,128)(2,1)S(1)}, u32[]{:S(2)}, u32[]{:S(2)}) collective-permute-start(bf16[256,1024]{1,0:T(8,128)(2,1)S(1)} %constant_dynamic-slice_fusion), channel_id=1, source_target_pairs={{0,1},{1,0},{2,3},{3,2},{4,5},{5,4},{6,7},{7,6},{8,9},{9,8},{10,11... | collective-permute-start | bytes 1572872 | tf_op jit(solution)/shard_map/ppermute | solution.py:323
  32.2 16.7 %all-to-all-start.1 = ((bf16[8,192,128]{2,1,0:T(8,128)(2,1)}), bf16[8,192,128]{2,1,0:T(8,128)(2,1)S(1)}, u32[]{:S(2)}, u32[]{:S(2)}) async-start(bf16[8,192,128]{2,1,0:T(8,128)(2,1)} %project.3), calls=%async_computation.1 | async-start | bytes 786432 | tf_op jit(solution)/shard_map/all_to_all | solution.py:1235
  38.3 162.2 %all-gather.3.cloned.1.call-start = ((), (), s32[]{:S(2)}) async-start(), calls=%async_computation.7 | async-start | bytes 8912896 | tf_op jit(solution)/shard_map/all_gather | solution.py:1307
  48.9 35.9 %collective-permute-start.5 = (bf16[256,1024]{1,0:T(8,128)(2,1)}, bf16[256,1024]{1,0:T(8,128)(2,1)}, u32[]{:S(2)}, u32[]{:S(2)}) collective-permute-start(bf16[256,1024]{1,0:T(8,128)(2,1)} %pad_maximum_fusion), channel_id=1, source_target_pairs={{0,1},{1,0},{2,3},{3,2},{4,5},{5,4},{6,7},{7,6},{8,9},{9,8},{10,11... | collective-permute-start | bytes 1572872 | tf_op jit(solution)/shard_map/ppermute | solution.py:323
  50.5 29.2 %collective-permute-start.6 = (bf16[128,1024]{1,0:T(8,128)(2,1)}, bf16[128,1024]{1,0:T(8,128)(2,1)S(1)}, u32[]{:S(2)}, u32[]{:S(2)}) collective-permute-start(bf16[128,1024]{1,0:T(8,128)(2,1)} %param.32), channel_id=1, source_target_pairs={{0,1},{1,0},{2,3},{3,2},{4,5},{5,4},{6,7},{7,6},{8,9},{9,8},{10,11... | collective-permute-start | bytes 786440 | tf_op jit(solution)/shard_map/ppermute | solution.py:323
  75.6 17.3 %all-to-all-start.2 = ((bf16[8,128,128]{2,1,0:T(8,128)(2,1)}), bf16[8,128,128]{2,1,0:T(8,128)(2,1)S(1)}, u32[]{:S(2)}, u32[]{:S(2)}) async-start(bf16[8,128,128]{2,1,0:T(8,128)(2,1)} %get-tuple-element.114), calls=%async_computation.2 | async-start | bytes 524288 | tf_op jit(solution)/shard_map/all_to_all | solution.py:1235
  79.5 136.9 %reduce-scatter.2.cloned.1.call-start = ((), (), s32[]{:S(2)}) async-start(), calls=%async_computation.8 | async-start | bytes 11141120 | tf_op jit(solution)/shard_map/reduce_scatter | solution.py:1380
  92.9 6.6 %collective-permute-start.7 = (bf16[8,128,128]{2,1,0:T(8,128)(2,1)S(1)}, bf16[8,128,128]{2,1,0:T(8,128)(2,1)S(1)}, u32[]{:S(2)}, u32[]{:S(2)}) collective-permute-start(bf16[8,128,128]{2,1,0:T(8,128)(2,1)S(1)} %all-to-all-done.2.in_ref), channel_id=1, source_target_pairs={{0,1},{1,0},{2,3},{3,2},{4,5},{5,4},{6,7},{7,6},{8,9},{9,8},{10,11... | collective-permute-start | bytes 786440 | tf_op jit(solution)/shard_map/ppermute | solution.py:323
  108.1 9.0 %collective-permute-start.8 = (bf16[128,1024]{1,0:T(8,128)(2,1)S(1)}, bf16[128,1024]{1,0:T(8,128)(2,1)S(1)}, u32[]{:S(2)}, u32[]{:S(2)}) collective-permute-start(bf16[128,1024]{1,0:T(8,128)(2,1)S(1)} %convolution_convert_fusion.3.own_ref), channel_id=1, source_target_pairs={{0,1},{1,0},{2,3},{3,2},{4,5},{5,4},{6,7},{7,6},{8,9},{9,8},{10,11... | collective-permute-start | bytes 786440 | tf_op jit(solution)/shard_map/ppermute | solution.py:323
  111.7 9.7 %collective-permute-start.9 = (bf16[128,1024]{1,0:T(8,128)(2,1)S(1)}, bf16[128,1024]{1,0:T(8,128)(2,1)S(1)}, u32[]{:S(2)}, u32[]{:S(2)}) collective-permute-start(bf16[128,1024]{1,0:T(8,128)(2,1)S(1)} %convolution_convert_fusion.2.own_ref), channel_id=1, source_target_pairs={{0,1},{1,0},{2,3},{3,2},{4,5},{5,4},{6,7},{7,6},{8,9},{9,8},{10,11... | collective-permute-start | bytes 786440 | tf_op jit(solution)/shard_map/ppermute | solution.py:323
  142.4 7.5 %collective-permute-start.11 = (bf16[128,1024]{1,0:T(8,128)(2,1)S(1)}, bf16[128,1024]{1,0:T(8,128)(2,1)S(1)}, u32[]{:S(2)}, u32[]{:S(2)}) collective-permute-start(bf16[128,1024]{1,0:T(8,128)(2,1)S(1)} %convolution_convert_fusion.own_ref), channel_id=1, source_target_pairs={{0,1},{1,0},{2,3},{3,2},{4,5},{5,4},{6,7},{7,6},{8,9},{9,8},{10,11... | collective-permute-start | bytes 786440 | tf_op jit(solution)/shard_map/ppermute | solution.py:323
  143.9 8.7 %collective-permute-start.10 = (bf16[128,1024]{1,0:T(8,128)(2,1)S(1)}, bf16[128,1024]{1,0:T(8,128)(2,1)S(1)}, u32[]{:S(2)}, u32[]{:S(2)}) collective-permute-start(bf16[128,1024]{1,0:T(8,128)(2,1)S(1)} %convolution_convert_fusion.1.own_ref), channel_id=1, source_target_pairs={{0,1},{1,0},{2,3},{3,2},{4,5},{5,4},{6,7},{7,6},{8,9},{9,8},{10,11... | collective-permute-start | bytes 786440 | tf_op jit(solution)/shard_map/ppermute | solution.py:323
  155.1 13.7 %all-to-all-start.3 = ((bf16[8,128,128]{2,1,0:T(8,128)(2,1)}), bf16[8,128,128]{2,1,0:T(8,128)(2,1)S(1)}, u32[]{:S(2)}, u32[]{:S(2)}) async-start(bf16[8,128,128]{2,1,0:T(8,128)(2,1)} %ctx_grad.1), calls=%async_computation.3 | async-start | bytes 524288 | tf_op jit(solution)/shard_map/all_to_all | solution.py:1235
  186.7 29.7 %all-to-all-start.4 = ((bf16[8,384,128]{2,1,0:T(8,128)(2,1)}), bf16[8,384,128]{2,1,0:T(8,128)(2,1)}, u32[]{:S(2)}, u32[]{:S(2)}) async-start(bf16[8,384,128]{2,1,0:T(8,128)(2,1)} %combine.1.own_ref), calls=%async_computation.4 | async-start | bytes 1572864 | tf_op jit(solution)/shard_map/all_to_all | solution.py:1235
  190.9 64.9 %all-gather.5.cloned.1.call-start = ((), (), s32[]{:S(2)}) async-start(), calls=%async_computation.9 | async-start | bytes 2228224 | tf_op jit(solution)/shard_map/all_gather | solution.py:1425
  191.0 9.5 %collective-permute-start.13 = (bf16[8,384,128]{2,1,0:T(8,128)(2,1)}, bf16[8,384,128]{2,1,0:T(8,128)(2,1)}, u32[]{:S(2)}, u32[]{:S(2)}) collective-permute-start(bf16[8,384,128]{2,1,0:T(8,128)(2,1)} %combine.1.own_ref), channel_id=1, source_target_pairs={{0,2},{2,0},{4,6},{6,4},{8,10},{10,8},{12,14},{14,12},{16,18},{18,... | collective-permute-start | bytes 2359304 | tf_op jit(solution)/shard_map/ppermute | solution.py:323
  219.6 18.7 %collective-permute-start.21 = (bf16[4,256,128]{2,1,0:T(8,128)(2,1)}, bf16[4,256,128]{2,1,0:T(8,128)(2,1)}, u32[]{:S(2)}, u32[]{:S(2)}) collective-permute-start(bf16[4,256,128]{2,1,0:T(8,128)(2,1)} %copy-done.51), channel_id=1, source_target_pairs={{0,4},{2,6},{4,0},{6,2},{8,12},{10,14},{12,8},{14,10},{16,20},{18,... | collective-permute-start | bytes 786440 | tf_op jit(solution)/shard_map/ppermute | solution.py:323
  222.3 9.2 %collective-permute-start.18 = (f32[16,512]{1,0:T(8,128)S(1)}, f32[16,512]{1,0:T(8,128)S(1)}, u32[]{:S(2)}, u32[]{:S(2)}) collective-permute-start(f32[16,512]{1,0:T(8,128)S(1)} %add.99), channel_id=1, source_target_pairs={{0,8},{2,10},{4,12},{6,14},{8,0},{10,2},{12,4},{14,6},{16,24},{18,... | collective-permute-start | bytes 98312 | tf_op jit(solution)/shard_map/ppermute | solution.py:323
  229.9 8.4 %collective-permute-start.20 = (bf16[128,1024]{1,0:T(8,128)(2,1)}, bf16[128,1024]{1,0:T(8,128)(2,1)S(1)}, u32[]{:S(2)}, u32[]{:S(2)}) collective-permute-start(bf16[128,1024]{1,0:T(8,128)(2,1)} %get-tuple-element.188), channel_id=1, source_target_pairs={{0,1},{1,0},{2,3},{3,2},{4,5},{5,4},{6,7},{7,6},{8,9},{9,8},{10,11... | collective-permute-start | bytes 786440 | tf_op jit(solution)/shard_map/ppermute | solution.py:323
  231.6 6.6 %collective-permute-start.19 = (f32[16,512]{1,0:T(8,128)S(1)}, f32[16,512]{1,0:T(8,128)S(1)}, u32[]{:S(2)}, u32[]{:S(2)}) collective-permute-start(f32[16,512]{1,0:T(8,128)S(1)} %add.100), channel_id=1, source_target_pairs={{0,16},{2,18},{4,20},{6,22},{8,24},{10,26},{12,28},{14,30},{16,0},... | collective-permute-start | bytes 98312 | tf_op jit(solution)/shard_map/ppermute | solution.py:323
  233.3 19.8 %all-to-all-start.5 = ((bf16[8,96,128]{2,1,0:T(8,128)(2,1)}), bf16[8,96,128]{2,1,0:T(8,128)(2,1)S(1)}, u32[]{:S(2)}, u32[]{:S(2)}) async-start(bf16[8,96,128]{2,1,0:T(8,128)(2,1)} %head_grad.1), calls=%async_computation.6 | async-start | bytes 393216 | tf_op jit(solution)/shard_map/all_to_all | solution.py:1235
  239.3 9.8 %collective-permute-start.22 = (bf16[2,256,128]{2,1,0:T(8,128)(2,1)S(1)}, bf16[2,256,128]{2,1,0:T(8,128)(2,1)S(1)}, u32[]{:S(2)}, u32[]{:S(2)}) collective-permute-start(bf16[2,256,128]{2,1,0:T(8,128)(2,1)S(1)} %get-tuple-element.197), channel_id=1, source_target_pairs={{0,8},{2,10},{4,12},{6,14},{8,0},{10,2},{12,4},{14,6},{16,24},{18,... | collective-permute-start | bytes 393224 | tf_op jit(solution)/shard_map/ppermute | solution.py:323
  (80 other events, 650.0 us)
Sparse Core Ops, SparseCore 0:
  49.0 52.9 all-gather.2
  136.0 70.1 reduce-scatter.1
  218.1 36.7 all-gather.4

commit v5 on v4

--- a/solution.py
+++ b/solution.py
@@ -1037,7 +1037,7 @@
 
 def widen(values):
     rows, width = values.shape
-    steps = 4
+    steps = 2
     block = pl.BlockSpec((rows // steps, width), lambda i: (i, 0))
     return pl.pallas_call(
         widen_body,

time: 268 us -> 269 us (level)
  waiting for transfers between devices: 57.4 us -> 60.9 us
  starting transfers between devices: 53.7 us -> 50.9 us
    ppermute x24, waiting for transfers between devices: 31.8 us -> 35.6 us  [swap_over(): lax.ppermute(value, axis, [(index, index ^ mask) for index in range(count)])]
  transfers between devices with their start and end apart: 33 -> 33, of which waited for: 15 -> 15; matrix products, arithmetic and copies ran while one was open for 16% -> 16% of each run, Pallas kernels for 28% -> 29%
where the time goes in v5:
time: 269 us; the launch traced here: 267 us
  Pallas kernels  80.3 us (30%)
  waiting for transfers between devices  60.9 us (23%)
  starting transfers between devices  50.9 us (19%)
  local copies, waits for them, and re-layouts  26.1 us (10%)
  matrix products  22 us (8%)
  between operations  16 us (6%)
  other arithmetic  11.2 us (4%)
    ppermute x24, waiting for transfers between devices, swap_over(): lax.ppermute(value, axis, [(index, index ^ mask) for index in range(count)])  35.6 us
    all_to_all x6, starting transfers between devices, to_heads(): lax.all_to_all(value, 'pass', 0, 0, axis_index_groups=same_core, tiled=True)  27.5 us
    all_to_all x6, waiting for transfers between devices, to_heads(): lax.all_to_all(value, 'pass', 0, 0, axis_index_groups=same_core, tiled=True)  25.3 us
    ppermute x24, starting transfers between devices, swap_over(): lax.ppermute(value, axis, [(index, index ^ mask) for index in range(count)])  23.1 us
    pallas_call x1, Pallas kernels, attend(): pl.pallas_call(attend_body, in_specs=[pl.BlockSpec(memory_space=pltpu.SME...  23 us
    unnamed x150, local copies, waits for them, and re-layouts  22 us
    pallas_call x1, Pallas kernels, attend_back(): pl.pallas_call(attend_back_body, in_specs=[pl.BlockSpec(memory_space=pltp...  12.7 us
    dot_general x4, matrix products, contract_cols(): lax.dot_general(left, right, (((1,), (1,)), ((), ())), preferred_element_...  10 us
  transfers between devices with their start and end apart: 33, of which 15 were waited for; matrix products, arithmetic and copies ran while one was open for 16% of the time, Pallas kernels for 29%

profile of v5, /device:TPU:0, one launch (start us, length us, event | category | flops | bytes accessed | tf_op | source)
XLA Modules:
  0.0 267.5 jit_solution(16893629051366731530)
XLA Ops:
  10.2 3.4 %project.2 = bf16[8,192,128]{2,1,0:T(8,128)(2,1)} custom-call(bf16[128,1024]{1,0:T(8,128)(2,1)} %x_ref.1, bf16[1024,512]{1,0:T(8,128)(2,1)} %wq_ref.5, bf16[1024,512]{1,0:T(8,128)(2,1)} %wk_ref.5, bf16[1024,512]{1,0:T(8,128)(2,1)} %wv_ref.5), custom_call_target="tpu_custom_call" | custom-call | flops 402653184 | bytes 4194304 | tf_op jit(solution)/shard_map/project/pallas_call | solution.py:386
  13.6 5.8 %all-to-all-start = ((bf16[8,192,128]{2,1,0:T(8,128)(2,1)}), bf16[8,192,128]{2,1,0:T(8,128)(2,1)S(1)}, u32[]{:S(2)}, u32[]{:S(2)}) async-start(bf16[8,192,128]{2,1,0:T(8,128)(2,1)} %project.2), calls=%async_computation | async-start | bytes 786432 | tf_op jit(solution)/shard_map/all_to_all | solution.py:1235
  24.6 3.9 %copy.37 = bf16[1024,1024]{0,1:T(8,128)(2,1)} copy(bf16[1024,1024]{1,0:T(8,128)(2,1)} %param.29) | data formatting | bytes 4194304 | tf_op args[12]
  28.8 3.4 %project.3 = bf16[8,192,128]{2,1,0:T(8,128)(2,1)} custom-call(bf16[128,1024]{1,0:T(8,128)(2,1)} %copy-done.63, bf16[1024,512]{1,0:T(8,128)(2,1)} %wq_ref.5, bf16[1024,512]{1,0:T(8,128)(2,1)} %wk_ref.5, bf16[1024,512]{1,0:T(8,128)(2,1)} %wv_ref.5), custom_call_target="tpu_custom_call" | custom-call | flops 402653184 | bytes 4194304 | tf_op jit(solution)/shard_map/project/pallas_call | solution.py:386
  32.2 6.1 %all-to-all-start.1 = ((bf16[8,192,128]{2,1,0:T(8,128)(2,1)}), bf16[8,192,128]{2,1,0:T(8,128)(2,1)S(1)}, u32[]{:S(2)}, u32[]{:S(2)}) async-start(bf16[8,192,128]{2,1,0:T(8,128)(2,1)} %project.3), calls=%async_computation.1 | async-start | bytes 786432 | tf_op jit(solution)/shard_map/all_to_all | solution.py:1235
  44.6 4.3 %all-to-all-done.1.far_ref = bf16[8,192,128]{2,1,0:T(8,128)(2,1)S(1)} async-done(((bf16[8,192,128]{2,1,0:T(8,128)(2,1)}), bf16[8,192,128]{2,1,0:T(8,128)(2,1)S(1)}, u32[]{:S(2)}, u32[]{:S(2)}) %all-to-all-start.1) | async-done | bytes 393248 | tf_op jit(solution)/shard_map/all_to_all | solution.py:1235
  53.0 23.0 %attend.1 = (bf16[8,128,128]{2,1,0:T(8,128)(2,1)}, f32[8,64,256]{2,1,0:T(8,128)}, f32[8,8,256]{2,1,0:T(8,128)}) custom-call(s32[36]{0:T(128)} %concatenate.16.info_ref, bf16[8,192,128]{2,1,0:T(8,128)(2,1)} %copy-done.7, bf16[8,192,128]{2,1,0:T(8,128)(2,1)} %copy-done.9, bf16[8,192,128]{2,1,0:T(8,128)(2,1)} %copy-done.24, bf16[8,192,128]{2,1,0:T(8,128)(2,1)} %copy-done.26), custom_call_target="tpu_custom_call" | custom-call | flops 1342177280 | bytes 4194304 | tf_op jit(solution)/shard_map/attend/pallas_call | solution.py:534
  76.0 3.8 %all-to-all-start.2 = ((bf16[8,128,128]{2,1,0:T(8,128)(2,1)}), bf16[8,128,128]{2,1,0:T(8,128)(2,1)S(1)}, u32[]{:S(2)}, u32[]{:S(2)}) async-start(bf16[8,128,128]{2,1,0:T(8,128)(2,1)} %get-tuple-element.114), calls=%async_computation.2 | async-start | bytes 524288 | tf_op jit(solution)/shard_map/all_to_all | solution.py:1235
  88.3 4.9 %all-to-all-done.2.in_ref = bf16[8,128,128]{2,1,0:T(8,128)(2,1)S(1)} async-done(((bf16[8,128,128]{2,1,0:T(8,128)(2,1)}), bf16[8,128,128]{2,1,0:T(8,128)(2,1)S(1)}, u32[]{:S(2)}, u32[]{:S(2)}) %all-to-all-start.2) | async-done | bytes 262176 | tf_op jit(solution)/shard_map/all_to_all | solution.py:1235
  94.3 7.5 %collective-permute-done.7.other_ref = bf16[8,128,128]{2,1,0:T(8,128)(2,1)S(1)} collective-permute-done((bf16[8,128,128]{2,1,0:T(8,128)(2,1)S(1)}, bf16[8,128,128]{2,1,0:T(8,128)(2,1)S(1)}, u32[]{:S(2)}, u32[]{:S(2)}) %collective-permute-start.7) | collective-permute-done | bytes 262176 | tf_op jit(solution)/shard_map/ppermute | solution.py:323
  105.6 4.0 %fusion.17 = (f32[128,2048]{1,0:T(8,128)S(1)}, bf16[128,2048]{1,0:T(8,128)(2,1)S(1)}) fusion(bf16[128,1024]{1,0:T(8,128)(2,1)S(1)} %get-tuple-element.129.refs_1_, bf16[1024,2048]{1,0:T(8,128)(2,1)} %param.24), kind=kOutput, calls=%fused_computation.24 | convolution fusion | flops 539492352 | bytes 6029312 | tf_op jit(solution)/shard_map/dot_general | solution.py:344
  114.5 5.2 %collective-permute-done.8.recv_ref = bf16[128,1024]{1,0:T(8,128)(2,1)S(1)} collective-permute-done((bf16[128,1024]{1,0:T(8,128)(2,1)S(1)}, bf16[128,1024]{1,0:T(8,128)(2,1)S(1)}, u32[]{:S(2)}, u32[]{:S(2)}) %collective-permute-start.8) | collective-permute-done | bytes 262176 | tf_op jit(solution)/shard_map/ppermute | solution.py:323
  129.2 9.2 %late_grad.1 = bf16[1024,5120]{1,0:T(8,128)(2,1)} custom-call(s32[1]{0:T(128)} %bitcast.9.first_ref, bf16[128,1024]{1,0:T(8,128)(2,1)} %copy-done.28, bf16[128,1024]{1,0:T(8,128)(2,1)} %copy-done.29, bf16[128,2048]{1,0:T(8,128)(2,1)} %fusion.2.refs_2_, bf16[128,2048]{1,0:T(8,128)(2,1)} %fusion.3.refs_3_, bf16[128,1024]{1,0:T(8,128)(2,1)} %copy-done.11, ...), custom_call_target="tpu_custom_call" | custom-call | flops 2684354560 | bytes 13631488 | tf_op jit(solution)/shard_map/late_grad/pallas_call | solution.py:996
  139.5 3.8 %convolution_convert_fusion.1.own_ref = bf16[128,1024]{1,0:T(8,128)(2,1)S(1)} fusion(bf16[128,2048]{1,0:T(8,128)(2,1)S(1)} %copy-done.58, bf16[1024,2048]{1,0:T(8,128)(2,1)} %param.24), kind=kOutput, calls=%fused_computation.14 | convolution fusion | flops 537001984 | bytes 4980736 | tf_op jit(solution)/shard_map/dot_general | solution.py:68
  147.0 7.2 %collective-permute-done.11.recv_ref = bf16[128,1024]{1,0:T(8,128)(2,1)S(1)} collective-permute-done((bf16[128,1024]{1,0:T(8,128)(2,1)S(1)}, bf16[128,1024]{1,0:T(8,128)(2,1)S(1)}, u32[]{:S(2)}, u32[]{:S(2)}) %collective-permute-start.11) | collective-permute-done | bytes 262176 | tf_op jit(solution)/shard_map/ppermute | solution.py:323
  159.9 3.4 %all-to-all-start.3 = ((bf16[8,128,128]{2,1,0:T(8,128)(2,1)}), bf16[8,128,128]{2,1,0:T(8,128)(2,1)S(1)}, u32[]{:S(2)}, u32[]{:S(2)}) async-start(bf16[8,128,128]{2,1,0:T(8,128)(2,1)} %ctx_grad.1), calls=%async_computation.3 | async-start | bytes 524288 | tf_op jit(solution)/shard_map/all_to_all | solution.py:1235
  165.4 8.5 %all-to-all-done.3.dctx_ref = bf16[8,128,128]{2,1,0:T(8,128)(2,1)S(1)} async-done(((bf16[8,128,128]{2,1,0:T(8,128)(2,1)}), bf16[8,128,128]{2,1,0:T(8,128)(2,1)S(1)}, u32[]{:S(2)}, u32[]{:S(2)}) %all-to-all-start.3) | async-done | bytes 262176 | tf_op jit(solution)/shard_map/all_to_all | solution.py:1235
  174.6 12.7 %attend_back.1 = (bf16[8,256,128]{2,1,0:T(8,128)(2,1)}, bf16[8,256,128]{2,1,0:T(8,128)(2,1)}, bf16[8,128,128]{2,1,0:T(8,128)(2,1)}) custom-call(s32[36]{0:T(128)} %concatenate.16.info_ref, bf16[16,256,128]{2,1,0:T(8,128)(2,1)} %copy-done.44, bf16[16,64,256]{2,1,0:T(8,128)(2,1)} %copy-done.45, bf16[8,256,128]{2,1,0:T(8,128)(2,1)} %copy-done.46, ...), custom_call_target="tpu_custom_call" | custom-call | flops 3355443200 | bytes 5242880 | tf_op jit(solution)/shard_map/attend_back/pallas_call | solution.py:660
  192.6 4.2 %all-to-all-start.4 = ((bf16[8,384,128]{2,1,0:T(8,128)(2,1)}), bf16[8,384,128]{2,1,0:T(8,128)(2,1)}, u32[]{:S(2)}, u32[]{:S(2)}) async-start(bf16[8,384,128]{2,1,0:T(8,128)(2,1)} %combine.1.own_ref), calls=%async_computation.4 | async-start | bytes 1572864 | tf_op jit(solution)/shard_map/all_to_all | solution.py:1235
  206.4 7.4 %head_grad.1 = bf16[8,96,128]{2,1,0:T(8,128)(2,1)} custom-call(s32[36]{0:T(128)S(1)} %copy-done.40, bf16[4096,1024]{1,0:T(8,128)(2,1)} %all-gather.3.cloned.1.call-done.tok_ref, bf16[8,384,128]{2,1,0:T(8,128)(2,1)} %combine.1.own_ref, bf16[8,384,128]{2,1,0:T(8,128)(2,1)} %collective-permute-done.13.sib_ref), custom_call_target="tpu_custom_call" | custom-call | flops 1610612736 | bytes 8388608 | tf_op jit(solution)/shard_map/head_grad/pallas_call | solution.py:835
  213.8 7.6 %all-to-all-done.4.in_ref = bf16[8,384,128]{2,1,0:T(8,128)(2,1)} async-done(((bf16[8,384,128]{2,1,0:T(8,128)(2,1)}), bf16[8,384,128]{2,1,0:T(8,128)(2,1)}, u32[]{:S(2)}, u32[]{:S(2)}) %all-to-all-start.4) | async-done | bytes 786464 | tf_op jit(solution)/shard_map/all_to_all | solution.py:1235
  235.8 4.1 %all-to-all-start.5 = ((bf16[8,96,128]{2,1,0:T(8,128)(2,1)}), bf16[8,96,128]{2,1,0:T(8,128)(2,1)S(1)}, u32[]{:S(2)}, u32[]{:S(2)}) async-start(bf16[8,96,128]{2,1,0:T(8,128)(2,1)} %head_grad.1), calls=%async_computation.6 | async-start | bytes 393216 | tf_op jit(solution)/shard_map/all_to_all | solution.py:1235
  246.2 4.6 %collective-permute-done.22.came_ref = bf16[2,256,128]{2,1,0:T(8,128)(2,1)S(1)} collective-permute-done((bf16[2,256,128]{2,1,0:T(8,128)(2,1)S(1)}, bf16[2,256,128]{2,1,0:T(8,128)(2,1)S(1)}, u32[]{:S(2)}, u32[]{:S(2)}) %collective-permute-start.22) | collective-permute-done | bytes 131104 | tf_op jit(solution)/shard_map/ppermute | solution.py:323
  257.6 3.4 %widen.1 = f32[1024,1024]{1,0:T(8,128)} custom-call(bf16[1024,1024]{1,0:T(8,128)(2,1)} %all-gather.5.cloned.1.call-done.in_ref), custom_call_target="tpu_custom_call" | custom-call | flops 1048576 | bytes 6291456 | tf_op jit(solution)/shard_map/widen/pallas_call | solution.py:1042
  (261 shorter events, 99.9 us)
Async XLA Ops:
  7.2 14.1 %collective-permute-start = (bf16[128,1024]{1,0:T(8,128)(2,1)}, bf16[128,1024]{1,0:T(8,128)(2,1)S(1)}, u32[]{:S(2)}, u32[]{:S(2)}) collective-permute-start(bf16[128,1024]{1,0:T(8,128)(2,1)} %x_ref.1), channel_id=1, source_target_pairs={{0,1},{1,0},{2,3},{3,2},{4,5},{5,4},{6,7},{7,6},{8,9},{9,8},{10,11... | collective-permute-start | bytes 786440 | tf_op jit(solution)/shard_map/ppermute | solution.py:323
  13.6 18.6 %all-to-all-start = ((bf16[8,192,128]{2,1,0:T(8,128)(2,1)}), bf16[8,192,128]{2,1,0:T(8,128)(2,1)S(1)}, u32[]{:S(2)}, u32[]{:S(2)}) async-start(bf16[8,192,128]{2,1,0:T(8,128)(2,1)} %project.2), calls=%async_computation | async-start | bytes 786432 | tf_op jit(solution)/shard_map/all_to_all | solution.py:1235
  21.3 17.1 %collective-permute-start.2 = (bf16[256,1024]{1,0:T(8,128)(2,1)S(1)}, bf16[256,1024]{1,0:T(8,128)(2,1)S(1)}, u32[]{:S(2)}, u32[]{:S(2)}) collective-permute-start(bf16[256,1024]{1,0:T(8,128)(2,1)S(1)} %constant_dynamic-slice_fusion), channel_id=1, source_target_pairs={{0,1},{1,0},{2,3},{3,2},{4,5},{5,4},{6,7},{7,6},{8,9},{9,8},{10,11... | collective-permute-start | bytes 1572872 | tf_op jit(solution)/shard_map/ppermute | solution.py:323
  32.2 16.7 %all-to-all-start.1 = ((bf16[8,192,128]{2,1,0:T(8,128)(2,1)}), bf16[8,192,128]{2,1,0:T(8,128)(2,1)S(1)}, u32[]{:S(2)}, u32[]{:S(2)}) async-start(bf16[8,192,128]{2,1,0:T(8,128)(2,1)} %project.3), calls=%async_computation.1 | async-start | bytes 786432 | tf_op jit(solution)/shard_map/all_to_all | solution.py:1235
  38.3 168.1 %all-gather.3.cloned.1.call-start = ((), (), s32[]{:S(2)}) async-start(), calls=%async_computation.7 | async-start | bytes 8912896 | tf_op jit(solution)/shard_map/all_gather | solution.py:1307
  38.4 5.4 %collective-permute-start.3 = (bf16[256,1024]{1,0:T(8,128)(2,1)S(1)}, bf16[256,1024]{1,0:T(8,128)(2,1)S(1)}, u32[]{:S(2)}, u32[]{:S(2)}) collective-permute-start(bf16[256,1024]{1,0:T(8,128)(2,1)S(1)} %collective-permute-done.2.w_mine_ref), channel_id=1, source_target_pairs={{0,2},{2,0},{4,6},{6,4},{8,10},{10,8},{12,14},{14,12},{16,18},{18,... | collective-permute-start | bytes 1572872 | tf_op jit(solution)/shard_map/ppermute | solution.py:323
  48.9 36.3 %collective-permute-start.5 = (bf16[256,1024]{1,0:T(8,128)(2,1)}, bf16[256,1024]{1,0:T(8,128)(2,1)}, u32[]{:S(2)}, u32[]{:S(2)}) collective-permute-start(bf16[256,1024]{1,0:T(8,128)(2,1)} %pad_maximum_fusion), channel_id=1, source_target_pairs={{0,1},{1,0},{2,3},{3,2},{4,5},{5,4},{6,7},{7,6},{8,9},{9,8},{10,11... | collective-permute-start | bytes 1572872 | tf_op jit(solution)/shard_map/ppermute | solution.py:323
  50.5 29.6 %collective-permute-start.6 = (bf16[128,1024]{1,0:T(8,128)(2,1)}, bf16[128,1024]{1,0:T(8,128)(2,1)S(1)}, u32[]{:S(2)}, u32[]{:S(2)}) collective-permute-start(bf16[128,1024]{1,0:T(8,128)(2,1)} %param.32), channel_id=1, source_target_pairs={{0,1},{1,0},{2,3},{3,2},{4,5},{5,4},{6,7},{7,6},{8,9},{9,8},{10,11... | collective-permute-start | bytes 786440 | tf_op jit(solution)/shard_map/ppermute | solution.py:323
  76.0 17.2 %all-to-all-start.2 = ((bf16[8,128,128]{2,1,0:T(8,128)(2,1)}), bf16[8,128,128]{2,1,0:T(8,128)(2,1)S(1)}, u32[]{:S(2)}, u32[]{:S(2)}) async-start(bf16[8,128,128]{2,1,0:T(8,128)(2,1)} %get-tuple-element.114), calls=%async_computation.2 | async-start | bytes 524288 | tf_op jit(solution)/shard_map/all_to_all | solution.py:1235
  79.9 141.6 %reduce-scatter.2.cloned.1.call-start = ((), (), s32[]{:S(2)}) async-start(), calls=%async_computation.8 | async-start | bytes 11141120 | tf_op jit(solution)/shard_map/reduce_scatter | solution.py:1380
  93.2 8.6 %collective-permute-start.7 = (bf16[8,128,128]{2,1,0:T(8,128)(2,1)S(1)}, bf16[8,128,128]{2,1,0:T(8,128)(2,1)S(1)}, u32[]{:S(2)}, u32[]{:S(2)}) collective-permute-start(bf16[8,128,128]{2,1,0:T(8,128)(2,1)S(1)} %all-to-all-done.2.in_ref), channel_id=1, source_target_pairs={{0,1},{1,0},{2,3},{3,2},{4,5},{5,4},{6,7},{7,6},{8,9},{9,8},{10,11... | collective-permute-start | bytes 786440 | tf_op jit(solution)/shard_map/ppermute | solution.py:323
  110.4 9.3 %collective-permute-start.8 = (bf16[128,1024]{1,0:T(8,128)(2,1)S(1)}, bf16[128,1024]{1,0:T(8,128)(2,1)S(1)}, u32[]{:S(2)}, u32[]{:S(2)}) collective-permute-start(bf16[128,1024]{1,0:T(8,128)(2,1)S(1)} %convolution_convert_fusion.3.own_ref), channel_id=1, source_target_pairs={{0,1},{1,0},{2,3},{3,2},{4,5},{5,4},{6,7},{7,6},{8,9},{9,8},{10,11... | collective-permute-start | bytes 786440 | tf_op jit(solution)/shard_map/ppermute | solution.py:323
  113.6 10.3 %collective-permute-start.9 = (bf16[128,1024]{1,0:T(8,128)(2,1)S(1)}, bf16[128,1024]{1,0:T(8,128)(2,1)S(1)}, u32[]{:S(2)}, u32[]{:S(2)}) collective-permute-start(bf16[128,1024]{1,0:T(8,128)(2,1)S(1)} %convolution_convert_fusion.2.own_ref), channel_id=1, source_target_pairs={{0,1},{1,0},{2,3},{3,2},{4,5},{5,4},{6,7},{7,6},{8,9},{9,8},{10,11... | collective-permute-start | bytes 786440 | tf_op jit(solution)/shard_map/ppermute | solution.py:323
  144.9 9.3 %collective-permute-start.11 = (bf16[128,1024]{1,0:T(8,128)(2,1)S(1)}, bf16[128,1024]{1,0:T(8,128)(2,1)S(1)}, u32[]{:S(2)}, u32[]{:S(2)}) collective-permute-start(bf16[128,1024]{1,0:T(8,128)(2,1)S(1)} %convolution_convert_fusion.own_ref), channel_id=1, source_target_pairs={{0,1},{1,0},{2,3},{3,2},{4,5},{5,4},{6,7},{7,6},{8,9},{9,8},{10,11... | collective-permute-start | bytes 786440 | tf_op jit(solution)/shard_map/ppermute | solution.py:323
  146.3 11.1 %collective-permute-start.10 = (bf16[128,1024]{1,0:T(8,128)(2,1)S(1)}, bf16[128,1024]{1,0:T(8,128)(2,1)S(1)}, u32[]{:S(2)}, u32[]{:S(2)}) collective-permute-start(bf16[128,1024]{1,0:T(8,128)(2,1)S(1)} %convolution_convert_fusion.1.own_ref), channel_id=1, source_target_pairs={{0,1},{1,0},{2,3},{3,2},{4,5},{5,4},{6,7},{7,6},{8,9},{9,8},{10,11... | collective-permute-start | bytes 786440 | tf_op jit(solution)/shard_map/ppermute | solution.py:323
  159.9 14.0 %all-to-all-start.3 = ((bf16[8,128,128]{2,1,0:T(8,128)(2,1)}), bf16[8,128,128]{2,1,0:T(8,128)(2,1)S(1)}, u32[]{:S(2)}, u32[]{:S(2)}) async-start(bf16[8,128,128]{2,1,0:T(8,128)(2,1)} %ctx_grad.1), calls=%async_computation.3 | async-start | bytes 524288 | tf_op jit(solution)/shard_map/all_to_all | solution.py:1235
  192.6 28.9 %all-to-all-start.4 = ((bf16[8,384,128]{2,1,0:T(8,128)(2,1)}), bf16[8,384,128]{2,1,0:T(8,128)(2,1)}, u32[]{:S(2)}, u32[]{:S(2)}) async-start(bf16[8,384,128]{2,1,0:T(8,128)(2,1)} %combine.1.own_ref), calls=%async_computation.4 | async-start | bytes 1572864 | tf_op jit(solution)/shard_map/all_to_all | solution.py:1235
  196.8 60.8 %all-gather.5.cloned.1.call-start = ((), (), s32[]{:S(2)}) async-start(), calls=%async_computation.9 | async-start | bytes 2228224 | tf_op jit(solution)/shard_map/all_gather | solution.py:1425
  196.8 9.5 %collective-permute-start.13 = (bf16[8,384,128]{2,1,0:T(8,128)(2,1)}, bf16[8,384,128]{2,1,0:T(8,128)(2,1)}, u32[]{:S(2)}, u32[]{:S(2)}) collective-permute-start(bf16[8,384,128]{2,1,0:T(8,128)(2,1)} %combine.1.own_ref), channel_id=1, source_target_pairs={{0,2},{2,0},{4,6},{6,4},{8,10},{10,8},{12,14},{14,12},{16,18},{18,... | collective-permute-start | bytes 2359304 | tf_op jit(solution)/shard_map/ppermute | solution.py:323
  224.2 15.7 %collective-permute-start.21 = (bf16[4,256,128]{2,1,0:T(8,128)(2,1)}, bf16[4,256,128]{2,1,0:T(8,128)(2,1)}, u32[]{:S(2)}, u32[]{:S(2)}) collective-permute-start(bf16[4,256,128]{2,1,0:T(8,128)(2,1)} %copy-done.51), channel_id=1, source_target_pairs={{0,4},{2,6},{4,0},{6,2},{8,12},{10,14},{12,8},{14,10},{16,20},{18,... | collective-permute-start | bytes 786440 | tf_op jit(solution)/shard_map/ppermute | solution.py:323
  231.1 8.8 %collective-permute-start.20 = (bf16[128,1024]{1,0:T(8,128)(2,1)}, bf16[128,1024]{1,0:T(8,128)(2,1)S(1)}, u32[]{:S(2)}, u32[]{:S(2)}) collective-permute-start(bf16[128,1024]{1,0:T(8,128)(2,1)} %get-tuple-element.188), channel_id=1, source_target_pairs={{0,1},{1,0},{2,3},{3,2},{4,5},{5,4},{6,7},{7,6},{8,9},{9,8},{10,11... | collective-permute-start | bytes 786440 | tf_op jit(solution)/shard_map/ppermute | solution.py:323
  232.8 7.1 %collective-permute-start.19 = (f32[16,512]{1,0:T(8,128)S(1)}, f32[16,512]{1,0:T(8,128)S(1)}, u32[]{:S(2)}, u32[]{:S(2)}) collective-permute-start(f32[16,512]{1,0:T(8,128)S(1)} %add.100), channel_id=1, source_target_pairs={{0,16},{2,18},{4,20},{6,22},{8,24},{10,26},{12,28},{14,30},{16,0},... | collective-permute-start | bytes 98312 | tf_op jit(solution)/shard_map/ppermute | solution.py:323
  235.8 19.3 %all-to-all-start.5 = ((bf16[8,96,128]{2,1,0:T(8,128)(2,1)}), bf16[8,96,128]{2,1,0:T(8,128)(2,1)S(1)}, u32[]{:S(2)}, u32[]{:S(2)}) async-start(bf16[8,96,128]{2,1,0:T(8,128)(2,1)} %head_grad.1), calls=%async_computation.6 | async-start | bytes 393216 | tf_op jit(solution)/shard_map/all_to_all | solution.py:1235
  241.0 9.9 %collective-permute-start.22 = (bf16[2,256,128]{2,1,0:T(8,128)(2,1)S(1)}, bf16[2,256,128]{2,1,0:T(8,128)(2,1)S(1)}, u32[]{:S(2)}, u32[]{:S(2)}) collective-permute-start(bf16[2,256,128]{2,1,0:T(8,128)(2,1)S(1)} %get-tuple-element.197), channel_id=1, source_target_pairs={{0,8},{2,10},{4,12},{6,14},{8,0},{10,2},{12,4},{14,6},{16,24},{18,... | collective-permute-start | bytes 393224 | tf_op jit(solution)/shard_map/ppermute | solution.py:323
  (80 other events, 652.5 us)
Sparse Core Ops, SparseCore 0:
  49.0 52.9 all-gather.2
  138.6 65.9 reduce-scatter.1
  223.2 33.1 all-gather.4
